TPU v7x, 32 devices: a whole 2x2x4 slice. The times are simulated.
32 devices in a mesh: seq: 32 (over z, y, x, core), head: 1.
Axes of the slice: x: 2, y: 2, z: 4, core: 2. Of those that a mesh axis runs over, the one named last changes fastest.
Arguments:
- queries: bfloat16 [4096, 128], P('seq'), may hold values from -6 to 6
- key_rows: bfloat16 [4096, 128], P('seq'), may hold values from -0.01171875 to 0.01171875
- values: bfloat16 [4096, 5120], P('seq', 'head'), may hold values from -6 to 6
- gate_rows: bfloat16 [4096, 5120], P('seq', 'head'), may hold values from -6 to 6
- log_decay: float32 [4096, 80], P('seq', 'head'), may hold values from -0.69 to 0
- skip_gain: float32 [80], P('head'), may hold values from 0.3 to 4.2
- lam_index: int32 [4096], P('seq'), may hold values from 0 to 63
- segments: int32 [4096], P('seq'), may hold values from 0 to 127, never falling along the last dimension, each value on 1 to 64 neighbouring positions
- lam_table: float32 [64, 7, 80], P(None, None, 'head'), may hold values from 0.2 to 2
- norm_gain: float32 [5120], P('head'), may hold values from 0.25 to 1.75
- out_proj: bfloat16 [5120, 2560], P('head', 'seq'), may hold values from -0.078125 to 0.078125
Outputs:
- mixer_out: bfloat16 [4096, 2560], P(('seq', 'head'))
Inputs may be any that keep to these rules, and one draw needn't show every extreme that they name: `segments`: stretch numbers never fall along the sequence; each stretch has 1 to 64 tokens.
All inputs are finite; a program needn't handle non-finite values.
Results may differ from a plain program's by a relative error of at most 0.012.
Values may be sent and summed in bfloat16 or wider, within the bound.
A program may use at most 128 MiB of HBM per device.

v0:
```python
import jax
import jax.numpy as jnp
from jax import lax
from jax.sharding import PartitionSpec as P

DI = 5120


epsilon = 1e-05
highest = lax.Precision.HIGHEST


def swapped(value, axis, distance):
    mask = 2**distance
    pairs = [(source, source ^ mask) for source in range(lax.axis_size(axis))]
    return lax.ppermute(value, axis, pairs)


def widen(matrix, head_dim):
    return jnp.repeat(matrix, head_dim, axis=-1)


def per_device(
    queries,
    key_rows,
    values,
    gate_rows,
    log_decay,
    skip_gain,
    lam_index,
    segments,
    lam_table,
    norm_gain,
    out_proj,
):
    tok_rows, state_dim = queries.shape
    head_count = log_decay.shape[1]
    col_count = values.shape[1]
    head_dim = col_count // head_count
    class_count = lam_table.shape[0]
    level_count = lam_table.shape[1]
    cross_levels = level_count - 2
    shard_pos = lax.axis_index("seq")
    cum_decay = jnp.cumsum(log_decay, axis=0)
    onehot = (lam_index[:, None] == jnp.arange(class_count, dtype=jnp.int32)[None, :]).astype(
        jnp.float32
    )
    level_wts = jnp.dot(
        onehot, lam_table.reshape(class_count, level_count * head_count), precision=highest
    )
    level_wts = level_wts.reshape(tok_rows, level_count, head_count)
    decay_end = widen(jnp.exp(cum_decay[-1][None, :] - cum_decay), head_dim)
    decayed = (values.astype(jnp.float32) * decay_end).astype(jnp.bfloat16)
    end_state = jnp.dot(key_rows.T, decayed, preferred_element_type=jnp.float32).astype(
        jnp.bfloat16
    )
    shard_span = cum_decay[-1]
    totals = lax.all_gather(shard_span[None, :], "seq", axis=0, tiled=True)
    bounds = jnp.concatenate(
        [jnp.zeros((1, head_count), jnp.float32), jnp.cumsum(totals, axis=0)], axis=0
    )
    here_bound = lax.dynamic_index_in_dim(bounds, shard_pos, 0, keepdims=False)
    bucket_list = []
    group_state = end_state
    for level_pos in range(cross_levels):
        partner_state = swapped(group_state, "seq", level_pos)
        is_upper = jnp.bitwise_and(jnp.right_shift(shard_pos, level_pos), 1) == 1
        group_idx = jnp.right_shift(shard_pos, level_pos)
        start_row = jnp.left_shift(group_idx, level_pos)
        start_bound = lax.dynamic_index_in_dim(bounds, start_row, 0, keepdims=False)
        factor = widen(jnp.exp(here_bound - start_bound), head_dim)[None, :]
        bucket_list.append(jnp.where(is_upper, factor * partner_state.astype(jnp.float32), 0.0))
        if level_pos + 1 < cross_levels:
            upper_start = jnp.bitwise_or(start_row, 2**level_pos)
            upper_begin = lax.dynamic_index_in_dim(bounds, upper_start, 0, keepdims=False)
            upper_end = lax.dynamic_index_in_dim(
                bounds, upper_start + 2**level_pos, 0, keepdims=False
            )
            span_factor = widen(jnp.exp(upper_end - upper_begin), head_dim)[None, :]
            upper_state = jnp.where(is_upper, group_state, partner_state).astype(jnp.float32)
            lower_state = jnp.where(is_upper, partner_state, group_state).astype(jnp.float32)
            group_state = (upper_state + span_factor * lower_state).astype(jnp.bfloat16)
    buckets = jnp.stack(bucket_list)
    block_rows = min(tok_rows, 512)
    block_count = tok_rows // block_rows
    value_heads = values.reshape(tok_rows, head_count, head_dim)
    key_cols = cum_decay.T
    key_pos = jnp.arange(tok_rows, dtype=jnp.int32)

    def local_block(block_pos):
        first_row = block_pos * block_rows
        scores = jnp.dot(queries, key_rows.T, preferred_element_type=jnp.float32)
        query_pos = first_row + jnp.arange(block_rows, dtype=jnp.int32)
        causal = query_pos[:, None] >= key_pos[None, :]
        log_gaps = jnp.where(causal[None], cum_decay.T[:, :, None] - key_cols[:, None, :], -jnp.inf)
        same_seg = segments[:, None] == segments[None, :]
        level_w = jnp.where(
            same_seg[None], level_wts[:, 0, :].T[:, :, None], level_wts[:, 1, :].T[:, :, None]
        )
        weights_bf = (scores[None] * jnp.exp(log_gaps) * level_w).astype(jnp.bfloat16)
        block_out = jnp.einsum(
            "htj,jhp->thp", weights_bf, value_heads, preferred_element_type=jnp.float32
        )
        return block_out.reshape(block_rows, col_count)

    local_out = lax.map(local_block, jnp.arange(block_count, dtype=jnp.int32)).reshape(
        tok_rows, col_count
    )
    query_f32 = queries.astype(jnp.float32)
    cross_out = jnp.zeros((tok_rows, col_count), jnp.float32)
    for level_pos in range(cross_levels):
        level_read = jnp.dot(query_f32, buckets[level_pos], precision=highest)
        cross_out = cross_out + level_read * widen(level_wts[:, 2 + level_pos, :], head_dim)
    cross_out = cross_out * widen(jnp.exp(cum_decay), head_dim)
    mixer_sum = (
        local_out + cross_out + widen(skip_gain, head_dim)[None, :] * values.astype(jnp.float32)
    )
    gated = mixer_sum * jax.nn.silu(gate_rows.astype(jnp.float32))
    square_sum = lax.psum(jnp.sum(gated * gated, axis=1), "head")
    inv_rms = lax.rsqrt(square_sum / DI + epsilon)
    normed = (gated * inv_rms[:, None] * norm_gain[None, :]).astype(jnp.bfloat16)
    partial_terms = jnp.dot(
        normed,
        lax.all_gather(out_proj, "seq", axis=1, tiled=True),
        preferred_element_type=jnp.float32,
    )
    return lax.psum_scatter(
        partial_terms.astype(jnp.bfloat16), "head", scatter_dimension=0, tiled=True
    )


def solution(mesh):
    return jax.shard_map(
        per_device,
        mesh=mesh,
        in_specs=(
            P("seq", None),
            P("seq", None),
            P("seq", "head"),
            P("seq", "head"),
            P("seq", "head"),
            P("head"),
            P("seq"),
            P("seq"),
            P(None, None, "head"),
            P("head"),
            P("head", "seq"),
        ),
        out_specs=P(("seq", "head"), None),
        check_vma=False,
    )
```

profile of v0, /device:TPU:0, one launch (start us, length us, event | category | flops | bytes accessed | tf_op | source)
XLA Modules:
  0.0 310.2 jit_solution(3015980585906839721)
XLA Ops:
  8.4 1.8 copy.35
  10.5 1.6 fusion.13
  12.6 43.5 %all-gather = f32[32,1,80]{2,1,0:T(1,128)S(1)} all-gather(f32[1,1,80]{2,1,0:T(1,128)S(1)} %get-tuple-element.44), channel_id=1, replica_groups=mesh['seq'=32,'head'=1] {'seq'}, dimensions={0}, use_global_device_ids=true | all-gather | bytes 10560 | tf_op jit(solution)/shard_map/all_gather | solution.py:58
  56.3 3.7 %add_convert_fusion.3 = bf16[128,5120]{0,1:T(8,128)(2,1)S(1)} fusion(bf16[128,5120]{0,1:T(8,128)(2,1)S(1)} %collective-permute-done, bf16[128,5120]{0,1:T(8,128)(2,1)} %fusion.13, f32[5120]{0:T(1024)S(1)} %mul.175, pred[]{:T(512)S(6)} %eq.58), kind=kLoop, calls=%fused_computation.48 | loop fusion | flops 4587520 | bytes 3952641 | tf_op jit(solution)/shard_map/convert_element_type | solution.py:82
  60.4 41.4 %collective-permute-done.1 = bf16[128,5120]{0,1:T(8,128)(2,1)} collective-permute-done((bf16[128,5120]{0,1:T(8,128)(2,1)S(1)}, bf16[128,5120]{0,1:T(8,128)(2,1)}, u32[]{:S(2)}, u32[]{:S(2)}) %collective-permute-start.1) | collective-permute-done | bytes 1310752 | tf_op jit(solution)/shard_map/ppermute | solution.py:16
  101.9 3.3 %add_convert_fusion.2 = bf16[128,5120]{0,1:T(8,128)(2,1)S(1)} fusion(bf16[128,5120]{0,1:T(8,128)(2,1)} %collective-permute-done.1, bf16[128,5120]{0,1:T(8,128)(2,1)S(1)} %add_convert_fusion.3, f32[5120]{0:T(1024)S(1)} %mul.182, pred[]{:T(512)S(6)} %eq.59), kind=kLoop, calls=%fused_computation.44 | loop fusion | flops 4587520 | bytes 3952641 | tf_op jit(solution)/shard_map/convert_element_type | solution.py:82
  105.2 1.5 collective-permute-start.2
  108.4 2.5 copy.39
  112.3 44.5 %collective-permute-done.2 = bf16[128,5120]{0,1:T(8,128)(2,1)S(1)} collective-permute-done((bf16[128,5120]{0,1:T(8,128)(2,1)S(1)}, bf16[128,5120]{0,1:T(8,128)(2,1)S(1)}, u32[]{:S(2)}, u32[]{:S(2)}) %collective-permute-start.2) | collective-permute-done | bytes 1310752 | tf_op jit(solution)/shard_map/ppermute | solution.py:16
  156.7 2.2 add_convert_fusion.1
  158.9 1.4 collective-permute-start.3
  160.4 4.2 %fusion.14 = f32[80,128,64]{1,2,0:T(8,128)S(1)} fusion(bf16[128,80,64]{0,2,1:T(8,128)(2,1)S(1)} %bitcast.113, f32[80,128]{1,0:T(8,128)S(1)} %get-tuple-element.40, f32[80,128]{1,0:T(8,128)S(1)} %get-tuple-element.42, f32[80,128]{1,0:T(8,128)S(1)} %copy.31, f32[128,128]{1,0:T(8,128)S(1)} %fusion.79, pred[128,128]{1,0:T(8,128)(4,1)S(1)} %get-tuple-element.63, ...), kind=kOutput, calls=%fused_computation.26 | convolution fusion | flops 175636480 | bytes 4153344 | tf_op jit(solution)/shard_map/while/body/eval_jaxpr/htj,jhp->thp/dot_general | solution.py:101
  164.8 1.1 copy-done.5
  166.0 3.2 %fusion.11 = f32[128,5120]{0,1:T(8,128)S(1)} fusion(f32[128,5120]{0,1:T(8,128)S(1)} %bitcast.109, bf16[128,128]{1,0:T(8,128)(2,1)S(1)} %copy-done, bf16[128,5120]{0,1:T(8,128)(2,1)S(1)} %copy-done.5, f32[5120]{0:T(1024)S(1)} %mul.168, pred[]{:T(512)S(6)} %eq.58), kind=kOutput, calls=%fused_computation.16 | convolution fusion | flops 1009254400 | bytes 6606849 | tf_op jit(solution)/shard_map/dot_general | solution.py:112
  169.2 52.7 %collective-permute-done.3 = bf16[128,5120]{0,1:T(8,128)(2,1)S(1)} collective-permute-done((bf16[128,5120]{0,1:T(8,128)(2,1)S(1)}, bf16[128,5120]{0,1:T(8,128)(2,1)S(1)}, u32[]{:S(2)}, u32[]{:S(2)}) %collective-permute-start.3) | collective-permute-done | bytes 1310752 | tf_op jit(solution)/shard_map/ppermute | solution.py:16
  221.8 2.2 add_convert_fusion
  224.0 1.5 collective-permute-start.4
  225.7 4.3 %fusion.10 = f32[128,5120]{0,1:T(8,128)S(1)} fusion(f32[128,5120]{0,1:T(8,128)S(1)} %fusion.11, f32[128,5120]{0,1:T(8,128)S(1)} %bitcast.110, bf16[128,128]{1,0:T(8,128)(2,1)S(1)} %copy-done, bf16[128,5120]{0,1:T(8,128)(2,1)} %collective-permute-done.1, f32[5120]{0:T(1024)S(1)} %mul.173, pred[]{:T(512)S(6)} %eq.59), kind=kOutput, calls=%fused_computation.14 | convolution fusion | flops 1009909760 | bytes 9228289 | tf_op jit(solution)/shard_map/dot_general | solution.py:112
  230.2 3.3 %fusion.8 = f32[128,5120]{0,1:T(8,128)S(1)} fusion(f32[128,5120]{0,1:T(8,128)S(1)} %fusion.10, f32[128,5120]{0,1:T(8,128)S(1)} %bitcast.111, bf16[128,128]{1,0:T(8,128)(2,1)S(1)} %copy-done, bf16[128,5120]{0,1:T(8,128)(2,1)S(1)} %collective-permute-done.2, f32[5120]{0:T(1024)S(1)} %mul.180, pred[]{:T(512)S(6)} %eq.60), kind=kOutput, calls=%fused_computation.11 | convolution fusion | flops 1009909760 | bytes 9228289 | tf_op jit(solution)/shard_map/dot_general | solution.py:112
  233.6 3.3 %fusion.6 = f32[128,5120]{0,1:T(8,128)S(1)} fusion(f32[128,5120]{0,1:T(8,128)S(1)} %fusion.8, f32[128,5120]{0,1:T(8,128)S(1)} %bitcast.112, bf16[128,128]{1,0:T(8,128)(2,1)S(1)} %copy-done, bf16[128,5120]{0,1:T(8,128)(2,1)S(1)} %collective-permute-done.3, f32[5120]{0:T(1024)S(1)} %mul.187, pred[]{:T(512)S(6)} %eq.61), kind=kOutput, calls=%fused_computation.8 | convolution fusion | flops 1009909760 | bytes 9228289 | tf_op jit(solution)/shard_map/dot_general | solution.py:112
  236.9 42.7 %collective-permute-done.4 = bf16[128,5120]{0,1:T(8,128)(2,1)S(1)} collective-permute-done((bf16[128,5120]{0,1:T(8,128)(2,1)S(1)}, bf16[128,5120]{0,1:T(8,128)(2,1)S(1)}, u32[]{:S(2)}, u32[]{:S(2)}) %collective-permute-start.4) | collective-permute-done | bytes 1310752 | tf_op jit(solution)/shard_map/ppermute | solution.py:16
  279.9 1.0 copy-done.6
  280.9 6.6 %multiply_reduce_fusion = (f32[128]{0:T(128)S(1)}, f32[128,5120]{0,1:T(8,128)S(1)}) fusion(bf16[128,5120]{0,1:T(8,128)(2,1)S(1)} %copy-done.6, bf16[128,5120]{0,1:T(8,128)(2,1)S(1)} %copy-done.3, f32[5120]{0:T(1024)S(1)} %mul.202, f32[128,5120]{0,1:T(8,128)S(1)} %bitcast.119, f32[128,5120]{0,1:T(8,128)S(1)} %bitcast.115, f32[128,5120]{0,1:T(8,128)S(1)} %fusion.6, ...), kind=kOutput, calls=%fused_computation.32 | convolution fusion | flops 1018429312 | bytes 17113600 | tf_op jit(solution)/shard_map/dot_general | solution.py:112
  287.5 15.8 %convolution_convert_fusion.1 = bf16[128,2560]{1,0:T(8,128)(2,1)} fusion(bf16[5120,2560]{0,1:T(8,128)(2,1)} %all-gather.3.cloned.1.call-done, f32[128,5120]{0,1:T(8,128)S(1)} %get-tuple-element.61, f32[5120]{0:T(1024)S(1)} %copy-done.9, f32[128]{0:T(128)S(1)} %add_rsqrt_fusion), kind=kOutput, calls=%fused_computation.21 | convolution fusion | flops 3357736960 | bytes 29512192 | tf_op jit(solution)/shard_map/dot_general | solution.py:122
  (73 shorter events, 7.4 us)
Async XLA Ops:
  6.5 105.1 %copy-start = (bf16[128,128]{1,0:T(8,128)(2,1)S(1)}, bf16[128,128]{1,0:T(8,128)(2,1)}, u32[]{:S(2)}) copy-start(bf16[128,128]{1,0:T(8,128)(2,1)} %param.11) | copy-start | bytes 98308
  6.5 281.0 %all-gather.3.cloned.1.call-start = ((), (), s32[]{:S(2)}) async-start(), calls=%async_computation | async-start | bytes 27033600 | tf_op jit(solution)/shard_map/all_gather | solution.py:124
  8.4 2.1 copy-start.8
  10.2 1.9 copy-start.2
  12.1 44.2 %collective-permute-start = (bf16[128,5120]{0,1:T(8,128)(2,1)}, bf16[128,5120]{0,1:T(8,128)(2,1)S(1)}, u32[]{:S(2)}, u32[]{:S(2)}) collective-permute-start(bf16[128,5120]{0,1:T(8,128)(2,1)} %fusion.13), channel_id=1, source_target_pairs={{0,1},{1,0},{2,3},{3,2},{4,5},{5,4},{6,7},{7,6},{8,9},{9,8},{10,11... | collective-permute-start | bytes 3932168 | tf_op jit(solution)/shard_map/ppermute | solution.py:16
  56.3 4.1 %copy-start.4 = (bf16[128,5120]{0,1:T(8,128)(2,1)}, bf16[128,5120]{0,1:T(8,128)(2,1)S(1)}, u32[]{:S(2)}) copy-start(bf16[128,5120]{0,1:T(8,128)(2,1)S(1)} %collective-permute-done) | copy-start | bytes 3932164
  60.1 47.1 %copy-start.7 = (f32[64,7,80]{2,0,1:T(8,128)S(1)}, f32[64,7,80]{2,0,1:T(8,128)}, u32[]{:S(2)}) copy-start(f32[64,7,80]{2,0,1:T(8,128)} %param.19) | copy-start | bytes 430084
  60.1 41.8 %collective-permute-start.1 = (bf16[128,5120]{0,1:T(8,128)(2,1)S(1)}, bf16[128,5120]{0,1:T(8,128)(2,1)}, u32[]{:S(2)}, u32[]{:S(2)}) collective-permute-start(bf16[128,5120]{0,1:T(8,128)(2,1)S(1)} %add_convert_fusion.3), channel_id=1, source_target_pairs={{0,2},{1,3},{2,0},{3,1},{4,6},{5,7},{6,4},{7,5},{8,10},{9,11},{10,... | collective-permute-start | bytes 3932168 | tf_op jit(solution)/shard_map/ppermute | solution.py:16
  105.1 6.7 %copy-start.11 = (s32[128]{0:T(128)S(1)}, s32[128]{0:T(128)}, u32[]{:S(2)}) copy-start(s32[128]{0:T(128)} %param.17) | copy-start | bytes 1540
  105.2 51.6 %collective-permute-start.2 = (bf16[128,5120]{0,1:T(8,128)(2,1)S(1)}, bf16[128,5120]{0,1:T(8,128)(2,1)S(1)}, u32[]{:S(2)}, u32[]{:S(2)}) collective-permute-start(bf16[128,5120]{0,1:T(8,128)(2,1)S(1)} %add_convert_fusion.2), channel_id=1, source_target_pairs={{0,4},{1,5},{2,6},{3,7},{4,0},{5,1},{6,2},{7,3},{8,12},{9,13},{10,... | collective-permute-start | bytes 3932168 | tf_op jit(solution)/shard_map/ppermute | solution.py:16
  110.9 49.4 %copy-start.10 = (s32[128]{0:T(128)S(1)}, s32[128]{0:T(128)}, u32[]{:S(2)}) copy-start(s32[128]{0:T(128)} %param.18) | copy-start | bytes 1540
  111.7 48.7 %copy-start.3 = (bf16[128,5120]{0,1:T(8,128)(2,1)S(1)}, bf16[128,5120]{0,1:T(8,128)(2,1)}, u32[]{:S(2)}) copy-start(bf16[128,5120]{0,1:T(8,128)(2,1)} %copy-done.2) | copy-start | bytes 3932164
  158.9 62.9 %collective-permute-start.3 = (bf16[128,5120]{0,1:T(8,128)(2,1)S(1)}, bf16[128,5120]{0,1:T(8,128)(2,1)S(1)}, u32[]{:S(2)}, u32[]{:S(2)}) collective-permute-start(bf16[128,5120]{0,1:T(8,128)(2,1)S(1)} %add_convert_fusion.1), channel_id=1, source_target_pairs={{0,8},{1,9},{2,10},{3,11},{4,12},{5,13},{6,14},{7,15},{8,0},{9,1},... | collective-permute-start | bytes 3932168 | tf_op jit(solution)/shard_map/ppermute | solution.py:16
  164.6 1.3 copy-start.5
  224.0 55.6 %collective-permute-start.4 = (bf16[128,5120]{0,1:T(8,128)(2,1)S(1)}, bf16[128,5120]{0,1:T(8,128)(2,1)S(1)}, u32[]{:S(2)}, u32[]{:S(2)}) collective-permute-start(bf16[128,5120]{0,1:T(8,128)(2,1)S(1)} %add_convert_fusion), channel_id=1, source_target_pairs={{0,16},{1,17},{2,18},{3,19},{4,20},{5,21},{6,22},{7,23},{8,24},{9,... | collective-permute-start | bytes 3932168 | tf_op jit(solution)/shard_map/ppermute | solution.py:16
  279.6 1.3 copy-start.6
  280.9 6.6 %copy-start.9 = (f32[5120]{0:T(1024)S(1)}, f32[5120]{0:T(1024)}, u32[]{:S(2)}) copy-start(f32[5120]{0:T(1024)} %param.20) | copy-start | bytes 61444
  287.5 15.9 %copy-start.1 = (bf16[128,128]{1,0:T(8,128)(2,1)S(1)}, bf16[128,128]{1,0:T(8,128)(2,1)}, u32[]{:S(2)}) copy-start(bf16[128,128]{1,0:T(8,128)(2,1)} %param.11) | copy-start | bytes 98308
Sparse Core Ops, SparseCore 0:
  10.2 212.7 all-gather.2
where the time goes:
time: 311 us; the launch traced here: 310 us
  waiting for transfers between devices  182 us (59%)
  blocking collectives  43.5 us (14%)
  matrix products  42.8 us (14%)
  between operations  13.7 us (4%)
  other arithmetic  12 us (4%)
  local copies, waits for them, and re-layouts  11.2 us (4%)
  starting transfers between devices  4.97 us (2%)
    ppermute x5, waiting for transfers between devices, swapped(): return lax.ppermute(value, axis, pairs)  181 us
    all_gather x1, blocking collectives, per_device(): totals = lax.all_gather(shard_span[None, :], 'seq', axis=0, tiled=True)  43.5 us
    dot_general x5, matrix products, per_device(): level_read = jnp.dot(query_f32, buckets[level_pos], precision=highest)  20.6 us
    dot_general x1, matrix products, per_device(): jnp.dot(normed, lax.all_gather(out_proj, 'seq', axis=1, tiled=True), pref...  15.8 us
    convert_element_type x4, other arithmetic, per_device(): group_state = (upper_state + span_factor * lower_state).astype(jnp.bfloat16)  11.3 us
    unnamed x29, local copies, waits for them, and re-layouts  7.43 us
  transfers between devices with their start and end apart: 6, of which 4 were waited for; matrix products, arithmetic and copies ran while one was open for 15% of the time, Pallas kernels for 0%

commit v1 on v0

v1 whole, which is shorter than its diff:
```python
import math

import jax
import jax.numpy as jnp
from jax import lax
from jax.sharding import PartitionSpec as P

epsilon = 1e-05
highest = lax.Precision.HIGHEST
f32 = jnp.float32
bf16 = jnp.bfloat16


def xor_permute(value, mask):
    pairs = [(source, source ^ mask) for source in range(lax.axis_size("seq"))]
    return lax.ppermute(value, "seq", pairs)


def widen(matrix, head_dim):
    return jnp.repeat(matrix, head_dim, axis=-1)


def per_device(
    queries,
    key_rows,
    values,
    gate_rows,
    log_decay,
    skip_gain,
    lam_index,
    segments,
    lam_table,
    norm_gain,
    out_proj,
):
    tok, state_dim = queries.shape
    head_count = log_decay.shape[1]
    cols = values.shape[1]
    head_dim = cols // head_count
    classes, level_count = lam_table.shape[:2]
    dev_count = lax.axis_size("seq")
    inner_total = cols * lax.axis_size("head")
    A = math.gcd(math.gcd(head_count, 8), dev_count)
    Z = dev_count // A
    a_bits = A.bit_length() - 1
    z_bits = Z.bit_length() - 1
    hg = head_count // A
    cg = hg * head_dim
    rows = A * tok
    out_cols = out_proj.shape[1]
    groups = [[z * A + i for i in range(A)] for z in range(Z)]
    me = lax.axis_index("seq")
    in_pos = lax.rem(me, A)
    z_pos = lax.div(me, A)

    def exchange(blocks):
        return lax.all_to_all(
            blocks, "seq", 0, 0, tiled=True, axis_index_groups=groups
        )

    def my_heads(array, width, axis):
        return lax.dynamic_slice_in_dim(array, in_pos * width, width, axis)

    w_blocks = out_proj.T.reshape(out_cols, A, cg).swapaxes(0, 1)
    w_block = exchange(w_blocks).reshape(A * out_cols, cg)

    shared = jnp.concatenate([queries, key_rows], axis=1)
    packed = jnp.concatenate(
        [
            values.reshape(tok, A, cg).swapaxes(0, 1),
            jnp.broadcast_to(shared[None], (A, tok, 2 * state_dim)),
        ],
        axis=2,
    )
    small = jnp.concatenate(
        [
            log_decay.reshape(tok, A, hg).swapaxes(0, 1),
            jnp.broadcast_to(lam_index.astype(f32)[None, :, None], (A, tok, 1)),
            jnp.broadcast_to(segments.astype(f32)[None, :, None], (A, tok, 1)),
        ],
        axis=2,
    )
    small = exchange(small)
    packed = exchange(packed)
    gates = exchange(gate_rows.reshape(tok, A, cg).swapaxes(0, 1))

    w_ring = [w_block]
    for _ in range(Z - 1):
        w_ring.append(
            lax.ppermute(
                w_ring[-1], "seq", [(s, (s + A) % dev_count) for s in range(dev_count)]
            )
        )

    x = packed[:, :, :cg]
    q = packed[:, :, cg : cg + state_dim]
    k = packed[:, :, cg + state_dim :]
    ld = small[:, :, :hg]
    lam = small[:, :, hg].reshape(rows).astype(jnp.int32)
    seg = small[:, :, hg + 1]

    cum = jnp.cumsum(ld, axis=1)
    span = cum[:, -1, :]
    onehot = (lam[:, None] == jnp.arange(classes, dtype=jnp.int32)[None, :]).astype(f32)
    table = my_heads(lam_table, hg, 2).reshape(classes, level_count * hg)
    lw = jnp.dot(onehot, table, precision=highest).reshape(A, tok, level_count, hg)

    decayed = (x.astype(f32) * widen(jnp.exp(span[:, None, :] - cum), head_dim)).astype(bf16)
    state = jnp.einsum("sjn,sjc->snc", k, decayed, preferred_element_type=f32).astype(bf16)

    cross = jnp.zeros((rows, cg), f32)
    total = span
    prefix = jnp.zeros((A, hg), f32)
    for b in range(a_bits):
        pairs = A >> (b + 1)
        lower, upper = state[0::2], state[1::2]
        low_total, up_total = total[0::2], total[1::2]
        wide = 2**b
        q_up = q.reshape(pairs, 2, wide * tok, state_dim)[:, 1]
        read = jnp.einsum("gtn,gnc->gtc", q_up, lower, preferred_element_type=f32)
        scale = (jnp.exp(cum + prefix[:, None, :]) * lw[:, :, 2 + b, :]).reshape(
            pairs, 2, wide * tok, hg
        )[:, 1]
        read = read * widen(scale, head_dim)
        cross = cross + jnp.stack([jnp.zeros_like(read), read], axis=1).reshape(rows, cg)
        factor = widen(jnp.exp(up_total), head_dim)[:, None, :]
        state = (upper.astype(f32) + factor * lower.astype(f32)).astype(bf16)
        is_up = jnp.arange(A, dtype=jnp.int32) // wide % 2 == 1
        low_rows = jnp.repeat(low_total, 2 * wide, axis=0)
        prefix = prefix + jnp.where(is_up[:, None], low_rows, 0.0)
        total = low_total + up_total
    state, total = state[0], total[0]
    q_rows = q.reshape(rows, state_dim)
    for zb in range(z_bits):
        other = xor_permute(state, A << zb)
        other_total = xor_permute(total[None, :], A << zb)[0]
        is_up = jnp.bitwise_and(jnp.right_shift(z_pos, zb), 1) == 1
        read = jnp.dot(q_rows, other, preferred_element_type=f32)
        scale = jnp.exp(cum + prefix[:, None, :]) * lw[:, :, 2 + a_bits + zb, :]
        scale = jnp.where(is_up, scale, 0.0).reshape(rows, hg)
        cross = cross + read * widen(scale, head_dim)
        if zb + 1 < z_bits:
            up_state = jnp.where(is_up, state, other).astype(f32)
            low_state = jnp.where(is_up, other, state).astype(f32)
            factor = widen(jnp.exp(jnp.where(is_up, total, other_total)), head_dim)
            state = (up_state + factor[None, :] * low_state).astype(bf16)
            prefix = prefix + jnp.where(is_up, other_total, 0.0)[None, :]
            total = total + other_total

    scores = jnp.einsum("stn,sjn->stj", q, k, preferred_element_type=f32)
    pos = jnp.arange(tok, dtype=jnp.int32)
    causal = pos[:, None] >= pos[None, :]
    cum_h = cum.swapaxes(1, 2)
    gaps = jnp.where(causal, cum_h[:, :, :, None] - cum_h[:, :, None, :], -jnp.inf)
    same = seg[:, :, None] == seg[:, None, :]
    lw0 = lw[:, :, 0, :].swapaxes(1, 2)[:, :, :, None]
    lw1 = lw[:, :, 1, :].swapaxes(1, 2)[:, :, :, None]
    weights = (
        scores[:, None] * jnp.exp(gaps) * jnp.where(same[:, None], lw0, lw1)
    ).astype(bf16)
    local = jnp.einsum(
        "shtj,sjhp->sthp",
        weights,
        x.reshape(A, tok, hg, head_dim),
        preferred_element_type=f32,
    ).reshape(rows, cg)

    skip = widen(my_heads(skip_gain, hg, 0), head_dim)[None, :]
    mixer = local + cross + skip * x.reshape(rows, cg).astype(f32)
    gated = mixer * jax.nn.silu(gates.reshape(rows, cg).astype(f32))
    squares = jnp.sum(gated * gated, axis=1)
    hidden = (gated * my_heads(norm_gain, cg, 0)[None, :]).astype(bf16)

    def reduce_group(part, order, narrow):
        left = list(range(a_bits))[::-1]
        part = part.reshape((2,) * a_bits + part.shape[1:])
        for b in order:
            axis = left.index(b)
            left.remove(b)
            bit = jnp.bitwise_and(jnp.right_shift(in_pos, b), 1)
            mine = lax.dynamic_index_in_dim(part, bit, axis, keepdims=False)
            theirs = lax.dynamic_index_in_dim(part, 1 - bit, axis, keepdims=False)
            part = mine + xor_permute(theirs.astype(narrow), 2**b).astype(f32)
        return part

    bits = list(range(a_bits))
    flipped = bits[:1] + bits[1:][::-1]
    square_sum = reduce_group(squares.reshape(A, tok), bits, f32)
    square_sum = lax.psum(square_sum, "head")
    inv_rms = lax.rsqrt(square_sum / inner_total + epsilon)[:, None]
    block_cols = A * out_cols
    out = jnp.zeros((tok, Z * block_cols), bf16)
    for step in range(Z):
        part = lax.dot_general(
            hidden, w_ring[step], (((1,), (1,)), ((), ())), preferred_element_type=f32
        )
        part = reduce_group(
            part.reshape(A, tok, block_cols), flipped if step % 2 else bits, bf16
        )
        block = lax.rem(z_pos - step + Z, Z)
        out = lax.dynamic_update_slice_in_dim(
            out, (part * inv_rms).astype(bf16), block * block_cols, 1
        )
    return lax.psum_scatter(out, "head", scatter_dimension=0, tiled=True)


def solution(mesh):
    return jax.shard_map(
        per_device,
        mesh=mesh,
        in_specs=(
            P("seq", None),
            P("seq", None),
            P("seq", "head"),
            P("seq", "head"),
            P("seq", "head"),
            P("head"),
            P("seq"),
            P("seq"),
            P(None, None, "head"),
            P("head"),
            P("head", "seq"),
        ),
        out_specs=P(("seq", "head"), None),
        check_vma=False,
    )
```

time: 311 us -> 194 us (0.62)
  waiting for transfers between devices: 182 us -> 37.4 us
  blocking collectives: 43.5 us -> 0 us
  local copies, waits for them, and re-layouts: 11.2 us -> 52.4 us
  starting transfers between devices: 4.97 us -> 42.1 us
  other arithmetic: 12 us -> 35.8 us
  matrix products: 42.8 us -> 24.2 us
  between operations: 13.7 us -> 0.91 us
    ppermute x5 -> x21, waiting for transfers between devices: 181 us -> 37.4 us  [the longest x18 25 us: xor_permute(): return lax.ppermute(value, 'seq', pairs)]
    all_gather x1 -> x0, blocking collectives: 43.5 us -> none  [per_device(): totals = lax.all_gather(shard_span[None, :], 'seq', axis=0, tiled=True)]
    another operation x2 -> x1, other arithmetic: 0.23 us -> 23.3 us  [per_device(): cum = jnp.cumsum(ld, axis=1)]
    ppermute x5 -> x21, starting transfers between devices: 4.96 us -> 24 us  [the longest x18 23.5 us: xor_permute(): return lax.ppermute(value, 'seq', pairs)]
    dot_general x10 -> x13, matrix products: 42.8 us -> 24.2 us  [the longest x2 9.97 us: per_device(): read = jnp.dot(q_rows, other, preferred_element_type=f32)]
    all_to_all x0 -> x4, starting transfers between devices: none -> 18 us  [exchange(): lax.all_to_all(blocks, 'seq', 0, 0, tiled=True, axis_index_groups=groups)]
    reshape x1 -> x9, local copies, waits for them, and re-layouts: 0.12 us -> 15.9 us  [the longest x4 9.42 us: widen(): return jnp.repeat(matrix, head_dim, axis=-1)]
    convert_element_type x5 -> x6, other arithmetic: 11.6 us -> 2.66 us  [the longest x1 0.78 us: per_device(): state = (up_state + factor[None, :] * low_state).astype(bf16)]
  transfers between devices with their start and end apart: 6 -> 25, of which waited for: 4 -> 10; matrix products, arithmetic and copies ran while one was open for 15% -> 55% of each run, Pallas kernels for 0% -> 0%
where the time goes in v1:
time: 194 us; the launch traced here: 193 us
  local copies, waits for them, and re-layouts  52.4 us (27%)
  starting transfers between devices  42.1 us (22%)
  waiting for transfers between devices  37.4 us (19%)
  other arithmetic  35.8 us (18%)
  matrix products  24.2 us (12%)
    ppermute x18, waiting for transfers between devices, xor_permute(): return lax.ppermute(value, 'seq', pairs)  25 us
    ppermute x18, starting transfers between devices, xor_permute(): return lax.ppermute(value, 'seq', pairs)  23.5 us
    another operation x1, other arithmetic, per_device(): cum = jnp.cumsum(ld, axis=1)  23.3 us
    all_to_all x4, starting transfers between devices, exchange(): lax.all_to_all(blocks, 'seq', 0, 0, tiled=True, axis_index_groups=groups)  18 us
    ppermute x3, waiting for transfers between devices, per_device(): lax.ppermute(w_ring[-1], 'seq', [(s, (s + A) % dev_count) for s in range(...  12.3 us
    dot_general x2, matrix products, per_device(): read = jnp.dot(q_rows, other, preferred_element_type=f32)  9.97 us
    reshape x4, local copies, waits for them, and re-layouts, widen(): return jnp.repeat(matrix, head_dim, axis=-1)  9.42 us
    dot_general x4, matrix products, per_device(): lax.dot_general(hidden, w_ring[step], (((1,), (1,)), ((), ())), preferred...  7.74 us
  transfers between devices with their start and end apart: 25, of which 10 were waited for; matrix products, arithmetic and copies ran while one was open for 55% of the time, Pallas kernels for 0%

profile of v1, /device:TPU:0, one launch (start us, length us, event | category | flops | bytes accessed | tf_op | source)
XLA Modules:
  0.0 192.7 jit_solution(12464175671526946658)
XLA Ops:
  2.8 5.2 %all-to-all-start.1 = ((f32[8,128,12]{1,2,0:T(8,128)}), f32[8,128,12]{1,2,0:T(8,128)S(1)}, u32[]{:S(2)}, u32[]{:S(2)}) async-start(f32[8,128,12]{1,2,0:T(8,128)} %pad_maximum_fusion.2), calls=%async_computation.1 | async-start | bytes 131072 | tf_op jit(solution)/shard_map/all_to_all | solution.py:57
  15.7 4.2 %all-to-all-start.3 = ((bf16[8,80,640]{2,1,0:T(8,128)(2,1)}), bf16[8,80,640]{2,1,0:T(8,128)(2,1)S(1)}, u32[]{:S(2)}, u32[]{:S(2)}) async-start(bf16[8,80,640]{2,1,0:T(8,128)(2,1)} %bitcast.292), calls=%async_computation.3 | async-start | bytes 1638400 | tf_op jit(solution)/shard_map/all_to_all | solution.py:57
  20.1 23.3 %fusion.78 = f32[8,128,10]{2,0,1:T(8,128)S(1)} fusion(f32[8,128,10]{2,0,1:T(8,128)S(1)} %copy.29), kind=kOutput, calls=%fused_computation.181 | output fusion | flops 1300480 | bytes 81920 | tf_op jit(solution)/shard_map/jit(cumsum)/reduce_window_sum | solution.py:102
  49.6 4.2 %all-to-all-start = ((bf16[8,128,896]{1,2,0:T(8,128)(2,1)}), bf16[8,128,896]{1,2,0:T(8,128)(2,1)S(1)}, u32[]{:S(2)}, u32[]{:S(2)}) async-start(bf16[8,128,896]{1,2,0:T(8,128)(2,1)} %pad_maximum_fusion), calls=%async_computation | async-start | bytes 3670016 | tf_op jit(solution)/shard_map/all_to_all | solution.py:57
  69.7 3.2 %copy.54 = f32[1024,640]{1,0:T(8,128)} copy(f32[1024,640]{0,1:T(8,128)} %bitcast.296) | data formatting | bytes 5242880 | tf_op jit(solution)/shard_map/reshape | solution.py:20
  74.2 1.9 broadcast_in_dim.178
  76.1 3.2 %copy.57 = f32[1024,640]{1,0:T(8,128)} copy(f32[1024,640]{0,1:T(8,128)} %bitcast.297) | data formatting | bytes 5242880 | tf_op jit(solution)/shard_map/reshape | solution.py:20
  79.3 3.5 %collective-permute-done.9 = bf16[640,640]{1,0:T(8,128)(2,1)} collective-permute-done((bf16[640,640]{1,0:T(8,128)(2,1)}, bf16[640,640]{1,0:T(8,128)(2,1)}, u32[]{:S(2)}, u32[]{:S(2)}) %collective-permute-start.9) | collective-permute-done | bytes 819232 | tf_op jit(solution)/shard_map/ppermute | solution.py:90
  82.8 4.4 %all-to-all-start.2 = ((bf16[8,128,640]{2,1,0:T(8,128)(2,1)}), bf16[8,128,640]{2,1,0:T(8,128)(2,1)}, u32[]{:S(2)}, u32[]{:S(2)}) async-start(bf16[8,128,640]{2,1,0:T(8,128)(2,1)} %bitcast.290), calls=%async_computation.2 | async-start | bytes 2621440 | tf_op jit(solution)/shard_map/all_to_all | solution.py:57
  99.2 1.9 fusion.73
  101.5 4.2 %fusion.18 = f32[8,128,10,64]{1,3,2,0:T(8,128)S(1)} fusion(bf16[8,128,10,64]{1,3,2,0:T(8,128)(2,1)S(1)} %bitcast.317, f32[8,10,128]{2,1,0:T(8,128)S(1)} %copy-done.17, f32[8,10,128]{2,1,0:T(8,128)S(1)} %copy-done.18, f32[8,10,128]{2,1,0:T(8,128)S(1)} %copy-done.19, f32[8,128,128]{2,1,0:T(8,128)S(1)} %fusion.44, pred[8,128,128]{2,1,0:T(8,128)(4,1)S(1)} %copy-done.16, ...), kind=kOutput, calls=%fused_computation.29 | convolution fusion | flops 175636480 | bytes 4726784 | tf_op jit(solution)/shard_map/shtj,sjhp->sthp/dot_general | solution.py:161
  109.5 2.1 %copy.97 = f32[80,8,8,128]{3,1,2,0:T(8,128)} copy(f32[80,8,8,128]{3,2,1,0:T(8,128)S(1)} %bitcast.298) | data formatting | bytes 5242880
  111.6 3.4 %copy.58 = f32[1024,640]{1,0:T(8,128)} copy(f32[1024,640]{0,1:T(8,128)} %bitcast.299) | data formatting | bytes 5242880 | tf_op jit(solution)/shard_map/reshape | solution.py:166
  115.0 2.1 %copy.59 = f32[8,128,640]{2,1,0:T(8,128)} copy(f32[8,128,640]{1,2,0:T(8,128)S(1)} %copy-done.3) | data formatting | bytes 5242880 | tf_op jit(solution)/shard_map/convert_element_type | solution.py:108
  117.9 3.0 %collective-permute-start.2 = (bf16[128,640]{1,0:T(8,128)(2,1)}, bf16[128,640]{1,0:T(8,128)(2,1)S(1)}, u32[]{:S(2)}, u32[]{:S(2)}) collective-permute-start(bf16[128,640]{1,0:T(8,128)(2,1)} %add_convert_fusion.2), channel_id=1, source_target_pairs={{0,16},{1,17},{2,18},{3,19},{4,20},{5,21},{6,22},{7,23},{8,24},{9,... | collective-permute-start | bytes 491528 | tf_op jit(solution)/shard_map/ppermute | solution.py:16
  120.9 2.0 %fusion.79 = f32[1024,640]{1,0:T(8,128)} fusion(bf16[1024,128]{1,0:T(8,128)(2,1)S(1)} %bitcast.307, bf16[128,640]{1,0:T(8,128)(2,1)S(1)} %collective-permute-done), kind=kOutput, calls=%fused_computation.182 | convolution fusion | flops 167772160 | bytes 3047424 | tf_op jit(solution)/shard_map/dot_general | solution.py:138
  122.9 5.7 %collective-permute-done.2 = bf16[128,640]{1,0:T(8,128)(2,1)S(1)} collective-permute-done((bf16[128,640]{1,0:T(8,128)(2,1)}, bf16[128,640]{1,0:T(8,128)(2,1)S(1)}, u32[]{:S(2)}, u32[]{:S(2)}) %collective-permute-start.2) | collective-permute-done | bytes 163872 | tf_op jit(solution)/shard_map/ppermute | solution.py:16
  128.6 8.0 %multiply_reduce_fusion = (f32[1024]{0:T(1024)S(1)}, bf16[1024,640]{1,0:T(8,128)(2,1)S(1)}) fusion(f32[640]{0:T(1024)S(1)} %dynamic_slice.108, bf16[1024,640]{1,0:T(8,128)(2,1)} %bitcast.51, f32[8,128,640]{2,1,0:T(8,128)} %copy.59, f32[640]{0:T(1024)S(1)} %mul.193, f32[1024,640]{1,0:T(8,128)} %copy.58, f32[1024,640]{1,0:T(8,128)} %copy.57, ...), kind=kOutput, calls=%fused_computation.18 | convolution fusion | flops 180222976 | bytes 24028160 | tf_op jit(solution)/shard_map/dot_general | solution.py:138
  136.7 2.6 %fusion.81 = f32[1024,640]{1,0:T(8,128)S(1)} fusion(bf16[1024,640]{1,0:T(8,128)(2,1)S(1)} %get-tuple-element.10, bf16[640,640]{1,0:T(8,128)(2,1)} %collective-permute-done.9), kind=kOutput, calls=%fused_computation.184 | convolution fusion | flops 838860800 | bytes 4751360 | tf_op jit(solution)/shard_map/dot_general | solution.py:194
  147.2 2.5 %fusion.82 = f32[1024,640]{1,0:T(8,128)S(1)} fusion(bf16[1024,640]{1,0:T(8,128)(2,1)S(1)} %get-tuple-element.10, bf16[640,640]{1,0:T(8,128)(2,1)} %collective-permute-done.13), kind=kOutput, calls=%fused_computation.185 | convolution fusion | flops 838860800 | bytes 4751360 | tf_op jit(solution)/shard_map/dot_general | solution.py:194
  153.6 6.7 %collective-permute-done.11 = bf16[2,128,640]{2,1,0:T(8,128)(2,1)S(1)} collective-permute-done((bf16[2,128,640]{2,1,0:T(8,128)(2,1)S(1)}, bf16[2,128,640]{2,1,0:T(8,128)(2,1)S(1)}, u32[]{:S(2)}, u32[]{:S(2)}) %collective-permute-start.11) | collective-permute-done | bytes 327712 | tf_op jit(solution)/shard_map/ppermute | solution.py:16
  163.7 8.8 %collective-permute-done.17 = bf16[640,640]{1,0:T(8,128)(2,1)S(1)} collective-permute-done((bf16[640,640]{1,0:T(8,128)(2,1)}, bf16[640,640]{1,0:T(8,128)(2,1)S(1)}, u32[]{:S(2)}, u32[]{:S(2)}) %collective-permute-start.17) | collective-permute-done | bytes 819232 | tf_op jit(solution)/shard_map/ppermute | solution.py:90
  178.1 6.4 %collective-permute-done.15 = bf16[2,128,640]{2,1,0:T(8,128)(2,1)S(1)} collective-permute-done((bf16[2,128,640]{2,1,0:T(8,128)(2,1)S(1)}, bf16[2,128,640]{2,1,0:T(8,128)(2,1)S(1)}, u32[]{:S(2)}, u32[]{:S(2)}) %collective-permute-start.15) | collective-permute-done | bytes 327712 | tf_op jit(solution)/shard_map/ppermute | solution.py:16
  188.0 2.4 %collective-permute-done.16 = bf16[128,640]{1,0:T(8,128)(2,1)S(1)} collective-permute-done((bf16[128,640]{1,0:T(8,128)(2,1)S(1)}, bf16[128,640]{1,0:T(8,128)(2,1)S(1)}, u32[]{:S(2)}, u32[]{:S(2)}) %collective-permute-start.16) | collective-permute-done | bytes 163872 | tf_op jit(solution)/shard_map/ppermute | solution.py:16
  (223 shorter events, 76.9 us)
Async XLA Ops:
  2.8 12.9 %all-to-all-start.1 = ((f32[8,128,12]{1,2,0:T(8,128)}), f32[8,128,12]{1,2,0:T(8,128)S(1)}, u32[]{:S(2)}, u32[]{:S(2)}) async-start(f32[8,128,12]{1,2,0:T(8,128)} %pad_maximum_fusion.2), calls=%async_computation.1 | async-start | bytes 131072 | tf_op jit(solution)/shard_map/all_to_all | solution.py:57
  15.7 33.0 %all-to-all-start.3 = ((bf16[8,80,640]{2,1,0:T(8,128)(2,1)}), bf16[8,80,640]{2,1,0:T(8,128)(2,1)S(1)}, u32[]{:S(2)}, u32[]{:S(2)}) async-start(bf16[8,80,640]{2,1,0:T(8,128)(2,1)} %bitcast.292), calls=%async_computation.3 | async-start | bytes 1638400 | tf_op jit(solution)/shard_map/all_to_all | solution.py:57
  43.6 5.1 %collective-permute-start.1 = (f32[1,10]{1,0:T(1,128)S(1)}, f32[1,10]{1,0:T(1,128)S(1)}, u32[]{:S(2)}, u32[]{:S(2)}) collective-permute-start(f32[1,10]{1,0:T(1,128)S(1)} %get-tuple-element.35), channel_id=1, source_target_pairs={{0,8},{1,9},{2,10},{3,11},{4,12},{5,13},{6,14},{7,15},{8,0},{9,1},... | collective-permute-start | bytes 128 | tf_op jit(solution)/shard_map/ppermute | solution.py:16
  49.6 33.2 %all-to-all-start = ((bf16[8,128,896]{1,2,0:T(8,128)(2,1)}), bf16[8,128,896]{1,2,0:T(8,128)(2,1)S(1)}, u32[]{:S(2)}, u32[]{:S(2)}) async-start(bf16[8,128,896]{1,2,0:T(8,128)(2,1)} %pad_maximum_fusion), calls=%async_computation | async-start | bytes 3670016 | tf_op jit(solution)/shard_map/all_to_all | solution.py:57
  60.0 22.8 %collective-permute-start.9 = (bf16[640,640]{1,0:T(8,128)(2,1)}, bf16[640,640]{1,0:T(8,128)(2,1)}, u32[]{:S(2)}, u32[]{:S(2)}) collective-permute-start(bf16[640,640]{1,0:T(8,128)(2,1)} %bitcast.321), channel_id=1, source_target_pairs={{0,8},{1,9},{2,10},{3,11},{4,12},{5,13},{6,14},{7,15},{8,16},{9,17... | collective-permute-start | bytes 2457608 | tf_op jit(solution)/shard_map/ppermute | solution.py:90
  82.8 64.4 %collective-permute-start.13 = (bf16[640,640]{1,0:T(8,128)(2,1)}, bf16[640,640]{1,0:T(8,128)(2,1)}, u32[]{:S(2)}, u32[]{:S(2)}) collective-permute-start(bf16[640,640]{1,0:T(8,128)(2,1)} %collective-permute-done.9), channel_id=1, source_target_pairs={{0,8},{1,9},{2,10},{3,11},{4,12},{5,13},{6,14},{7,15},{8,16},{9,17... | collective-permute-start | bytes 2457608 | tf_op jit(solution)/shard_map/ppermute | solution.py:90
  82.8 40.1 %all-to-all-start.2 = ((bf16[8,128,640]{2,1,0:T(8,128)(2,1)}), bf16[8,128,640]{2,1,0:T(8,128)(2,1)}, u32[]{:S(2)}, u32[]{:S(2)}) async-start(bf16[8,128,640]{2,1,0:T(8,128)(2,1)} %bitcast.290), calls=%async_computation.2 | async-start | bytes 2621440 | tf_op jit(solution)/shard_map/all_to_all | solution.py:57
  97.8 19.3 %collective-permute-start = (bf16[128,640]{1,0:T(8,128)(2,1)}, bf16[128,640]{1,0:T(8,128)(2,1)S(1)}, u32[]{:S(2)}, u32[]{:S(2)}) collective-permute-start(bf16[128,640]{1,0:T(8,128)(2,1)} %fusion.46), channel_id=1, source_target_pairs={{0,8},{1,9},{2,10},{3,11},{4,12},{5,13},{6,14},{7,15},{8,0},{9,1},... | collective-permute-start | bytes 491528 | tf_op jit(solution)/shard_map/ppermute | solution.py:16
  117.9 10.8 %collective-permute-start.2 = (bf16[128,640]{1,0:T(8,128)(2,1)}, bf16[128,640]{1,0:T(8,128)(2,1)S(1)}, u32[]{:S(2)}, u32[]{:S(2)}) collective-permute-start(bf16[128,640]{1,0:T(8,128)(2,1)} %add_convert_fusion.2), channel_id=1, source_target_pairs={{0,16},{1,17},{2,18},{3,19},{4,20},{5,21},{6,22},{7,23},{8,24},{9,... | collective-permute-start | bytes 491528 | tf_op jit(solution)/shard_map/ppermute | solution.py:16
  136.6 3.3 %collective-permute-start.6 = (f32[2,2,128]{2,1,0:T(2,128)S(1)}, f32[2,2,128]{2,1,0:T(2,128)S(1)}, u32[]{:S(2)}, u32[]{:S(2)}) collective-permute-start(f32[2,2,128]{2,1,0:T(2,128)S(1)} %bitcast.346), channel_id=1, source_target_pairs={{0,1},{1,0},{2,3},{3,2},{4,5},{5,4},{6,7},{7,6},{8,9},{9,8},{10,11... | collective-permute-start | bytes 6152 | tf_op jit(solution)/shard_map/ppermute | solution.py:16
  139.4 10.6 %collective-permute-start.10 = (bf16[2,2,128,640]{3,2,1,0:T(8,128)(2,1)S(1)}, bf16[2,2,128,640]{3,2,1,0:T(8,128)(2,1)S(1)}, u32[]{:S(2)}, u32[]{:S(2)}) collective-permute-start(bf16[2,2,128,640]{3,2,1,0:T(8,128)(2,1)S(1)} %fusion.24), channel_id=1, source_target_pairs={{0,1},{1,0},{2,3},{3,2},{4,5},{5,4},{6,7},{7,6},{8,9},{9,8},{10,11... | collective-permute-start | bytes 1966088 | tf_op jit(solution)/shard_map/ppermute | solution.py:16
  139.9 3.6 %collective-permute-start.7 = (f32[2,128]{1,0:T(2,128)S(1)}, f32[2,128]{1,0:T(2,128)S(1)}, u32[]{:S(2)}, u32[]{:S(2)}) collective-permute-start(f32[2,128]{1,0:T(2,128)S(1)} %bitcast.347), channel_id=1, source_target_pairs={{0,2},{1,3},{2,0},{3,1},{4,6},{5,7},{6,4},{7,5},{8,10},{9,11},{10,... | collective-permute-start | bytes 3080 | tf_op jit(solution)/shard_map/ppermute | solution.py:16
  143.6 3.6 %collective-permute-start.8 = (f32[128]{0:T(128)S(1)}, f32[128]{0:T(128)S(1)}, u32[]{:S(2)}, u32[]{:S(2)}) collective-permute-start(f32[128]{0:T(128)S(1)} %fusion.70), channel_id=1, source_target_pairs={{0,4},{1,5},{2,6},{3,7},{4,0},{5,1},{6,2},{7,3},{8,12},{9,13},{10,... | collective-permute-start | bytes 1544 | tf_op jit(solution)/shard_map/ppermute | solution.py:16
  145.4 6.5 %collective-permute-start.3 = (bf16[2,2,128,640]{3,2,1,0:T(8,128)(2,1)S(1)}, bf16[2,2,128,640]{3,2,1,0:T(8,128)(2,1)S(1)}, u32[]{:S(2)}, u32[]{:S(2)}) collective-permute-start(bf16[2,2,128,640]{3,2,1,0:T(8,128)(2,1)S(1)} %fusion.22), channel_id=1, source_target_pairs={{0,1},{1,0},{2,3},{3,2},{4,5},{5,4},{6,7},{7,6},{8,9},{9,8},{10,11... | collective-permute-start | bytes 1966088 | tf_op jit(solution)/shard_map/ppermute | solution.py:16
  149.8 24.3 %collective-permute-start.14 = (bf16[2,2,128,640]{3,2,0,1:T(8,128)(2,1)S(1)}, bf16[2,2,128,640]{3,2,0,1:T(8,128)(2,1)S(1)}, u32[]{:S(2)}, u32[]{:S(2)}) collective-permute-start(bf16[2,2,128,640]{3,2,0,1:T(8,128)(2,1)S(1)} %fusion.23), channel_id=1, source_target_pairs={{0,1},{1,0},{2,3},{3,2},{4,5},{5,4},{6,7},{7,6},{8,9},{9,8},{10,11... | collective-permute-start | bytes 1966088 | tf_op jit(solution)/shard_map/ppermute | solution.py:16
  149.9 22.7 %collective-permute-start.17 = (bf16[640,640]{1,0:T(8,128)(2,1)}, bf16[640,640]{1,0:T(8,128)(2,1)S(1)}, u32[]{:S(2)}, u32[]{:S(2)}) collective-permute-start(bf16[640,640]{1,0:T(8,128)(2,1)} %collective-permute-done.13), channel_id=1, source_target_pairs={{0,8},{1,9},{2,10},{3,11},{4,12},{5,13},{6,14},{7,15},{8,16},{9,17... | collective-permute-start | bytes 2457608 | tf_op jit(solution)/shard_map/ppermute | solution.py:90
  150.2 10.1 %collective-permute-start.11 = (bf16[2,128,640]{2,1,0:T(8,128)(2,1)S(1)}, bf16[2,128,640]{2,1,0:T(8,128)(2,1)S(1)}, u32[]{:S(2)}, u32[]{:S(2)}) collective-permute-start(bf16[2,128,640]{2,1,0:T(8,128)(2,1)S(1)} %fusion.28), channel_id=1, source_target_pairs={{0,4},{1,5},{2,6},{3,7},{4,0},{5,1},{6,2},{7,3},{8,12},{9,13},{10,... | collective-permute-start | bytes 983048 | tf_op jit(solution)/shard_map/ppermute | solution.py:16
  152.1 10.0 %collective-permute-start.4 = (bf16[2,128,640]{2,1,0:T(8,128)(2,1)S(1)}, bf16[2,128,640]{2,1,0:T(8,128)(2,1)S(1)}, u32[]{:S(2)}, u32[]{:S(2)}) collective-permute-start(bf16[2,128,640]{2,1,0:T(8,128)(2,1)S(1)} %fusion.27), channel_id=1, source_target_pairs={{0,2},{1,3},{2,0},{3,1},{4,6},{5,7},{6,4},{7,5},{8,10},{9,11},{10,... | collective-permute-start | bytes 983048 | tf_op jit(solution)/shard_map/ppermute | solution.py:16
  160.4 15.8 %collective-permute-start.12 = (bf16[128,640]{1,0:T(8,128)(2,1)S(1)}, bf16[128,640]{1,0:T(8,128)(2,1)S(1)}, u32[]{:S(2)}, u32[]{:S(2)}) collective-permute-start(bf16[128,640]{1,0:T(8,128)(2,1)S(1)} %fusion.48), channel_id=1, source_target_pairs={{0,2},{1,3},{2,0},{3,1},{4,6},{5,7},{6,4},{7,5},{8,10},{9,11},{10,... | collective-permute-start | bytes 491528 | tf_op jit(solution)/shard_map/ppermute | solution.py:16
  162.2 13.8 %collective-permute-start.5 = (bf16[128,640]{1,0:T(8,128)(2,1)S(1)}, bf16[128,640]{1,0:T(8,128)(2,1)S(1)}, u32[]{:S(2)}, u32[]{:S(2)}) collective-permute-start(bf16[128,640]{1,0:T(8,128)(2,1)S(1)} %fusion.47), channel_id=1, source_target_pairs={{0,4},{1,5},{2,6},{3,7},{4,0},{5,1},{6,2},{7,3},{8,12},{9,13},{10,... | collective-permute-start | bytes 491528 | tf_op jit(solution)/shard_map/ppermute | solution.py:16
  174.3 10.2 %collective-permute-start.15 = (bf16[2,128,640]{2,1,0:T(8,128)(2,1)S(1)}, bf16[2,128,640]{2,1,0:T(8,128)(2,1)S(1)}, u32[]{:S(2)}, u32[]{:S(2)}) collective-permute-start(bf16[2,128,640]{2,1,0:T(8,128)(2,1)S(1)} %fusion.29), channel_id=1, source_target_pairs={{0,2},{1,3},{2,0},{3,1},{4,6},{5,7},{6,4},{7,5},{8,10},{9,11},{10,... | collective-permute-start | bytes 983048 | tf_op jit(solution)/shard_map/ppermute | solution.py:16
  176.4 9.9 %collective-permute-start.19 = (bf16[2,128,640]{2,1,0:T(8,128)(2,1)S(1)}, bf16[2,128,640]{2,1,0:T(8,128)(2,1)S(1)}, u32[]{:S(2)}, u32[]{:S(2)}) collective-permute-start(bf16[2,128,640]{2,1,0:T(8,128)(2,1)S(1)} %fusion.30), channel_id=1, source_target_pairs={{0,4},{1,5},{2,6},{3,7},{4,0},{5,1},{6,2},{7,3},{8,12},{9,13},{10,... | collective-permute-start | bytes 983048 | tf_op jit(solution)/shard_map/ppermute | solution.py:16
  184.5 5.8 %collective-permute-start.16 = (bf16[128,640]{1,0:T(8,128)(2,1)S(1)}, bf16[128,640]{1,0:T(8,128)(2,1)S(1)}, u32[]{:S(2)}, u32[]{:S(2)}) collective-permute-start(bf16[128,640]{1,0:T(8,128)(2,1)S(1)} %fusion.49), channel_id=1, source_target_pairs={{0,4},{1,5},{2,6},{3,7},{4,0},{5,1},{6,2},{7,3},{8,12},{9,13},{10,... | collective-permute-start | bytes 491528 | tf_op jit(solution)/shard_map/ppermute | solution.py:16
  186.4 5.5 %collective-permute-start.20 = (bf16[128,640]{1,0:T(8,128)(2,1)S(1)}, bf16[128,640]{1,0:T(8,128)(2,1)S(1)}, u32[]{:S(2)}, u32[]{:S(2)}) collective-permute-start(bf16[128,640]{1,0:T(8,128)(2,1)S(1)} %fusion.50), channel_id=1, source_target_pairs={{0,2},{1,3},{2,0},{3,1},{4,6},{5,7},{6,4},{7,5},{8,10},{9,11},{10,... | collective-permute-start | bytes 491528 | tf_op jit(solution)/shard_map/ppermute | solution.py:16
  (25 other events, 111.8 us)

commit v2 on v1

--- a/solution.py
+++ b/solution.py
@@ -3,6 +3,8 @@
 import jax
 import jax.numpy as jnp
 from jax import lax
+from jax.experimental import pallas as pl
+from jax.experimental.pallas import tpu as pltpu
 from jax.sharding import PartitionSpec as P
 
 epsilon = 1e-05
@@ -18,6 +20,192 @@
 
 def widen(matrix, head_dim):
     return jnp.repeat(matrix, head_dim, axis=-1)
+
+
+def spread(scale, expand):
+    return jnp.dot(scale, expand, precision=highest, preferred_element_type=f32)
+
+
+def state_kernel(bits, state_dim, packed_ref, scale_ref, up_ref, expand_ref, *outs):
+    A = packed_ref.shape[0]
+    expand = expand_ref[...]
+    up_wide = spread(up_ref[...], expand)
+    for s in range(A):
+        decayed = packed_ref[s, :, 2 * state_dim :].astype(f32) * spread(scale_ref[s], expand)
+        keys = packed_ref[s, :, state_dim : 2 * state_dim]
+        outs[0][s] = lax.dot_general(
+            keys,
+            decayed.astype(bf16),
+            (((0,), (0,)), ((), ())),
+            preferred_element_type=f32,
+        ).astype(bf16)
+    row = 0
+    for b in range(bits):
+        for g in range(A >> (b + 1)):
+            low = outs[b][2 * g].astype(f32)
+            high = outs[b][2 * g + 1].astype(f32)
+            merged = (high + up_wide[row : row + 1] * low).astype(bf16)
+            if b + 1 < bits:
+                outs[b + 1][g] = merged
+            else:
+                outs[b + 1][...] = merged
+            row += 1
+
+
+def state_call(packed, end_scale, up_rows, expand, *, state_dim, bits):
+    A, _, width = packed.shape
+    cg = width - 2 * state_dim
+    shapes = [(A >> b, state_dim, cg) for b in range(bits)] + [(state_dim, cg)]
+    vmem = pl.BlockSpec(memory_space=pltpu.VMEM)
+    return pl.pallas_call(
+        lambda *refs: state_kernel(bits, state_dim, *refs),
+        out_shape=[jax.ShapeDtypeStruct(shape, bf16) for shape in shapes],
+        in_specs=[vmem] * 4,
+        out_specs=[vmem] * len(shapes),
+        name="group_states",
+        cost_estimate=pl.CostEstimate(
+            flops=1 << 29, bytes_accessed=8 << 20, transcendentals=0
+        ),
+    )(packed, end_scale, up_rows, expand)
+
+
+def local_kernel(
+    state_dim, head_dim, bits, packed_ref, cum_ref, cum_t_ref, scale_ref, seg_ref,
+    seg_t_ref, skip_ref, expand_ref, *rest
+):
+    states, out_ref = rest[:bits], rest[bits]
+    tok, hg = cum_ref.shape[1:]
+    cg = expand_ref.shape[1]
+    q = packed_ref[0, :, :state_dim]
+    keys = packed_ref[0, :, state_dim : 2 * state_dim]
+    expand = expand_ref[...]
+    scores = lax.dot_general(
+        q, keys, (((1,), (1,)), ((), ())), preferred_element_type=f32
+    )
+    same = seg_ref[0] == seg_t_ref[0]
+    t_pos = lax.broadcasted_iota(jnp.int32, (tok, tok), 0)
+    j_pos = lax.broadcasted_iota(jnp.int32, (tok, tok), 1)
+    causal = t_pos >= j_pos
+    scales = scale_ref[0]
+    cum = cum_ref[0]
+    cum_t = cum_t_ref[0]
+    x_wide = packed_ref[0, :, 2 * state_dim :]
+    acc = skip_ref[...] * x_wide.astype(f32)
+    for b in range(bits):
+        read = jnp.dot(q, states[b][0], preferred_element_type=f32)
+        acc = acc + read * spread(scales[:, (2 + b) * hg : (3 + b) * hg], expand)
+    out_ref[...] = acc
+
+    def head_weights(h):
+        gaps = jnp.where(causal, cum[:, h : h + 1] - cum_t[h : h + 1, :], -jnp.inf)
+        level_w = jnp.where(same, scales[:, h : h + 1], scales[:, hg + h : hg + h + 1])
+        return (scores * jnp.exp(gaps) * level_w).astype(bf16)
+
+    per_tile = max(1, 128 // head_dim)
+    for first in range(0, hg, per_tile):
+        heads = range(first, min(first + per_tile, hg))
+        low, high = first * head_dim, min((first + per_tile) * head_dim, cg)
+        x_tile = x_wide[:, low:high]
+        lane_head = lax.broadcasted_iota(jnp.int32, (tok, high - low), 1) // head_dim
+        tile = None
+        for h in heads:
+            part = jnp.dot(head_weights(h), x_tile, preferred_element_type=f32)
+            tile = part if tile is None else jnp.where(lane_head == h - first, part, tile)
+        out_ref[:, low:high] += tile
+
+
+def local_call(
+    packed, cum, cum_t, scales, seg, level_states, skip, expand, *, state_dim, head_dim
+):
+    A, tok, width = packed.shape
+    cg = width - 2 * state_dim
+    hg = cum.shape[2]
+    bits = len(level_states)
+
+    def shard_spec(*dims):
+        return pl.BlockSpec((1,) + dims, lambda s: (s, 0, 0))
+
+    def sibling_spec(b):
+        return pl.BlockSpec(
+            (1, state_dim, cg), lambda s: (jnp.maximum(s // 2**b - 1, 0), 0, 0)
+        )
+
+    def whole_spec(shape):
+        return pl.BlockSpec(shape, lambda s: (0, 0))
+
+    return pl.pallas_call(
+        lambda *refs: local_kernel(state_dim, head_dim, bits, *refs),
+        grid=(A,),
+        out_shape=jax.ShapeDtypeStruct((A * tok, cg), f32),
+        in_specs=[
+            shard_spec(tok, width),
+            shard_spec(tok, hg),
+            shard_spec(hg, tok),
+            shard_spec(tok, scales.shape[2]),
+            shard_spec(tok, 1),
+            shard_spec(1, tok),
+            whole_spec((1, cg)),
+            whole_spec(expand.shape),
+        ]
+        + [sibling_spec(b) for b in range(bits)],
+        out_specs=pl.BlockSpec((tok, cg), lambda s: (s, 0)),
+        name="local_mix",
+        cost_estimate=pl.CostEstimate(
+            flops=1 << 32, bytes_accessed=12 << 20, transcendentals=1 << 21
+        ),
+    )(packed, cum, cum_t, scales, seg[:, :, None], seg[:, None, :], skip, expand, *level_states)
+
+
+def gate_kernel(levels, packed_ref, mixed_ref, scale_ref, gates_ref, gain_ref, expand_ref, *rest):
+    others, (hidden_ref, square_ref) = rest[:levels], rest[levels:]
+    hg = expand_ref.shape[0]
+    q = packed_ref[0]
+    expand = expand_ref[...]
+    scales = scale_ref[0]
+    acc = mixed_ref[...]
+    for level in range(levels):
+        read = jnp.dot(q, others[level][...], preferred_element_type=f32)
+        acc = acc + read * spread(scales[:, level * hg : (level + 1) * hg], expand)
+    gate = gates_ref[0].astype(f32)
+    gated = acc * (gate / (1.0 + jnp.exp(-gate)))
+    square_ref[0] = jnp.sum(gated * gated, axis=1, keepdims=True)
+    hidden_ref[...] = (gated * gain_ref[...]).astype(bf16)
+
+
+def gate_call(packed, mixed, others, other_scales, gates, gain, expand, *, state_dim):
+    A, tok, cg = gates.shape
+    levels = len(others)
+    scales = jnp.concatenate(other_scales, axis=2)
+
+    def shard_spec(*dims):
+        return pl.BlockSpec((1,) + dims, lambda s: (s, 0, 0))
+
+    def whole_spec(shape):
+        return pl.BlockSpec(shape, lambda s: (0, 0))
+
+    rows_spec = pl.BlockSpec((tok, cg), lambda s: (s, 0))
+    return pl.pallas_call(
+        lambda *refs: gate_kernel(levels, *refs),
+        grid=(A,),
+        out_shape=[
+            jax.ShapeDtypeStruct((A * tok, cg), bf16),
+            jax.ShapeDtypeStruct((A, tok, 1), f32),
+        ],
+        in_specs=[
+            shard_spec(tok, state_dim),
+            rows_spec,
+            shard_spec(tok, scales.shape[2]),
+            shard_spec(tok, cg),
+            whole_spec((1, cg)),
+            whole_spec(expand.shape),
+        ]
+        + [whole_spec((state_dim, cg))] * levels,
+        out_specs=[rows_spec, shard_spec(tok, 1)],
+        name="gate_mix",
+        cost_estimate=pl.CostEstimate(
+            flops=1 << 30, bytes_accessed=8 << 20, transcendentals=1 << 20
+        ),
+    )(packed, mixed, scales, gates, gain, expand, *others)
 
 
 def per_device(
@@ -64,17 +252,18 @@
     w_blocks = out_proj.T.reshape(out_cols, A, cg).swapaxes(0, 1)
     w_block = exchange(w_blocks).reshape(A * out_cols, cg)
 
+    cum_own = jnp.cumsum(log_decay, axis=0)
     shared = jnp.concatenate([queries, key_rows], axis=1)
     packed = jnp.concatenate(
         [
+            jnp.broadcast_to(shared[None], (A, tok, 2 * state_dim)),
             values.reshape(tok, A, cg).swapaxes(0, 1),
-            jnp.broadcast_to(shared[None], (A, tok, 2 * state_dim)),
         ],
         axis=2,
     )
     small = jnp.concatenate(
         [
-            log_decay.reshape(tok, A, hg).swapaxes(0, 1),
+            cum_own.reshape(tok, A, hg).swapaxes(0, 1),
             jnp.broadcast_to(lam_index.astype(f32)[None, :, None], (A, tok, 1)),
             jnp.broadcast_to(segments.astype(f32)[None, :, None], (A, tok, 1)),
         ],
@@ -92,53 +281,53 @@
             )
         )
 
-    x = packed[:, :, :cg]
-    q = packed[:, :, cg : cg + state_dim]
-    k = packed[:, :, cg + state_dim :]
-    ld = small[:, :, :hg]
+    cum = small[:, :, :hg]
     lam = small[:, :, hg].reshape(rows).astype(jnp.int32)
     seg = small[:, :, hg + 1]
-
-    cum = jnp.cumsum(ld, axis=1)
     span = cum[:, -1, :]
     onehot = (lam[:, None] == jnp.arange(classes, dtype=jnp.int32)[None, :]).astype(f32)
     table = my_heads(lam_table, hg, 2).reshape(classes, level_count * hg)
-    lw = jnp.dot(onehot, table, precision=highest).reshape(A, tok, level_count, hg)
-
-    decayed = (x.astype(f32) * widen(jnp.exp(span[:, None, :] - cum), head_dim)).astype(bf16)
-    state = jnp.einsum("sjn,sjc->snc", k, decayed, preferred_element_type=f32).astype(bf16)
-
-    cross = jnp.zeros((rows, cg), f32)
+    lw = jnp.dot(onehot, table, precision=highest).reshape(A, tok, level_count * hg)
+    expand = (
+        jnp.arange(hg, dtype=jnp.int32)[:, None]
+        == jnp.arange(cg, dtype=jnp.int32)[None, :] // head_dim
+    ).astype(f32)
+
     total = span
     prefix = jnp.zeros((A, hg), f32)
+    prefixes = []
+    up_factors = []
     for b in range(a_bits):
-        pairs = A >> (b + 1)
-        lower, upper = state[0::2], state[1::2]
+        wide = 2**b
         low_total, up_total = total[0::2], total[1::2]
-        wide = 2**b
-        q_up = q.reshape(pairs, 2, wide * tok, state_dim)[:, 1]
-        read = jnp.einsum("gtn,gnc->gtc", q_up, lower, preferred_element_type=f32)
-        scale = (jnp.exp(cum + prefix[:, None, :]) * lw[:, :, 2 + b, :]).reshape(
-            pairs, 2, wide * tok, hg
-        )[:, 1]
-        read = read * widen(scale, head_dim)
-        cross = cross + jnp.stack([jnp.zeros_like(read), read], axis=1).reshape(rows, cg)
-        factor = widen(jnp.exp(up_total), head_dim)[:, None, :]
-        state = (upper.astype(f32) + factor * lower.astype(f32)).astype(bf16)
-        is_up = jnp.arange(A, dtype=jnp.int32) // wide % 2 == 1
-        low_rows = jnp.repeat(low_total, 2 * wide, axis=0)
-        prefix = prefix + jnp.where(is_up[:, None], low_rows, 0.0)
+        is_up = (jnp.arange(A, dtype=jnp.int32) // wide % 2 == 1)[:, None]
+        prefixes.append(jnp.where(is_up, prefix, -jnp.inf))
+        up_factors.append(jnp.exp(up_total))
+        prefix = prefix + jnp.where(is_up, jnp.repeat(low_total, 2 * wide, axis=0), 0.0)
         total = low_total + up_total
-    state, total = state[0], total[0]
-    q_rows = q.reshape(rows, state_dim)
+    total = total[0]
+
+    def level_scale(before, level):
+        weight = lw[:, :, (2 + level) * hg : (3 + level) * hg]
+        return jnp.exp(cum + before[:, None, :]) * weight
+
+    end_scale = jnp.exp(span[:, None, :] - cum)
+    up_rows = jnp.concatenate(up_factors, axis=0)
+    *level_states, state = state_call(
+        packed, end_scale, up_rows, expand, state_dim=state_dim, bits=a_bits
+    )
+    local_scales = [lw[:, :, : 2 * hg]]
+    local_scales += [level_scale(before, b) for b, before in enumerate(prefixes)]
+    local_scales = jnp.concatenate(local_scales, axis=2)
+
+    others, other_scales = [], []
     for zb in range(z_bits):
         other = xor_permute(state, A << zb)
         other_total = xor_permute(total[None, :], A << zb)[0]
         is_up = jnp.bitwise_and(jnp.right_shift(z_pos, zb), 1) == 1
-        read = jnp.dot(q_rows, other, preferred_element_type=f32)
-        scale = jnp.exp(cum + prefix[:, None, :]) * lw[:, :, 2 + a_bits + zb, :]
-        scale = jnp.where(is_up, scale, 0.0).reshape(rows, hg)
-        cross = cross + read * widen(scale, head_dim)
+        others.append(other)
+        before = jnp.where(is_up, prefix, -jnp.inf)
+        other_scales.append(level_scale(before, a_bits + zb))
         if zb + 1 < z_bits:
             up_state = jnp.where(is_up, state, other).astype(f32)
             low_state = jnp.where(is_up, other, state).astype(f32)
@@ -147,29 +336,15 @@
             prefix = prefix + jnp.where(is_up, other_total, 0.0)[None, :]
             total = total + other_total
 
-    scores = jnp.einsum("stn,sjn->stj", q, k, preferred_element_type=f32)
-    pos = jnp.arange(tok, dtype=jnp.int32)
-    causal = pos[:, None] >= pos[None, :]
-    cum_h = cum.swapaxes(1, 2)
-    gaps = jnp.where(causal, cum_h[:, :, :, None] - cum_h[:, :, None, :], -jnp.inf)
-    same = seg[:, :, None] == seg[:, None, :]
-    lw0 = lw[:, :, 0, :].swapaxes(1, 2)[:, :, :, None]
-    lw1 = lw[:, :, 1, :].swapaxes(1, 2)[:, :, :, None]
-    weights = (
-        scores[:, None] * jnp.exp(gaps) * jnp.where(same[:, None], lw0, lw1)
-    ).astype(bf16)
-    local = jnp.einsum(
-        "shtj,sjhp->sthp",
-        weights,
-        x.reshape(A, tok, hg, head_dim),
-        preferred_element_type=f32,
-    ).reshape(rows, cg)
-
     skip = widen(my_heads(skip_gain, hg, 0), head_dim)[None, :]
-    mixer = local + cross + skip * x.reshape(rows, cg).astype(f32)
-    gated = mixer * jax.nn.silu(gates.reshape(rows, cg).astype(f32))
-    squares = jnp.sum(gated * gated, axis=1)
-    hidden = (gated * my_heads(norm_gain, cg, 0)[None, :]).astype(bf16)
+    mixed = local_call(
+        packed, cum, cum.swapaxes(1, 2), local_scales, seg, level_states, skip, expand,
+        state_dim=state_dim, head_dim=head_dim,
+    )
+    gain = my_heads(norm_gain, cg, 0)[None, :]
+    hidden, squares = gate_call(
+        packed, mixed, others, other_scales, gates, gain, expand, state_dim=state_dim
+    )
 
     def reduce_group(part, order, narrow):
         left = list(range(a_bits))[::-1]

time: 194 us -> 199 us (1.026)
  local copies, waits for them, and re-layouts: 52.4 us -> 16.8 us
  waiting for transfers between devices: 37.4 us -> 67.9 us
  Pallas kernels: 0 us -> 28.5 us
  matrix products: 24.2 us -> 8.43 us
  starting transfers between devices: 42.1 us -> 40 us
    pallas_call x0 -> x3, Pallas kernels: none -> 28.5 us  [the longest x1 12.1 us: local_call(): pl.pallas_call(lambda *refs: local_kernel(state_dim, head_dim, bits, *ref...]
    all_to_all x4, waiting for transfers between devices: 0.01 us -> 24 us  [exchange(): lax.all_to_all(blocks, 'seq', 0, 0, tiled=True, axis_index_groups=groups)]
    dot_general x9 -> x1, matrix products: 16.4 us -> 0.44 us  [per_device(): jnp.dot(onehot, table, precision=highest).reshape(A, tok, level_count * hg)]
    reshape x6 -> x1, local copies, waits for them, and re-layouts: 13.6 us -> 0.72 us  [per_device(): values.reshape(tok, A, cg).swapaxes(0, 1)]
    ppermute x18, waiting for transfers between devices: 25 us -> 34.7 us  [xor_permute(): return lax.ppermute(value, 'seq', pairs)]
    broadcast_in_dim x12 -> x2, local copies, waits for them, and re-layouts: 7.28 us -> 0.14 us  [widen(): return jnp.repeat(matrix, head_dim, axis=-1)]
    exp x7 -> x0, local copies, waits for them, and re-layouts: 5.18 us -> none  [the longest x4 2.51 us: per_device(): jnp.exp(cum + prefix[:, None, :]) * lw[:, :, 2 + b, :]]
    slice x7 -> x1, local copies, waits for them, and re-layouts: 4.83 us -> 0.08 us  [per_device(): span = cum[:, -1, :]]
  transfers between devices with their start and end apart: 25 -> 25, of which waited for: 10 -> 13; matrix products, arithmetic and copies ran while one was open for 55% -> 16% of each run, Pallas kernels for 0% -> 14%
where the time goes in v2:
time: 199 us; the launch traced here: 198 us
  waiting for transfers between devices  67.9 us (34%)
  starting transfers between devices  40 us (20%)
  other arithmetic  35.7 us (18%)
  Pallas kernels  28.5 us (14%)
  local copies, waits for them, and re-layouts  16.8 us (8%)
  matrix products  8.43 us (4%)
    ppermute x18, waiting for transfers between devices, xor_permute(): return lax.ppermute(value, 'seq', pairs)  34.7 us
    all_to_all x4, waiting for transfers between devices, exchange(): lax.all_to_all(blocks, 'seq', 0, 0, tiled=True, axis_index_groups=groups)  24 us
    another operation x1, other arithmetic, per_device(): cum_own = jnp.cumsum(log_decay, axis=0)  23.3 us
    ppermute x18, starting transfers between devices, xor_permute(): return lax.ppermute(value, 'seq', pairs)  20.5 us
    all_to_all x4, starting transfers between devices, exchange(): lax.all_to_all(blocks, 'seq', 0, 0, tiled=True, axis_index_groups=groups)  17.4 us
    pallas_call x1, Pallas kernels, local_call(): pl.pallas_call(lambda *refs: local_kernel(state_dim, head_dim, bits, *ref...  12.1 us
    pallas_call x1, Pallas kernels, gate_call(): pl.pallas_call(lambda *refs: gate_kernel(levels, *refs), grid=(A,), out_s...  9.56 us
    ppermute x3, waiting for transfers between devices, per_device(): lax.ppermute(w_ring[-1], 'seq', [(s, (s + A) % dev_count) for s in range(...  9.2 us
  transfers between devices with their start and end apart: 25, of which 13 were waited for; matrix products, arithmetic and copies ran while one was open for 16% of the time, Pallas kernels for 14%

profile of v2, /device:TPU:0, one launch (start us, length us, event | category | flops | bytes accessed | tf_op | source)
XLA Modules:
  0.0 198.1 jit_solution(12048970454314969618)
XLA Ops:
  1.1 23.3 %fusion.49 = f32[128,8,10]{2,1,0:T(8,128)S(1)} fusion(f32[128,8,10]{2,1,0:T(8,128)S(1)} %copy.75), kind=kOutput, calls=%fused_computation.129 | output fusion | flops 1300480 | bytes 81920 | tf_op jit(solution)/shard_map/jit(cumsum)/reduce_window_sum | solution.py:255
  26.1 5.2 %all-to-all-start.1 = ((f32[8,128,12]{1,2,0:T(8,128)}), f32[8,128,12]{1,2,0:T(8,128)S(1)}, u32[]{:S(2)}, u32[]{:S(2)}) async-start(f32[8,128,12]{1,2,0:T(8,128)} %copy.76), calls=%async_computation.1 | async-start | bytes 131072 | tf_op jit(solution)/shard_map/all_to_all | solution.py:245
  31.3 1.8 copy.73
  37.1 4.3 %all-to-all-start.3 = ((bf16[8,80,640]{2,1,0:T(8,128)(2,1)}), bf16[8,80,640]{2,1,0:T(8,128)(2,1)}, u32[]{:S(2)}, u32[]{:S(2)}) async-start(bf16[8,80,640]{2,1,0:T(8,128)(2,1)} %bitcast.157), calls=%async_computation.3 | async-start | bytes 1638400 | tf_op jit(solution)/shard_map/all_to_all | solution.py:245
  46.4 1.6 collective-permute-start
  48.1 6.4 %all-to-all-done.3 = bf16[8,80,640]{2,1,0:T(8,128)(2,1)} async-done(((bf16[8,80,640]{2,1,0:T(8,128)(2,1)}), bf16[8,80,640]{2,1,0:T(8,128)(2,1)}, u32[]{:S(2)}, u32[]{:S(2)}) %all-to-all-start.3) | async-done | bytes 819232 | tf_op jit(solution)/shard_map/all_to_all | solution.py:245
  54.5 3.6 %all-to-all-start = ((bf16[8,128,896]{2,1,0:T(8,128)(2,1)}), bf16[8,128,896]{2,1,0:T(8,128)(2,1)S(1)}, u32[]{:S(2)}, u32[]{:S(2)}) async-start(bf16[8,128,896]{2,1,0:T(8,128)(2,1)} %pad_maximum_fusion), calls=%async_computation | async-start | bytes 3670016 | tf_op jit(solution)/shard_map/all_to_all | solution.py:245
  64.2 17.6 %all-to-all-done.refs_0_ = bf16[8,128,896]{2,1,0:T(8,128)(2,1)S(1)} async-done(((bf16[8,128,896]{2,1,0:T(8,128)(2,1)}), bf16[8,128,896]{2,1,0:T(8,128)(2,1)S(1)}, u32[]{:S(2)}, u32[]{:S(2)}) %all-to-all-start) | async-done | bytes 1835040 | tf_op jit(solution)/shard_map/all_to_all | solution.py:245
  83.1 4.3 %all-to-all-start.2 = ((bf16[8,128,640]{2,1,0:T(8,128)(2,1)}), bf16[8,128,640]{2,1,0:T(8,128)(2,1)}, u32[]{:S(2)}, u32[]{:S(2)}) async-start(bf16[8,128,640]{2,1,0:T(8,128)(2,1)} %bitcast.161), calls=%async_computation.2 | async-start | bytes 2621440 | tf_op jit(solution)/shard_map/all_to_all | solution.py:245
  87.4 2.7 %slice_multiply_fusion.1 = (f32[8,128,10]{2,1,0:T(8,128)S(1)}, f32[8,128,10]{2,1,0:T(8,128)S(1)}, f32[8,128,10]{2,1,0:T(8,128)S(1)}, f32[8,128,10]{2,1,0:T(8,128...) fusion(f32[8,128,70]{2,1,0:T(8,128)S(1)} %fusion.26, f32[8,128,10]{2,1,0:T(8,128)} %copy.102.refs_1_, ...), kind=kLoop, calls=%fused_computation.23 | loop fusion | flops 112640 | bytes 493152 | tf_op jit(solution)/shard_map/mul | solution.py:312
  90.1 6.8 %group_states.1 = (bf16[8,128,640]{2,1,0:T(8,128)(2,1)}, bf16[4,128,640]{2,1,0:T(8,128)(2,1)}, bf16[2,128,640]{2,1,0:T(8,128)(2,1)}, bf16[128,640]{1,0:T(8,128)(2,1)}) custom-call(bf16[8,128,896]{2,1,0:T(8,128)(2,1)} %copy-done.1, f32[8,128,10]{2,1,0:T(8,128)} %get-tuple-element.24.refs_1_, f32[7,10]{1,0:T(8,128)} %pad_maximum_fusion.5.refs_2_, ...), custom_call_target="tpu_custom_call" | custom-call | flops 536870912 | bytes 8388608 | tf_op jit(solution)/shard_map/group_states/pallas_call | solution.py:60
  98.5 2.0 %pad_maximum_fusion.3.refs_2_ = f32[8,128,20]{2,1,0:T(8,128)} fusion(f32[8,128,10]{2,1,0:T(8,128)} %get-tuple-element.23, f32[8,128,10]{2,1,0:T(8,128)S(1)} %get-tuple-element.19), kind=kLoop, calls=%fused_computation.29 | loop fusion | flops 20480 | bytes 163840 | tf_op jit(solution)/shard_map/concatenate | solution.py:178
  103.7 2.7 %collective-permute-start.2 = (bf16[128,640]{1,0:T(8,128)(2,1)S(1)}, bf16[128,640]{1,0:T(8,128)(2,1)S(1)}, u32[]{:S(2)}, u32[]{:S(2)}) collective-permute-start(bf16[128,640]{1,0:T(8,128)(2,1)S(1)} %add_convert_fusion), channel_id=1, source_target_pairs={{0,16},{1,17},{2,18},{3,19},{4,20},{5,21},{6,22},{7,23},{8,24},{9,... | collective-permute-start | bytes 491528 | tf_op jit(solution)/shard_map/ppermute | solution.py:18
  106.4 12.1 %local_mix.1.refs_1_ = f32[1024,640]{1,0:T(8,128)} custom-call(bf16[8,128,896]{2,1,0:T(8,128)(2,1)} %copy-done.1, f32[8,128,10]{2,1,0:T(8,128)} %copy.102.refs_1_, f32[8,10,128]{2,1,0:T(8,128)} %get-tuple-element.28.refs_2_, f32[8,128,50]{2,1,0:T(8,128)} %pad_maximum_fusion.2.refs_3_, f32[8,128,1]{2,1,0:T(8,128)} %copy.105.refs_4_, ...), custom_call_target="tpu_custom_call" | custom-call | flops 4294967296 | bytes 12582912 | tf_op jit(solution)/shard_map/local_mix/pallas_call | solution.py:136
  118.5 12.8 %collective-permute-done.2.refs_7_ = bf16[128,640]{1,0:T(8,128)(2,1)S(1)} collective-permute-done((bf16[128,640]{1,0:T(8,128)(2,1)S(1)}, bf16[128,640]{1,0:T(8,128)(2,1)S(1)}, u32[]{:S(2)}, u32[]{:S(2)}) %collective-permute-start.2) | collective-permute-done | bytes 163872 | tf_op jit(solution)/shard_map/ppermute | solution.py:18
  131.9 9.6 %gate_mix.1 = (bf16[1024,640]{1,0:T(8,128)(2,1)}, f32[8,128,1]{2,1,0:T(8,128)}) custom-call(bf16[8,128,896]{2,1,0:T(8,128)(2,1)} %copy-done.1, f32[1024,640]{1,0:T(8,128)} %local_mix.1.refs_1_, f32[8,128,20]{2,1,0:T(8,128)} %pad_maximum_fusion.3.refs_2_, bf16[8,128,640]{2,1,0:T(8,128)(2,1)} %all-to-all-done.2.refs_3_, f32[1,640]{1,0:T(1,128)} %broadcast_in_dim.120.refs_4_, ...), custom_call_target="tpu_custom_call" | custom-call | flops 1073741824 | bytes 8388608 | tf_op jit(solution)/shard_map/gate_mix/pallas_call | solution.py:187
  142.8 2.9 %fusion.51 = f32[1024,640]{1,0:T(8,128)S(1)} fusion(bf16[1024,640]{1,0:T(8,128)(2,1)} %get-tuple-element.15, bf16[640,640]{1,0:T(8,128)(2,1)} %collective-permute-done.9), kind=kOutput, calls=%fused_computation.131 | convolution fusion | flops 838860800 | bytes 4751360 | tf_op jit(solution)/shard_map/dot_general | solution.py:369
  146.4 1.7 collective-permute-start.7
  148.1 2.5 %fusion.50 = f32[2,2,2,128,640]{4,3,2,1,0:T(8,128)S(1)} fusion(bf16[2,2,2,128,640]{4,3,2,1,0:T(8,128)(2,1)S(1)} %bitcast.183, bf16[640,640,1,1,1]{1,0,4,3,2:T(8,128)(2,1)} %bitcast.21), kind=kOutput, calls=%fused_computation.130 | convolution fusion | flops 838860800 | bytes 4751360 | tf_op jit(solution)/shard_map/dot_general | solution.py:369
  152.3 1.9 collective-permute-done.8
  158.8 7.2 %collective-permute-done.11 = bf16[2,128,640]{2,1,0:T(8,128)(2,1)S(1)} collective-permute-done((bf16[2,128,640]{2,1,0:T(8,128)(2,1)S(1)}, bf16[2,128,640]{2,1,0:T(8,128)(2,1)S(1)}, u32[]{:S(2)}, u32[]{:S(2)}) %collective-permute-start.11) | collective-permute-done | bytes 327712 | tf_op jit(solution)/shard_map/ppermute | solution.py:18
  169.0 9.2 %collective-permute-done.17 = bf16[640,640]{1,0:T(8,128)(2,1)S(1)} collective-permute-done((bf16[640,640]{1,0:T(8,128)(2,1)S(1)}, bf16[640,640]{1,0:T(8,128)(2,1)S(1)}, u32[]{:S(2)}, u32[]{:S(2)}) %collective-permute-start.17) | collective-permute-done | bytes 819232 | tf_op jit(solution)/shard_map/ppermute | solution.py:279
  183.5 6.5 %collective-permute-done.15 = bf16[2,128,640]{2,1,0:T(8,128)(2,1)S(1)} collective-permute-done((bf16[2,128,640]{2,1,0:T(8,128)(2,1)S(1)}, bf16[2,128,640]{2,1,0:T(8,128)(2,1)S(1)}, u32[]{:S(2)}, u32[]{:S(2)}) %collective-permute-start.15) | collective-permute-done | bytes 327712 | tf_op jit(solution)/shard_map/ppermute | solution.py:18
  193.0 2.9 %collective-permute-done.16 = bf16[128,640]{1,0:T(8,128)(2,1)S(1)} collective-permute-done((bf16[128,640]{1,0:T(8,128)(2,1)S(1)}, bf16[128,640]{1,0:T(8,128)(2,1)S(1)}, u32[]{:S(2)}, u32[]{:S(2)}) %collective-permute-start.16) | collective-permute-done | bytes 163872 | tf_op jit(solution)/shard_map/ppermute | solution.py:18
  (150 shorter events, 45.7 us)
Async XLA Ops:
  26.1 11.1 %all-to-all-start.1 = ((f32[8,128,12]{1,2,0:T(8,128)}), f32[8,128,12]{1,2,0:T(8,128)S(1)}, u32[]{:S(2)}, u32[]{:S(2)}) async-start(f32[8,128,12]{1,2,0:T(8,128)} %copy.76), calls=%async_computation.1 | async-start | bytes 131072 | tf_op jit(solution)/shard_map/all_to_all | solution.py:245
  37.1 17.4 %all-to-all-start.3 = ((bf16[8,80,640]{2,1,0:T(8,128)(2,1)}), bf16[8,80,640]{2,1,0:T(8,128)(2,1)}, u32[]{:S(2)}, u32[]{:S(2)}) async-start(bf16[8,80,640]{2,1,0:T(8,128)(2,1)} %bitcast.157), calls=%async_computation.3 | async-start | bytes 1638400 | tf_op jit(solution)/shard_map/all_to_all | solution.py:245
  46.4 16.1 %collective-permute-start = (f32[1,10]{1,0:T(1,128)S(1)}, f32[1,10]{1,0:T(1,128)S(1)}, u32[]{:S(2)}, u32[]{:S(2)}) collective-permute-start(f32[1,10]{1,0:T(1,128)S(1)} %get-tuple-element.39), channel_id=1, source_target_pairs={{0,8},{1,9},{2,10},{3,11},{4,12},{5,13},{6,14},{7,15},{8,0},{9,1},... | collective-permute-start | bytes 128 | tf_op jit(solution)/shard_map/ppermute | solution.py:18
  54.5 27.3 %all-to-all-start = ((bf16[8,128,896]{2,1,0:T(8,128)(2,1)}), bf16[8,128,896]{2,1,0:T(8,128)(2,1)S(1)}, u32[]{:S(2)}, u32[]{:S(2)}) async-start(bf16[8,128,896]{2,1,0:T(8,128)(2,1)} %pad_maximum_fusion), calls=%async_computation | async-start | bytes 3670016 | tf_op jit(solution)/shard_map/all_to_all | solution.py:245
  62.5 39.4 %collective-permute-start.9 = (bf16[640,640]{1,0:T(8,128)(2,1)}, bf16[640,640]{1,0:T(8,128)(2,1)}, u32[]{:S(2)}, u32[]{:S(2)}) collective-permute-start(bf16[640,640]{1,0:T(8,128)(2,1)} %bitcast.19), channel_id=1, source_target_pairs={{0,8},{1,9},{2,10},{3,11},{4,12},{5,13},{6,14},{7,15},{8,16},{9,17... | collective-permute-start | bytes 2457608 | tf_op jit(solution)/shard_map/ppermute | solution.py:279
  83.1 35.3 %all-to-all-start.2 = ((bf16[8,128,640]{2,1,0:T(8,128)(2,1)}), bf16[8,128,640]{2,1,0:T(8,128)(2,1)}, u32[]{:S(2)}, u32[]{:S(2)}) async-start(bf16[8,128,640]{2,1,0:T(8,128)(2,1)} %bitcast.161), calls=%async_computation.2 | async-start | bytes 2621440 | tf_op jit(solution)/shard_map/all_to_all | solution.py:245
  96.9 6.7 %collective-permute-start.1 = (bf16[128,640]{1,0:T(8,128)(2,1)}, bf16[128,640]{1,0:T(8,128)(2,1)S(1)}, u32[]{:S(2)}, u32[]{:S(2)}) collective-permute-start(bf16[128,640]{1,0:T(8,128)(2,1)} %get-tuple-element.14), channel_id=1, source_target_pairs={{0,8},{1,9},{2,10},{3,11},{4,12},{5,13},{6,14},{7,15},{8,0},{9,1},... | collective-permute-start | bytes 491528 | tf_op jit(solution)/shard_map/ppermute | solution.py:18
  102.0 52.2 %collective-permute-start.13 = (bf16[640,640]{1,0:T(8,128)(2,1)}, bf16[640,640]{1,0:T(8,128)(2,1)S(1)}, u32[]{:S(2)}, u32[]{:S(2)}) collective-permute-start(bf16[640,640]{1,0:T(8,128)(2,1)} %collective-permute-done.9), channel_id=1, source_target_pairs={{0,8},{1,9},{2,10},{3,11},{4,12},{5,13},{6,14},{7,15},{8,16},{9,17... | collective-permute-start | bytes 2457608 | tf_op jit(solution)/shard_map/ppermute | solution.py:279
  103.7 27.5 %collective-permute-start.2 = (bf16[128,640]{1,0:T(8,128)(2,1)S(1)}, bf16[128,640]{1,0:T(8,128)(2,1)S(1)}, u32[]{:S(2)}, u32[]{:S(2)}) collective-permute-start(bf16[128,640]{1,0:T(8,128)(2,1)S(1)} %add_convert_fusion), channel_id=1, source_target_pairs={{0,16},{1,17},{2,18},{3,19},{4,20},{5,21},{6,22},{7,23},{8,24},{9,... | collective-permute-start | bytes 491528 | tf_op jit(solution)/shard_map/ppermute | solution.py:18
  142.7 3.6 %collective-permute-start.6 = (f32[2,2,128]{2,1,0:T(2,128)S(1)}, f32[2,2,128]{2,1,0:T(2,128)S(1)}, u32[]{:S(2)}, u32[]{:S(2)}) collective-permute-start(f32[2,2,128]{2,1,0:T(2,128)S(1)} %bitcast.181), channel_id=1, source_target_pairs={{0,1},{1,0},{2,3},{3,2},{4,5},{5,4},{6,7},{7,6},{8,9},{9,8},{10,11... | collective-permute-start | bytes 6152 | tf_op jit(solution)/shard_map/ppermute | solution.py:18
  145.8 10.0 %collective-permute-start.10 = (bf16[2,2,128,640]{3,2,1,0:T(8,128)(2,1)S(1)}, bf16[2,2,128,640]{3,2,1,0:T(8,128)(2,1)S(1)}, u32[]{:S(2)}, u32[]{:S(2)}) collective-permute-start(bf16[2,2,128,640]{3,2,1,0:T(8,128)(2,1)S(1)} %fusion.2), channel_id=1, source_target_pairs={{0,1},{1,0},{2,3},{3,2},{4,5},{5,4},{6,7},{7,6},{8,9},{9,8},{10,11... | collective-permute-start | bytes 1966088 | tf_op jit(solution)/shard_map/ppermute | solution.py:18
  146.4 4.2 %collective-permute-start.7 = (f32[2,128]{1,0:T(2,128)S(1)}, f32[2,128]{1,0:T(2,128)S(1)}, u32[]{:S(2)}, u32[]{:S(2)}) collective-permute-start(f32[2,128]{1,0:T(2,128)S(1)} %bitcast.182), channel_id=1, source_target_pairs={{0,2},{1,3},{2,0},{3,1},{4,6},{5,7},{6,4},{7,5},{8,10},{9,11},{10,... | collective-permute-start | bytes 3080 | tf_op jit(solution)/shard_map/ppermute | solution.py:18
  150.6 3.6 %collective-permute-start.8 = (f32[128]{0:T(128)S(1)}, f32[128]{0:T(128)S(1)}, u32[]{:S(2)}, u32[]{:S(2)}) collective-permute-start(f32[128]{0:T(128)S(1)} %fusion.46), channel_id=1, source_target_pairs={{0,4},{1,5},{2,6},{3,7},{4,0},{5,1},{6,2},{7,3},{8,12},{9,13},{10,... | collective-permute-start | bytes 1544 | tf_op jit(solution)/shard_map/ppermute | solution.py:18
  152.2 5.3 %collective-permute-start.3 = (bf16[2,2,128,640]{3,2,1,0:T(8,128)(2,1)S(1)}, bf16[2,2,128,640]{3,2,1,0:T(8,128)(2,1)S(1)}, u32[]{:S(2)}, u32[]{:S(2)}) collective-permute-start(bf16[2,2,128,640]{3,2,1,0:T(8,128)(2,1)S(1)} %fusion), channel_id=1, source_target_pairs={{0,1},{1,0},{2,3},{3,2},{4,5},{5,4},{6,7},{7,6},{8,9},{9,8},{10,11... | collective-permute-start | bytes 1966088 | tf_op jit(solution)/shard_map/ppermute | solution.py:18
  155.6 24.0 %collective-permute-start.14 = (bf16[2,2,128,640]{3,2,0,1:T(8,128)(2,1)S(1)}, bf16[2,2,128,640]{3,2,0,1:T(8,128)(2,1)S(1)}, u32[]{:S(2)}, u32[]{:S(2)}) collective-permute-start(bf16[2,2,128,640]{3,2,0,1:T(8,128)(2,1)S(1)} %fusion.1), channel_id=1, source_target_pairs={{0,1},{1,0},{2,3},{3,2},{4,5},{5,4},{6,7},{7,6},{8,9},{9,8},{10,11... | collective-permute-start | bytes 1966088 | tf_op jit(solution)/shard_map/ppermute | solution.py:18
  155.7 22.4 %collective-permute-start.17 = (bf16[640,640]{1,0:T(8,128)(2,1)S(1)}, bf16[640,640]{1,0:T(8,128)(2,1)S(1)}, u32[]{:S(2)}, u32[]{:S(2)}) collective-permute-start(bf16[640,640]{1,0:T(8,128)(2,1)S(1)} %collective-permute-done.13), channel_id=1, source_target_pairs={{0,8},{1,9},{2,10},{3,11},{4,12},{5,13},{6,14},{7,15},{8,16},{9,17... | collective-permute-start | bytes 2457608 | tf_op jit(solution)/shard_map/ppermute | solution.py:279
  156.0 10.1 %collective-permute-start.11 = (bf16[2,128,640]{2,1,0:T(8,128)(2,1)S(1)}, bf16[2,128,640]{2,1,0:T(8,128)(2,1)S(1)}, u32[]{:S(2)}, u32[]{:S(2)}) collective-permute-start(bf16[2,128,640]{2,1,0:T(8,128)(2,1)S(1)} %fusion.5), channel_id=1, source_target_pairs={{0,4},{1,5},{2,6},{3,7},{4,0},{5,1},{6,2},{7,3},{8,12},{9,13},{10,... | collective-permute-start | bytes 983048 | tf_op jit(solution)/shard_map/ppermute | solution.py:18
  157.7 9.8 %collective-permute-start.4 = (bf16[2,128,640]{2,1,0:T(8,128)(2,1)S(1)}, bf16[2,128,640]{2,1,0:T(8,128)(2,1)S(1)}, u32[]{:S(2)}, u32[]{:S(2)}) collective-permute-start(bf16[2,128,640]{2,1,0:T(8,128)(2,1)S(1)} %fusion.4), channel_id=1, source_target_pairs={{0,2},{1,3},{2,0},{3,1},{4,6},{5,7},{6,4},{7,5},{8,10},{9,11},{10,... | collective-permute-start | bytes 983048 | tf_op jit(solution)/shard_map/ppermute | solution.py:18
  166.2 15.0 %collective-permute-start.12 = (bf16[128,640]{1,0:T(8,128)(2,1)S(1)}, bf16[128,640]{1,0:T(8,128)(2,1)S(1)}, u32[]{:S(2)}, u32[]{:S(2)}) collective-permute-start(bf16[128,640]{1,0:T(8,128)(2,1)S(1)} %fusion.19), channel_id=1, source_target_pairs={{0,2},{1,3},{2,0},{3,1},{4,6},{5,7},{6,4},{7,5},{8,10},{9,11},{10,... | collective-permute-start | bytes 491528 | tf_op jit(solution)/shard_map/ppermute | solution.py:18
  167.6 13.4 %collective-permute-start.5 = (bf16[128,640]{1,0:T(8,128)(2,1)S(1)}, bf16[128,640]{1,0:T(8,128)(2,1)S(1)}, u32[]{:S(2)}, u32[]{:S(2)}) collective-permute-start(bf16[128,640]{1,0:T(8,128)(2,1)S(1)} %fusion.18), channel_id=1, source_target_pairs={{0,4},{1,5},{2,6},{3,7},{4,0},{5,1},{6,2},{7,3},{8,12},{9,13},{10,... | collective-permute-start | bytes 491528 | tf_op jit(solution)/shard_map/ppermute | solution.py:18
  179.9 10.2 %collective-permute-start.15 = (bf16[2,128,640]{2,1,0:T(8,128)(2,1)S(1)}, bf16[2,128,640]{2,1,0:T(8,128)(2,1)S(1)}, u32[]{:S(2)}, u32[]{:S(2)}) collective-permute-start(bf16[2,128,640]{2,1,0:T(8,128)(2,1)S(1)} %fusion.6), channel_id=1, source_target_pairs={{0,2},{1,3},{2,0},{3,1},{4,6},{5,7},{6,4},{7,5},{8,10},{9,11},{10,... | collective-permute-start | bytes 983048 | tf_op jit(solution)/shard_map/ppermute | solution.py:18
  181.9 9.8 %collective-permute-start.19 = (bf16[2,128,640]{2,1,0:T(8,128)(2,1)S(1)}, bf16[2,128,640]{2,1,0:T(8,128)(2,1)S(1)}, u32[]{:S(2)}, u32[]{:S(2)}) collective-permute-start(bf16[2,128,640]{2,1,0:T(8,128)(2,1)S(1)} %fusion.7), channel_id=1, source_target_pairs={{0,4},{1,5},{2,6},{3,7},{4,0},{5,1},{6,2},{7,3},{8,12},{9,13},{10,... | collective-permute-start | bytes 983048 | tf_op jit(solution)/shard_map/ppermute | solution.py:18
  190.1 5.8 %collective-permute-start.16 = (bf16[128,640]{1,0:T(8,128)(2,1)S(1)}, bf16[128,640]{1,0:T(8,128)(2,1)S(1)}, u32[]{:S(2)}, u32[]{:S(2)}) collective-permute-start(bf16[128,640]{1,0:T(8,128)(2,1)S(1)} %fusion.20), channel_id=1, source_target_pairs={{0,4},{1,5},{2,6},{3,7},{4,0},{5,1},{6,2},{7,3},{8,12},{9,13},{10,... | collective-permute-start | bytes 491528 | tf_op jit(solution)/shard_map/ppermute | solution.py:18
  191.8 5.5 %collective-permute-start.20 = (bf16[128,640]{1,0:T(8,128)(2,1)S(1)}, bf16[128,640]{1,0:T(8,128)(2,1)S(1)}, u32[]{:S(2)}, u32[]{:S(2)}) collective-permute-start(bf16[128,640]{1,0:T(8,128)(2,1)S(1)} %fusion.21), channel_id=1, source_target_pairs={{0,2},{1,3},{2,0},{3,1},{4,6},{5,7},{6,4},{7,5},{8,10},{9,11},{10,... | collective-permute-start | bytes 491528 | tf_op jit(solution)/shard_map/ppermute | solution.py:18
  (15 other events, 124.6 us)

commit v3 on v2

--- a/solution.py
+++ b/solution.py
@@ -22,8 +22,50 @@
     return jnp.repeat(matrix, head_dim, axis=-1)
 
 
+def pack_kernel(groups, q_ref, k_ref, x_ref, decay_ref, lam_ref, seg_ref, out_ref):
+    tok, state_dim = q_ref.shape
+    cg = x_ref.shape[1] // groups
+    hg = decay_ref.shape[1] // groups
+    t_pos = lax.broadcasted_iota(jnp.int32, (tok, tok), 0)
+    j_pos = lax.broadcasted_iota(jnp.int32, (tok, tok), 1)
+    ones = jnp.where(t_pos >= j_pos, 1.0, 0.0).astype(f32)
+    cum = jnp.dot(ones, decay_ref[...], precision=highest, preferred_element_type=f32)
+    first = cum.astype(bf16).astype(f32)
+    second = (cum - first).astype(bf16).astype(f32)
+    third = cum - first - second
+    pad = out_ref.shape[2] - 2 * state_dim - cg - 3 * hg - 2
+    tail = [lam_ref[...], seg_ref[...], jnp.zeros((tok, pad), f32)]
+    for s in range(groups):
+        out_ref[s, :, :state_dim] = q_ref[...]
+        out_ref[s, :, state_dim : 2 * state_dim] = k_ref[...]
+        out_ref[s, :, 2 * state_dim : 2 * state_dim + cg] = x_ref[:, s * cg : (s + 1) * cg]
+        parts = [part[:, s * hg : (s + 1) * hg] for part in (first, second, third)]
+        small = jnp.concatenate(parts + tail, axis=1)
+        out_ref[s, :, 2 * state_dim + cg :] = small.astype(bf16)
+
+
+def pack_call(queries, key_rows, values, log_decay, lam, seg, *, groups):
+    tok, state_dim = queries.shape
+    width = 2 * state_dim + values.shape[1] // groups + 3 * (log_decay.shape[1] // groups) + 2
+    vmem = pl.BlockSpec(memory_space=pltpu.VMEM)
+    return pl.pallas_call(
+        lambda *refs: pack_kernel(groups, *refs),
+        out_shape=jax.ShapeDtypeStruct((groups, tok, pl.cdiv(width + 1, 128) * 128), bf16),
+        in_specs=[vmem] * 6,
+        out_specs=vmem,
+        name="pack",
+        cost_estimate=pl.CostEstimate(
+            flops=1 << 22, bytes_accessed=4 << 20, transcendentals=0
+        ),
+    )(queries, key_rows, values, log_decay, lam, seg)
+
+
 def spread(scale, expand):
-    return jnp.dot(scale, expand, precision=highest, preferred_element_type=f32)
+    high = scale.astype(bf16)
+    low = (scale - high.astype(f32)).astype(bf16)
+    return jnp.dot(high, expand, preferred_element_type=f32) + jnp.dot(
+        low, expand, preferred_element_type=f32
+    )
 
 
 def state_kernel(bits, state_dim, packed_ref, scale_ref, up_ref, expand_ref, *outs):
@@ -31,7 +73,7 @@
     expand = expand_ref[...]
     up_wide = spread(up_ref[...], expand)
     for s in range(A):
-        decayed = packed_ref[s, :, 2 * state_dim :].astype(f32) * spread(scale_ref[s], expand)
+        decayed = packed_ref[s, :, 2 * state_dim : 2 * state_dim + expand.shape[1]].astype(f32) * spread(scale_ref[s], expand)
         keys = packed_ref[s, :, state_dim : 2 * state_dim]
         outs[0][s] = lax.dot_general(
             keys,
@@ -53,8 +95,8 @@
 
 
 def state_call(packed, end_scale, up_rows, expand, *, state_dim, bits):
-    A, _, width = packed.shape
-    cg = width - 2 * state_dim
+    A = packed.shape[0]
+    cg = expand.shape[1]
     shapes = [(A >> b, state_dim, cg) for b in range(bits)] + [(state_dim, cg)]
     vmem = pl.BlockSpec(memory_space=pltpu.VMEM)
     return pl.pallas_call(
@@ -89,7 +131,7 @@
     scales = scale_ref[0]
     cum = cum_ref[0]
     cum_t = cum_t_ref[0]
-    x_wide = packed_ref[0, :, 2 * state_dim :]
+    x_wide = packed_ref[0, :, 2 * state_dim : 2 * state_dim + cg]
     acc = skip_ref[...] * x_wide.astype(f32)
     for b in range(bits):
         read = jnp.dot(q, states[b][0], preferred_element_type=f32)
@@ -118,7 +160,7 @@
     packed, cum, cum_t, scales, seg, level_states, skip, expand, *, state_dim, head_dim
 ):
     A, tok, width = packed.shape
-    cg = width - 2 * state_dim
+    cg = expand.shape[1]
     hg = cum.shape[2]
     bits = len(level_states)
 
@@ -252,38 +294,34 @@
     w_blocks = out_proj.T.reshape(out_cols, A, cg).swapaxes(0, 1)
     w_block = exchange(w_blocks).reshape(A * out_cols, cg)
 
-    cum_own = jnp.cumsum(log_decay, axis=0)
-    shared = jnp.concatenate([queries, key_rows], axis=1)
-    packed = jnp.concatenate(
-        [
-            jnp.broadcast_to(shared[None], (A, tok, 2 * state_dim)),
-            values.reshape(tok, A, cg).swapaxes(0, 1),
-        ],
-        axis=2,
-    )
-    small = jnp.concatenate(
-        [
-            cum_own.reshape(tok, A, hg).swapaxes(0, 1),
-            jnp.broadcast_to(lam_index.astype(f32)[None, :, None], (A, tok, 1)),
-            jnp.broadcast_to(segments.astype(f32)[None, :, None], (A, tok, 1)),
-        ],
-        axis=2,
-    )
-    small = exchange(small)
+    packed = pack_call(
+        queries,
+        key_rows,
+        values,
+        log_decay,
+        lam_index.astype(f32)[:, None],
+        segments.astype(f32)[:, None],
+        groups=A,
+    )
     packed = exchange(packed)
-    gates = exchange(gate_rows.reshape(tok, A, cg).swapaxes(0, 1))
-
-    w_ring = [w_block]
-    for _ in range(Z - 1):
-        w_ring.append(
-            lax.ppermute(
-                w_ring[-1], "seq", [(s, (s + A) % dev_count) for s in range(dev_count)]
-            )
-        )
-
-    cum = small[:, :, :hg]
-    lam = small[:, :, hg].reshape(rows).astype(jnp.int32)
-    seg = small[:, :, hg + 1]
+    small = packed[:, :, 2 * state_dim + cg :].astype(f32)
+
+    def shift(block, step):
+        pairs = [(p, (p + step * A) % dev_count) for p in range(dev_count)]
+        return lax.ppermute(block, "seq", pairs)
+
+    w_ring = [(0, w_block)]
+    above = below = w_block
+    if Z > 1:
+        above = shift(w_block, 1)
+        w_ring.append((1, above))
+    if Z > 2:
+        below = shift(w_block, -1)
+        w_ring.append((-1, below))
+
+    cum = small[:, :, :hg] + small[:, :, hg : 2 * hg] + small[:, :, 2 * hg : 3 * hg]
+    lam = small[:, :, 3 * hg].reshape(rows).astype(jnp.int32)
+    seg = small[:, :, 3 * hg + 1]
     span = cum[:, -1, :]
     onehot = (lam[:, None] == jnp.arange(classes, dtype=jnp.int32)[None, :]).astype(f32)
     table = my_heads(lam_table, hg, 2).reshape(classes, level_count * hg)
@@ -291,7 +329,7 @@
     expand = (
         jnp.arange(hg, dtype=jnp.int32)[:, None]
         == jnp.arange(cg, dtype=jnp.int32)[None, :] // head_dim
-    ).astype(f32)
+    ).astype(bf16)
 
     total = span
     prefix = jnp.zeros((A, hg), f32)
@@ -316,6 +354,9 @@
     *level_states, state = state_call(
         packed, end_scale, up_rows, expand, state_dim=state_dim, bits=a_bits
     )
+    gate_blocks = gate_rows.reshape(tok, A, cg).swapaxes(0, 1)
+    gate_blocks, state, total = lax.optimization_barrier((gate_blocks, state, total))
+    gates = exchange(gate_blocks)
     local_scales = [lw[:, :, : 2 * hg]]
     local_scales += [level_scale(before, b) for b, before in enumerate(prefixes)]
     local_scales = jnp.concatenate(local_scales, axis=2)
@@ -336,6 +377,14 @@
             prefix = prefix + jnp.where(is_up, other_total, 0.0)[None, :]
             total = total + other_total
 
+    for distance in range(2, Z // 2 + 1):
+        above, others = lax.optimization_barrier((above, others))
+        above = shift(above, 1)
+        w_ring.append((distance, above))
+        if 2 * distance < Z:
+            below = shift(below, -1)
+            w_ring.append((-distance, below))
+
     skip = widen(my_heads(skip_gain, hg, 0), head_dim)[None, :]
     mixed = local_call(
         packed, cum, cum.swapaxes(1, 2), local_scales, seg, level_states, skip, expand,
@@ -365,14 +414,14 @@
     inv_rms = lax.rsqrt(square_sum / inner_total + epsilon)[:, None]
     block_cols = A * out_cols
     out = jnp.zeros((tok, Z * block_cols), bf16)
-    for step in range(Z):
+    for step, (distance, w_part) in enumerate(w_ring):
         part = lax.dot_general(
-            hidden, w_ring[step], (((1,), (1,)), ((), ())), preferred_element_type=f32
+            hidden, w_part, (((1,), (1,)), ((), ())), preferred_element_type=f32
         )
         part = reduce_group(
             part.reshape(A, tok, block_cols), flipped if step % 2 else bits, bf16
         )
-        block = lax.rem(z_pos - step + Z, Z)
+        block = lax.rem(z_pos - distance + Z, Z)
         out = lax.dynamic_update_slice_in_dim(
             out, (part * inv_rms).astype(bf16), block * block_cols, 1
         )

time: 199 us -> 156 us (0.78)
  waiting for transfers between devices: 67.9 us -> 44.8 us
  other arithmetic: 35.7 us -> 13.1 us
  local copies, waits for them, and re-layouts: 16.8 us -> 21.5 us
  starting transfers between devices: 40 us -> 36.1 us
  matrix products: 8.43 us -> 11.1 us
    another operation x1 -> x0, other arithmetic: 23.3 us -> none  [per_device(): cum_own = jnp.cumsum(log_decay, axis=0)]
    ppermute x18, waiting for transfers between devices: 34.7 us -> 22.9 us  [xor_permute(): return lax.ppermute(value, 'seq', pairs)]
    ppermute x3, waiting for transfers between devices: 9.2 us -> 0.01 us  [shift(): return lax.ppermute(block, 'seq', pairs)]
    all_to_all x4 -> x3, starting transfers between devices: 17.4 us -> 12.6 us  [exchange(): lax.all_to_all(blocks, 'seq', 0, 0, tiled=True, axis_index_groups=groups)]
    slice x0 -> x3, local copies, waits for them, and re-layouts: none -> 3.62 us  [the longest x2 2.03 us: level_scale(): weight = lw[:, :, (2 + level) * hg:(3 + level) * hg]]
    pallas_call x0 -> x1, Pallas kernels: none -> 3.36 us  [pack_call(): pl.pallas_call(lambda *refs: pack_kernel(groups, *refs), out_shape=jax.Sh...]
    dot_general x4, matrix products: 7.99 us -> 10.7 us  [per_device(): lax.dot_general(hidden, w_part, (((1,), (1,)), ((), ())), preferred_eleme...]
    ppermute x3, starting transfers between devices: 2.14 us -> 4.74 us  [shift(): return lax.ppermute(block, 'seq', pairs)]
  transfers between devices with their start and end apart: 25 -> 24, of which waited for: 13 -> 9; matrix products, arithmetic and copies ran while one was open for 16% -> 26% of each run, Pallas kernels for 14% -> 18%
where the time goes in v3:
time: 156 us; the launch traced here: 154 us
  waiting for transfers between devices  44.8 us (29%)
  starting transfers between devices  36.1 us (23%)
  Pallas kernels  27.2 us (17%)
  local copies, waits for them, and re-layouts  21.5 us (14%)
  other arithmetic  13.1 us (8%)
  matrix products  11.1 us (7%)
    ppermute x18, waiting for transfers between devices, xor_permute(): return lax.ppermute(value, 'seq', pairs)  22.9 us
    all_to_all x3, waiting for transfers between devices, exchange(): lax.all_to_all(blocks, 'seq', 0, 0, tiled=True, axis_index_groups=groups)  21.9 us
    ppermute x18, starting transfers between devices, xor_permute(): return lax.ppermute(value, 'seq', pairs)  18.7 us
    all_to_all x3, starting transfers between devices, exchange(): lax.all_to_all(blocks, 'seq', 0, 0, tiled=True, axis_index_groups=groups)  12.6 us
    dot_general x4, matrix products, per_device(): lax.dot_general(hidden, w_part, (((1,), (1,)), ((), ())), preferred_eleme...  10.7 us
    pallas_call x1, Pallas kernels, local_call(): pl.pallas_call(lambda *refs: local_kernel(state_dim, head_dim, bits, *ref...  10.4 us
    pallas_call x1, Pallas kernels, gate_call(): pl.pallas_call(lambda *refs: gate_kernel(levels, *refs), grid=(A,), out_s...  8.03 us
    unnamed x36, local copies, waits for them, and re-layouts  6.21 us
  transfers between devices with their start and end apart: 24, of which 9 were waited for; matrix products, arithmetic and copies ran while one was open for 26% of the time, Pallas kernels for 18%

profile of v3, /device:TPU:0, one launch (start us, length us, event | category | flops | bytes accessed | tf_op | source)
XLA Modules:
  0.0 154.4 jit_solution(10931895419089840559)
XLA Ops:
  0.0 2.1 %copy.115 = bf16[10,8,8,640]{3,2,0,1:T(8,128)(2,1)} copy(bf16[10,8,8,640]{3,2,1,0:T(8,128)(2,1)} %bitcast.162) | data formatting | bytes 1638400 | tf_op jit(solution)/shard_map/reshape | solution.py:294
  2.2 5.3 %all-to-all-start.2 = ((bf16[8,80,640]{2,1,0:T(8,128)(2,1)}), bf16[8,80,640]{2,1,0:T(8,128)(2,1)}, u32[]{:S(2)}, u32[]{:S(2)}) async-start(bf16[8,80,640]{2,1,0:T(8,128)(2,1)} %bitcast.151), calls=%async_computation.2 | async-start | bytes 1638400 | tf_op jit(solution)/shard_map/all_to_all | solution.py:287
  9.7 3.4 %pack.1 = bf16[8,128,1024]{2,1,0:T(8,128)(2,1)} custom-call(bf16[128,128]{1,0:T(8,128)(2,1)} %refs_0_.1, bf16[128,128]{1,0:T(8,128)(2,1)} %refs_1_.1, bf16[128,5120]{1,0:T(8,128)(2,1)} %refs_2_.1, f32[128,80]{1,0:T(8,128)} %copy.77.refs_3_, f32[128,1]{1,0:T(8,128)} %copy.78.refs_4_, f32[128,1]{1,0:T(8,128)} %copy.79.refs_5_), custom_call_target="tpu_custom_call" | custom-call | flops 4194304 | bytes 4194304 | tf_op jit(solution)/shard_map/pack/pallas_call | solution.py:51
  13.1 7.4 %all-to-all-done.2 = bf16[8,80,640]{2,1,0:T(8,128)(2,1)} async-done(((bf16[8,80,640]{2,1,0:T(8,128)(2,1)}), bf16[8,80,640]{2,1,0:T(8,128)(2,1)}, u32[]{:S(2)}, u32[]{:S(2)}) %all-to-all-start.2) | async-done | bytes 819232 | tf_op jit(solution)/shard_map/all_to_all | solution.py:287
  20.5 3.6 %all-to-all-start = ((bf16[8,128,1024]{2,1,0:T(8,128)(2,1)}), bf16[8,128,1024]{2,1,0:T(8,128)(2,1)S(1)}, u32[]{:S(2)}, u32[]{:S(2)}) async-start(bf16[8,128,1024]{2,1,0:T(8,128)(2,1)} %pack.1), calls=%async_computation | async-start | bytes 4194304 | tf_op jit(solution)/shard_map/all_to_all | solution.py:287
  25.3 2.4 %copy.91 = bf16[128,5120]{0,1:T(8,128)(2,1)} copy(bf16[128,5120]{1,0:T(8,128)(2,1)} %param.14) | data formatting | bytes 2621440 | tf_op args[3]
  27.8 2.4 %copy.92 = bf16[128,8,640]{2,0,1:T(8,128)(2,1)} copy(bf16[128,8,640]{0,2,1:T(8,128)(2,1)} %bitcast.155) | data formatting | bytes 2621440 | tf_op jit(solution)/shard_map/reshape | solution.py:357
  32.2 2.0 %collective-permute-start.1 = (bf16[640,640]{1,0:T(8,128)(2,1)}, bf16[640,640]{1,0:T(8,128)(2,1)}, u32[]{:S(2)}, u32[]{:S(2)}) collective-permute-start(bf16[640,640]{1,0:T(8,128)(2,1)} %bitcast.17), channel_id=1, source_target_pairs={{0,8},{1,9},{2,10},{3,11},{4,12},{5,13},{6,14},{7,15},{8,16},{9,17... | collective-permute-start | bytes 2457608 | tf_op jit(solution)/shard_map/ppermute | solution.py:311
  34.2 2.0 %collective-permute-start.13 = (bf16[640,640]{1,0:T(8,128)(2,1)}, bf16[640,640]{1,0:T(8,128)(2,1)}, u32[]{:S(2)}, u32[]{:S(2)}) collective-permute-start(bf16[640,640]{1,0:T(8,128)(2,1)} %bitcast.17), channel_id=1, source_target_pairs={{0,24},{1,25},{2,26},{3,27},{4,28},{5,29},{6,30},{7,31},{8,0},{9,1... | collective-permute-start | bytes 2457608 | tf_op jit(solution)/shard_map/ppermute | solution.py:311
  36.2 14.5 %all-to-all-done.refs_0_ = bf16[8,128,1024]{2,1,0:T(8,128)(2,1)S(1)} async-done(((bf16[8,128,1024]{2,1,0:T(8,128)(2,1)}), bf16[8,128,1024]{2,1,0:T(8,128)(2,1)S(1)}, u32[]{:S(2)}, u32[]{:S(2)}) %all-to-all-start) | async-done | bytes 2097184 | tf_op jit(solution)/shard_map/all_to_all | solution.py:287
  60.5 5.4 %group_states.1 = (bf16[8,128,640]{2,1,0:T(8,128)(2,1)}, bf16[4,128,640]{2,1,0:T(8,128)(2,1)}, bf16[2,128,640]{2,1,0:T(8,128)(2,1)}, bf16[128,640]{1,0:T(8,128)(2,1)}) custom-call(bf16[8,128,1024]{2,1,0:T(8,128)(2,1)} %copy-done.1, f32[8,128,10]{2,1,0:T(8,128)} %get-tuple-element.36.refs_1_, f32[7,10]{1,0:T(8,128)} %pad_maximum_fusion.2.refs_2_, ...), custom_call_target="tpu_custom_call" | custom-call | flops 536870912 | bytes 8388608 | tf_op jit(solution)/shard_map/group_states/pallas_call | solution.py:102
  65.9 2.0 %collective-permute-start = (f32[1,10]{1,0:T(1,128)S(1)}, f32[1,10]{1,0:T(1,128)S(1)}, u32[]{:S(2)}, u32[]{:S(2)}) collective-permute-start(f32[1,10]{1,0:T(1,128)S(1)} %bitcast.172), channel_id=1, source_target_pairs={{0,8},{1,9},{2,10},{3,11},{4,12},{5,13},{6,14},{7,15},{8,0},{9,1},... | collective-permute-start | bytes 128 | tf_op jit(solution)/shard_map/ppermute | solution.py:18
  68.3 3.7 %all-to-all-start.1 = ((bf16[8,128,640]{2,1,0:T(8,128)(2,1)}), bf16[8,128,640]{2,1,0:T(8,128)(2,1)S(1)}, u32[]{:S(2)}, u32[]{:S(2)}) async-start(bf16[8,128,640]{2,1,0:T(8,128)(2,1)} %bitcast.11), calls=%async_computation.1 | async-start | bytes 2621440 | tf_op jit(solution)/shard_map/all_to_all | solution.py:287
  72.7 2.3 %pad_maximum_fusion.refs_3_ = f32[8,128,50]{2,1,0:T(8,128)} fusion(f32[8,128,10]{2,1,0:T(8,128)S(1)} %get-tuple-element.37, f32[8,128,10]{2,1,0:T(8,128)} %get-tuple-element.38, f32[8,128,10]{2,1,0:T(8,128)S(1)} %copy-done.6, f32[8,128,20]{2,1,0:T(8,128)S(1)} %bitcast.153), kind=kLoop, calls=%fused_computation.28 | loop fusion | flops 153600 | bytes 409600 | tf_op jit(solution)/shard_map/concatenate | solution.py:362
  75.0 10.4 %local_mix.1.refs_1_ = f32[1024,640]{1,0:T(8,128)} custom-call(bf16[8,128,1024]{2,1,0:T(8,128)(2,1)} %copy-done.1, f32[8,128,10]{2,1,0:T(8,128)} %copy-done.2, f32[8,10,128]{2,1,0:T(8,128)} %copy.86.refs_2_, f32[8,128,50]{2,1,0:T(8,128)} %pad_maximum_fusion.refs_3_, f32[8,128,1]{2,1,0:T(8,128)} %get-tuple-element.42.refs_4_, f32[8,1,128]{2,1,0:T(1,128)} %bitcast.170, ...), custom_call_target="tpu_custom_call" | custom-call | flops 4294967296 | bytes 12582912 | tf_op jit(solution)/shard_map/local_mix/pallas_call | solution.py:178
  87.0 3.1 %collective-permute-start.3 = (bf16[128,640]{1,0:T(8,128)(2,1)S(1)}, bf16[128,640]{1,0:T(8,128)(2,1)S(1)}, u32[]{:S(2)}, u32[]{:S(2)}) collective-permute-start(bf16[128,640]{1,0:T(8,128)(2,1)S(1)} %add_convert_fusion), channel_id=1, source_target_pairs={{0,16},{1,17},{2,18},{3,19},{4,20},{5,21},{6,22},{7,23},{8,24},{9,... | collective-permute-start | bytes 491528 | tf_op jit(solution)/shard_map/ppermute | solution.py:18
  91.2 6.9 %collective-permute-done.3.refs_7_ = bf16[128,640]{1,0:T(8,128)(2,1)S(1)} collective-permute-done((bf16[128,640]{1,0:T(8,128)(2,1)S(1)}, bf16[128,640]{1,0:T(8,128)(2,1)S(1)}, u32[]{:S(2)}, u32[]{:S(2)}) %collective-permute-start.3) | collective-permute-done | bytes 163872 | tf_op jit(solution)/shard_map/ppermute | solution.py:18
  99.8 8.0 %gate_mix.1 = (bf16[1024,640]{1,0:T(8,128)(2,1)}, f32[8,128,1]{2,1,0:T(8,128)}) custom-call(bf16[8,128,1024]{2,1,0:T(8,128)(2,1)} %copy-done.1, f32[1024,640]{1,0:T(8,128)} %local_mix.1.refs_1_, f32[8,128,20]{2,1,0:T(8,128)} %copy.97.refs_2_, bf16[8,128,640]{2,1,0:T(8,128)(2,1)} %copy-done.5, f32[1,640]{1,0:T(1,128)} %broadcast_in_dim.111.refs_4_, ...), custom_call_target="tpu_custom_call" | custom-call | flops 1073741824 | bytes 8388608 | tf_op jit(solution)/shard_map/gate_mix/pallas_call | solution.py:229
  107.9 2.9 %fusion.49 = f32[2,2,2,128,640]{4,3,2,1,0:T(8,128)S(1)} fusion(bf16[2,2,2,128,640]{4,3,2,1,0:T(8,128)(2,1)} %bitcast.175, bf16[640,640,1,1,1]{1,0,4,3,2:T(8,128)(2,1)} %bitcast.21), kind=kOutput, calls=%fused_computation.132 | convolution fusion | flops 838860800 | bytes 4751360 | tf_op jit(solution)/shard_map/dot_general | solution.py:418
  112.7 2.9 %fusion.50 = f32[1024,640]{1,0:T(8,128)S(1)} fusion(bf16[1024,640]{1,0:T(8,128)(2,1)} %get-tuple-element.26, bf16[640,640]{1,0:T(8,128)(2,1)} %collective-permute-done.1), kind=kOutput, calls=%fused_computation.133 | convolution fusion | flops 838860800 | bytes 4751360 | tf_op jit(solution)/shard_map/dot_general | solution.py:418
  116.9 2.5 %fusion.51 = f32[1024,640]{1,0:T(8,128)S(1)} fusion(bf16[1024,640]{1,0:T(8,128)(2,1)S(1)} %copy-done.13, bf16[640,640]{1,0:T(8,128)(2,1)} %collective-permute-done.13), kind=kOutput, calls=%fused_computation.134 | convolution fusion | flops 838860800 | bytes 4751360 | tf_op jit(solution)/shard_map/dot_general | solution.py:418
  121.3 2.5 %fusion.52 = f32[1024,640]{1,0:T(8,128)S(1)} fusion(bf16[1024,640]{1,0:T(8,128)(2,1)S(1)} %copy-done.13, bf16[640,640]{1,0:T(8,128)(2,1)} %collective-permute-done.17), kind=kOutput, calls=%fused_computation.135 | convolution fusion | flops 838860800 | bytes 4751360 | tf_op jit(solution)/shard_map/dot_general | solution.py:418
  133.6 5.8 %collective-permute-done.5 = bf16[2,128,640]{2,1,0:T(8,128)(2,1)S(1)} collective-permute-done((bf16[2,128,640]{2,1,0:T(8,128)(2,1)S(1)}, bf16[2,128,640]{2,1,0:T(8,128)(2,1)S(1)}, u32[]{:S(2)}, u32[]{:S(2)}) %collective-permute-start.5) | collective-permute-done | bytes 327712 | tf_op jit(solution)/shard_map/ppermute | solution.py:18
  142.3 4.0 %collective-permute-done.15 = bf16[2,128,640]{2,1,0:T(8,128)(2,1)S(1)} collective-permute-done((bf16[2,128,640]{2,1,0:T(8,128)(2,1)S(1)}, bf16[2,128,640]{2,1,0:T(8,128)(2,1)S(1)}, u32[]{:S(2)}, u32[]{:S(2)}) %collective-permute-start.15) | collective-permute-done | bytes 327712 | tf_op jit(solution)/shard_map/ppermute | solution.py:18
  (155 shorter events, 46.3 us)
Async XLA Ops:
  2.2 18.4 %all-to-all-start.2 = ((bf16[8,80,640]{2,1,0:T(8,128)(2,1)}), bf16[8,80,640]{2,1,0:T(8,128)(2,1)}, u32[]{:S(2)}, u32[]{:S(2)}) async-start(bf16[8,80,640]{2,1,0:T(8,128)(2,1)} %bitcast.151), calls=%async_computation.2 | async-start | bytes 1638400 | tf_op jit(solution)/shard_map/all_to_all | solution.py:287
  20.5 30.2 %all-to-all-start = ((bf16[8,128,1024]{2,1,0:T(8,128)(2,1)}), bf16[8,128,1024]{2,1,0:T(8,128)(2,1)S(1)}, u32[]{:S(2)}, u32[]{:S(2)}) async-start(bf16[8,128,1024]{2,1,0:T(8,128)(2,1)} %pack.1), calls=%async_computation | async-start | bytes 4194304 | tf_op jit(solution)/shard_map/all_to_all | solution.py:287
  32.2 59.0 %collective-permute-start.1 = (bf16[640,640]{1,0:T(8,128)(2,1)}, bf16[640,640]{1,0:T(8,128)(2,1)}, u32[]{:S(2)}, u32[]{:S(2)}) collective-permute-start(bf16[640,640]{1,0:T(8,128)(2,1)} %bitcast.17), channel_id=1, source_target_pairs={{0,8},{1,9},{2,10},{3,11},{4,12},{5,13},{6,14},{7,15},{8,16},{9,17... | collective-permute-start | bytes 2457608 | tf_op jit(solution)/shard_map/ppermute | solution.py:311
  34.2 81.6 %collective-permute-start.13 = (bf16[640,640]{1,0:T(8,128)(2,1)}, bf16[640,640]{1,0:T(8,128)(2,1)}, u32[]{:S(2)}, u32[]{:S(2)}) collective-permute-start(bf16[640,640]{1,0:T(8,128)(2,1)} %bitcast.17), channel_id=1, source_target_pairs={{0,24},{1,25},{2,26},{3,27},{4,28},{5,29},{6,30},{7,31},{8,0},{9,1... | collective-permute-start | bytes 2457608 | tf_op jit(solution)/shard_map/ppermute | solution.py:311
  65.9 19.6 %collective-permute-start = (f32[1,10]{1,0:T(1,128)S(1)}, f32[1,10]{1,0:T(1,128)S(1)}, u32[]{:S(2)}, u32[]{:S(2)}) collective-permute-start(f32[1,10]{1,0:T(1,128)S(1)} %bitcast.172), channel_id=1, source_target_pairs={{0,8},{1,9},{2,10},{3,11},{4,12},{5,13},{6,14},{7,15},{8,0},{9,1},... | collective-permute-start | bytes 128 | tf_op jit(solution)/shard_map/ppermute | solution.py:18
  68.3 30.5 %all-to-all-start.1 = ((bf16[8,128,640]{2,1,0:T(8,128)(2,1)}), bf16[8,128,640]{2,1,0:T(8,128)(2,1)S(1)}, u32[]{:S(2)}, u32[]{:S(2)}) async-start(bf16[8,128,640]{2,1,0:T(8,128)(2,1)} %bitcast.11), calls=%async_computation.1 | async-start | bytes 2621440 | tf_op jit(solution)/shard_map/all_to_all | solution.py:287
  72.0 14.0 %collective-permute-start.2 = (bf16[128,640]{1,0:T(8,128)(2,1)}, bf16[128,640]{1,0:T(8,128)(2,1)S(1)}, u32[]{:S(2)}, u32[]{:S(2)}) collective-permute-start(bf16[128,640]{1,0:T(8,128)(2,1)} %get-tuple-element.23), channel_id=1, source_target_pairs={{0,8},{1,9},{2,10},{3,11},{4,12},{5,13},{6,14},{7,15},{8,0},{9,1},... | collective-permute-start | bytes 491528 | tf_op jit(solution)/shard_map/ppermute | solution.py:18
  87.0 11.0 %collective-permute-start.3 = (bf16[128,640]{1,0:T(8,128)(2,1)S(1)}, bf16[128,640]{1,0:T(8,128)(2,1)S(1)}, u32[]{:S(2)}, u32[]{:S(2)}) collective-permute-start(bf16[128,640]{1,0:T(8,128)(2,1)S(1)} %add_convert_fusion), channel_id=1, source_target_pairs={{0,16},{1,17},{2,18},{3,19},{4,20},{5,21},{6,22},{7,23},{8,24},{9,... | collective-permute-start | bytes 491528 | tf_op jit(solution)/shard_map/ppermute | solution.py:18
  98.0 23.3 %collective-permute-start.17 = (bf16[640,640]{1,0:T(8,128)(2,1)}, bf16[640,640]{1,0:T(8,128)(2,1)}, u32[]{:S(2)}, u32[]{:S(2)}) collective-permute-start(bf16[640,640]{1,0:T(8,128)(2,1)} %collective-permute-done.1), channel_id=1, source_target_pairs={{0,8},{1,9},{2,10},{3,11},{4,12},{5,13},{6,14},{7,15},{8,16},{9,17... | collective-permute-start | bytes 2457608 | tf_op jit(solution)/shard_map/ppermute | solution.py:311
  110.8 16.7 %collective-permute-start.4 = (bf16[2,2,128,640]{3,2,1,0:T(8,128)(2,1)S(1)}, bf16[2,2,128,640]{3,2,1,0:T(8,128)(2,1)}, u32[]{:S(2)}, u32[]{:S(2)}) collective-permute-start(bf16[2,2,128,640]{3,2,1,0:T(8,128)(2,1)S(1)} %fusion), channel_id=1, source_target_pairs={{0,1},{1,0},{2,3},{3,2},{4,5},{5,4},{6,7},{7,6},{8,9},{9,8},{10,11... | collective-permute-start | bytes 1966088 | tf_op jit(solution)/shard_map/ppermute | solution.py:18
  112.2 7.4 %collective-permute-start.7 = (f32[2,2,128]{2,1,0:T(2,128)S(1)}, f32[2,2,128]{2,1,0:T(2,128)S(1)}, u32[]{:S(2)}, u32[]{:S(2)}) collective-permute-start(f32[2,2,128]{2,1,0:T(2,128)S(1)} %bitcast.173), channel_id=1, source_target_pairs={{0,1},{1,0},{2,3},{3,2},{4,5},{5,4},{6,7},{7,6},{8,9},{9,8},{10,11... | collective-permute-start | bytes 6152 | tf_op jit(solution)/shard_map/ppermute | solution.py:18
  115.7 14.2 %collective-permute-start.10 = (bf16[2,2,128,640]{3,2,1,0:T(8,128)(2,1)S(1)}, bf16[2,2,128,640]{3,2,1,0:T(8,128)(2,1)S(1)}, u32[]{:S(2)}, u32[]{:S(2)}) collective-permute-start(bf16[2,2,128,640]{3,2,1,0:T(8,128)(2,1)S(1)} %fusion.2), channel_id=1, source_target_pairs={{0,1},{1,0},{2,3},{3,2},{4,5},{5,4},{6,7},{7,6},{8,9},{9,8},{10,11... | collective-permute-start | bytes 1966088 | tf_op jit(solution)/shard_map/ppermute | solution.py:18
  119.5 12.1 %collective-permute-start.14 = (bf16[2,2,128,640]{3,2,0,1:T(8,128)(2,1)S(1)}, bf16[2,2,128,640]{3,2,0,1:T(8,128)(2,1)S(1)}, u32[]{:S(2)}, u32[]{:S(2)}) collective-permute-start(bf16[2,2,128,640]{3,2,0,1:T(8,128)(2,1)S(1)} %fusion.1), channel_id=1, source_target_pairs={{0,1},{1,0},{2,3},{3,2},{4,5},{5,4},{6,7},{7,6},{8,9},{9,8},{10,11... | collective-permute-start | bytes 1966088 | tf_op jit(solution)/shard_map/ppermute | solution.py:18
  119.6 4.2 %collective-permute-start.8 = (f32[2,128]{1,0:T(2,128)S(1)}, f32[2,128]{1,0:T(2,128)S(1)}, u32[]{:S(2)}, u32[]{:S(2)}) collective-permute-start(f32[2,128]{1,0:T(2,128)S(1)} %bitcast.174), channel_id=1, source_target_pairs={{0,2},{1,3},{2,0},{3,1},{4,6},{5,7},{6,4},{7,5},{8,10},{9,11},{10,... | collective-permute-start | bytes 3080 | tf_op jit(solution)/shard_map/ppermute | solution.py:18
  123.9 3.6 %collective-permute-start.9 = (f32[128]{0:T(128)S(1)}, f32[128]{0:T(128)S(1)}, u32[]{:S(2)}, u32[]{:S(2)}) collective-permute-start(f32[128]{0:T(128)S(1)} %fusion.46), channel_id=1, source_target_pairs={{0,4},{1,5},{2,6},{3,7},{4,0},{5,1},{6,2},{7,3},{8,12},{9,13},{10,... | collective-permute-start | bytes 1544 | tf_op jit(solution)/shard_map/ppermute | solution.py:18
  125.5 7.4 %collective-permute-start.18 = (bf16[2,2,128,640]{3,2,1,0:T(8,128)(2,1)S(1)}, bf16[2,2,128,640]{3,2,1,0:T(8,128)(2,1)S(1)}, u32[]{:S(2)}, u32[]{:S(2)}) collective-permute-start(bf16[2,2,128,640]{3,2,1,0:T(8,128)(2,1)S(1)} %fusion.3), channel_id=1, source_target_pairs={{0,1},{1,0},{2,3},{3,2},{4,5},{5,4},{6,7},{7,6},{8,9},{9,8},{10,11... | collective-permute-start | bytes 1966088 | tf_op jit(solution)/shard_map/ppermute | solution.py:18
  128.8 10.6 %collective-permute-start.5 = (bf16[2,128,640]{2,1,0:T(8,128)(2,1)S(1)}, bf16[2,128,640]{2,1,0:T(8,128)(2,1)S(1)}, u32[]{:S(2)}, u32[]{:S(2)}) collective-permute-start(bf16[2,128,640]{2,1,0:T(8,128)(2,1)S(1)} %fusion.5), channel_id=1, source_target_pairs={{0,2},{1,3},{2,0},{3,1},{4,6},{5,7},{6,4},{7,5},{8,10},{9,11},{10,... | collective-permute-start | bytes 983048 | tf_op jit(solution)/shard_map/ppermute | solution.py:18
  130.1 11.0 %collective-permute-start.11 = (bf16[2,128,640]{2,1,0:T(8,128)(2,1)S(1)}, bf16[2,128,640]{2,1,0:T(8,128)(2,1)S(1)}, u32[]{:S(2)}, u32[]{:S(2)}) collective-permute-start(bf16[2,128,640]{2,1,0:T(8,128)(2,1)S(1)} %fusion.6), channel_id=1, source_target_pairs={{0,4},{1,5},{2,6},{3,7},{4,0},{5,1},{6,2},{7,3},{8,12},{9,13},{10,... | collective-permute-start | bytes 983048 | tf_op jit(solution)/shard_map/ppermute | solution.py:18
  131.8 14.5 %collective-permute-start.15 = (bf16[2,128,640]{2,1,0:T(8,128)(2,1)S(1)}, bf16[2,128,640]{2,1,0:T(8,128)(2,1)S(1)}, u32[]{:S(2)}, u32[]{:S(2)}) collective-permute-start(bf16[2,128,640]{2,1,0:T(8,128)(2,1)S(1)} %fusion.7), channel_id=1, source_target_pairs={{0,2},{1,3},{2,0},{3,1},{4,6},{5,7},{6,4},{7,5},{8,10},{9,11},{10,... | collective-permute-start | bytes 983048 | tf_op jit(solution)/shard_map/ppermute | solution.py:18
  133.0 15.1 %collective-permute-start.19 = (bf16[2,128,640]{2,1,0:T(8,128)(2,1)S(1)}, bf16[2,128,640]{2,1,0:T(8,128)(2,1)S(1)}, u32[]{:S(2)}, u32[]{:S(2)}) collective-permute-start(bf16[2,128,640]{2,1,0:T(8,128)(2,1)S(1)} %fusion.8), channel_id=1, source_target_pairs={{0,4},{1,5},{2,6},{3,7},{4,0},{5,1},{6,2},{7,3},{8,12},{9,13},{10,... | collective-permute-start | bytes 983048 | tf_op jit(solution)/shard_map/ppermute | solution.py:18
  139.6 10.8 %collective-permute-start.6 = (bf16[128,640]{1,0:T(8,128)(2,1)S(1)}, bf16[128,640]{1,0:T(8,128)(2,1)S(1)}, u32[]{:S(2)}, u32[]{:S(2)}) collective-permute-start(bf16[128,640]{1,0:T(8,128)(2,1)S(1)} %fusion.19), channel_id=1, source_target_pairs={{0,4},{1,5},{2,6},{3,7},{4,0},{5,1},{6,2},{7,3},{8,12},{9,13},{10,... | collective-permute-start | bytes 491528 | tf_op jit(solution)/shard_map/ppermute | solution.py:18
  141.2 9.3 %collective-permute-start.12 = (bf16[128,640]{1,0:T(8,128)(2,1)S(1)}, bf16[128,640]{1,0:T(8,128)(2,1)S(1)}, u32[]{:S(2)}, u32[]{:S(2)}) collective-permute-start(bf16[128,640]{1,0:T(8,128)(2,1)S(1)} %fusion.20), channel_id=1, source_target_pairs={{0,2},{1,3},{2,0},{3,1},{4,6},{5,7},{6,4},{7,5},{8,10},{9,11},{10,... | collective-permute-start | bytes 491528 | tf_op jit(solution)/shard_map/ppermute | solution.py:18
  146.4 5.7 %collective-permute-start.16 = (bf16[128,640]{1,0:T(8,128)(2,1)S(1)}, bf16[128,640]{1,0:T(8,128)(2,1)S(1)}, u32[]{:S(2)}, u32[]{:S(2)}) collective-permute-start(bf16[128,640]{1,0:T(8,128)(2,1)S(1)} %fusion.21), channel_id=1, source_target_pairs={{0,4},{1,5},{2,6},{3,7},{4,0},{5,1},{6,2},{7,3},{8,12},{9,13},{10,... | collective-permute-start | bytes 491528 | tf_op jit(solution)/shard_map/ppermute | solution.py:18
  148.2 5.4 %collective-permute-start.20 = (bf16[128,640]{1,0:T(8,128)(2,1)S(1)}, bf16[128,640]{1,0:T(8,128)(2,1)S(1)}, u32[]{:S(2)}, u32[]{:S(2)}) collective-permute-start(bf16[128,640]{1,0:T(8,128)(2,1)S(1)} %fusion.22), channel_id=1, source_target_pairs={{0,2},{1,3},{2,0},{3,1},{4,6},{5,7},{6,4},{7,5},{8,10},{9,11},{10,... | collective-permute-start | bytes 491528 | tf_op jit(solution)/shard_map/ppermute | solution.py:18
  (17 other events, 104.5 us)

commit v4 on v3

--- a/solution.py
+++ b/solution.py
@@ -68,12 +68,19 @@
     )
 
 
-def state_kernel(bits, state_dim, packed_ref, scale_ref, up_ref, expand_ref, *outs):
+def state_kernel(bits, state_dim, packed_ref, expand_ref, *outs):
     A = packed_ref.shape[0]
+    hg, cg = expand_ref.shape
     expand = expand_ref[...]
-    up_wide = spread(up_ref[...], expand)
+    totals = []
     for s in range(A):
-        decayed = packed_ref[s, :, 2 * state_dim : 2 * state_dim + expand.shape[1]].astype(f32) * spread(scale_ref[s], expand)
+        tail = packed_ref[s, :, 2 * state_dim + cg :].astype(f32)
+        cum = tail[:, :hg] + tail[:, hg : 2 * hg] + tail[:, 2 * hg : 3 * hg]
+        last = cum[-1:, :]
+        totals.append(last)
+        decayed = packed_ref[s, :, 2 * state_dim : 2 * state_dim + cg].astype(f32) * spread(
+            jnp.exp(last - cum), expand
+        )
         keys = packed_ref[s, :, state_dim : 2 * state_dim]
         outs[0][s] = lax.dot_general(
             keys,
@@ -81,20 +88,23 @@
             (((0,), (0,)), ((), ())),
             preferred_element_type=f32,
         ).astype(bf16)
-    row = 0
     for b in range(bits):
+        up_wide = [
+            spread(jnp.exp(jnp.broadcast_to(totals[2 * g + 1], (8, hg))), expand)[:1]
+            for g in range(A >> (b + 1))
+        ]
         for g in range(A >> (b + 1)):
             low = outs[b][2 * g].astype(f32)
             high = outs[b][2 * g + 1].astype(f32)
-            merged = (high + up_wide[row : row + 1] * low).astype(bf16)
+            merged = (high + up_wide[g] * low).astype(bf16)
             if b + 1 < bits:
                 outs[b + 1][g] = merged
             else:
                 outs[b + 1][...] = merged
-            row += 1
-
-
-def state_call(packed, end_scale, up_rows, expand, *, state_dim, bits):
+        totals = [totals[2 * g] + totals[2 * g + 1] for g in range(A >> (b + 1))]
+
+
+def state_call(packed, expand, *, state_dim, bits):
     A = packed.shape[0]
     cg = expand.shape[1]
     shapes = [(A >> b, state_dim, cg) for b in range(bits)] + [(state_dim, cg)]
@@ -102,13 +112,13 @@
     return pl.pallas_call(
         lambda *refs: state_kernel(bits, state_dim, *refs),
         out_shape=[jax.ShapeDtypeStruct(shape, bf16) for shape in shapes],
-        in_specs=[vmem] * 4,
+        in_specs=[vmem] * 2,
         out_specs=[vmem] * len(shapes),
         name="group_states",
         cost_estimate=pl.CostEstimate(
             flops=1 << 29, bytes_accessed=8 << 20, transcendentals=0
         ),
-    )(packed, end_scale, up_rows, expand)
+    )(packed, expand)
 
 
 def local_kernel(
@@ -304,7 +314,6 @@
         groups=A,
     )
     packed = exchange(packed)
-    small = packed[:, :, 2 * state_dim + cg :].astype(f32)
 
     def shift(block, step):
         pairs = [(p, (p + step * A) % dev_count) for p in range(dev_count)]
@@ -319,6 +328,13 @@
         below = shift(w_block, -1)
         w_ring.append((-1, below))
 
+    expand = (
+        jnp.arange(hg, dtype=jnp.int32)[:, None]
+        == jnp.arange(cg, dtype=jnp.int32)[None, :] // head_dim
+    ).astype(bf16)
+    *level_states, state = state_call(packed, expand, state_dim=state_dim, bits=a_bits)
+    tail, state = lax.optimization_barrier((packed[:, :, 2 * state_dim + cg :], state))
+    small = tail.astype(f32)
     cum = small[:, :, :hg] + small[:, :, hg : 2 * hg] + small[:, :, 2 * hg : 3 * hg]
     lam = small[:, :, 3 * hg].reshape(rows).astype(jnp.int32)
     seg = small[:, :, 3 * hg + 1]
@@ -326,21 +342,14 @@
     onehot = (lam[:, None] == jnp.arange(classes, dtype=jnp.int32)[None, :]).astype(f32)
     table = my_heads(lam_table, hg, 2).reshape(classes, level_count * hg)
     lw = jnp.dot(onehot, table, precision=highest).reshape(A, tok, level_count * hg)
-    expand = (
-        jnp.arange(hg, dtype=jnp.int32)[:, None]
-        == jnp.arange(cg, dtype=jnp.int32)[None, :] // head_dim
-    ).astype(bf16)
-
     total = span
     prefix = jnp.zeros((A, hg), f32)
     prefixes = []
-    up_factors = []
     for b in range(a_bits):
         wide = 2**b
         low_total, up_total = total[0::2], total[1::2]
         is_up = (jnp.arange(A, dtype=jnp.int32) // wide % 2 == 1)[:, None]
         prefixes.append(jnp.where(is_up, prefix, -jnp.inf))
-        up_factors.append(jnp.exp(up_total))
         prefix = prefix + jnp.where(is_up, jnp.repeat(low_total, 2 * wide, axis=0), 0.0)
         total = low_total + up_total
     total = total[0]
@@ -349,11 +358,6 @@
         weight = lw[:, :, (2 + level) * hg : (3 + level) * hg]
         return jnp.exp(cum + before[:, None, :]) * weight
 
-    end_scale = jnp.exp(span[:, None, :] - cum)
-    up_rows = jnp.concatenate(up_factors, axis=0)
-    *level_states, state = state_call(
-        packed, end_scale, up_rows, expand, state_dim=state_dim, bits=a_bits
-    )
     gate_blocks = gate_rows.reshape(tok, A, cg).swapaxes(0, 1)
     gate_blocks, state, total = lax.optimization_barrier((gate_blocks, state, total))
     gates = exchange(gate_blocks)
@@ -362,6 +366,7 @@
     local_scales = jnp.concatenate(local_scales, axis=2)
 
     others, other_scales = [], []
+    local_packed = packed
     for zb in range(z_bits):
         other = xor_permute(state, A << zb)
         other_total = xor_permute(total[None, :], A << zb)[0]
@@ -374,6 +379,7 @@
             low_state = jnp.where(is_up, other, state).astype(f32)
             factor = widen(jnp.exp(jnp.where(is_up, total, other_total)), head_dim)
             state = (up_state + factor[None, :] * low_state).astype(bf16)
+            local_packed, state = lax.optimization_barrier((local_packed, state))
             prefix = prefix + jnp.where(is_up, other_total, 0.0)[None, :]
             total = total + other_total
 
@@ -387,7 +393,7 @@
 
     skip = widen(my_heads(skip_gain, hg, 0), head_dim)[None, :]
     mixed = local_call(
-        packed, cum, cum.swapaxes(1, 2), local_scales, seg, level_states, skip, expand,
+        local_packed, cum, cum.swapaxes(1, 2), local_scales, seg, level_states, skip, expand,
         state_dim=state_dim, head_dim=head_dim,
     )
     gain = my_heads(norm_gain, cg, 0)[None, :]

time: 156 us -> 159 us (1.019)
  local copies, waits for them, and re-layouts: 21.5 us -> 24.9 us
    add x2, local copies, waits for them, and re-layouts: 0.38 us -> 2.53 us  [level_scale(): return jnp.exp(cum + before[:, None, :]) * weight]
    ppermute x18, starting transfers between devices: 18.7 us -> 16.9 us  [xor_permute(): return lax.ppermute(value, 'seq', pairs)]
    add x2, other arithmetic: 1.72 us -> 0.01 us  [per_device(): total = low_total + up_total]
    mul x3 -> x4, other arithmetic: 1.92 us -> 3.32 us  [level_scale(): return jnp.exp(cum + before[:, None, :]) * weight]
    unnamed x36 -> x30, local copies, waits for them, and re-layouts: 6.21 us -> 6.67 us
  transfers between devices with their start and end apart: 24 -> 24, of which waited for: 9 -> 9; matrix products, arithmetic and copies ran while one was open for 26% -> 26% of each run, Pallas kernels for 18% -> 17%
where the time goes in v4:
time: 159 us; the launch traced here: 157 us
  waiting for transfers between devices  46.3 us (29%)
  starting transfers between devices  35.3 us (22%)
  Pallas kernels  27.1 us (17%)
  local copies, waits for them, and re-layouts  24.9 us (16%)
  other arithmetic  11.9 us (7%)
  matrix products  11.1 us (7%)
    ppermute x18, waiting for transfers between devices, xor_permute(): return lax.ppermute(value, 'seq', pairs)  24.4 us
    all_to_all x3, waiting for transfers between devices, exchange(): lax.all_to_all(blocks, 'seq', 0, 0, tiled=True, axis_index_groups=groups)  21.9 us
    ppermute x18, starting transfers between devices, xor_permute(): return lax.ppermute(value, 'seq', pairs)  16.9 us
    all_to_all x3, starting transfers between devices, exchange(): lax.all_to_all(blocks, 'seq', 0, 0, tiled=True, axis_index_groups=groups)  12.5 us
    dot_general x4, matrix products, per_device(): lax.dot_general(hidden, w_part, (((1,), (1,)), ((), ())), preferred_eleme...  10.7 us
    pallas_call x1, Pallas kernels, local_call(): pl.pallas_call(lambda *refs: local_kernel(state_dim, head_dim, bits, *ref...  10.4 us
    pallas_call x1, Pallas kernels, gate_call(): pl.pallas_call(lambda *refs: gate_kernel(levels, *refs), grid=(A,), out_s...  8.04 us
    unnamed x30, local copies, waits for them, and re-layouts  6.67 us
  transfers between devices with their start and end apart: 24, of which 9 were waited for; matrix products, arithmetic and copies ran while one was open for 26% of the time, Pallas kernels for 17%

profile of v4, /device:TPU:0, one launch (start us, length us, event | category | flops | bytes accessed | tf_op | source)
XLA Modules:
  0.0 157.2 jit_solution(2281439335990541250)
XLA Ops:
  0.0 2.2 %copy.115 = bf16[10,8,8,640]{3,2,0,1:T(8,128)(2,1)} copy(bf16[10,8,8,640]{3,2,1,0:T(8,128)(2,1)} %bitcast.162) | data formatting | bytes 1638400 | tf_op jit(solution)/shard_map/reshape | solution.py:304
  2.2 5.3 %all-to-all-start.2 = ((bf16[8,80,640]{2,1,0:T(8,128)(2,1)}), bf16[8,80,640]{2,1,0:T(8,128)(2,1)}, u32[]{:S(2)}, u32[]{:S(2)}) async-start(bf16[8,80,640]{2,1,0:T(8,128)(2,1)} %bitcast.151), calls=%async_computation.2 | async-start | bytes 1638400 | tf_op jit(solution)/shard_map/all_to_all | solution.py:297
  9.7 3.4 %pack.1 = bf16[8,128,1024]{2,1,0:T(8,128)(2,1)} custom-call(bf16[128,128]{1,0:T(8,128)(2,1)} %refs_0_.1, bf16[128,128]{1,0:T(8,128)(2,1)} %refs_1_.1, bf16[128,5120]{1,0:T(8,128)(2,1)} %refs_2_.1, f32[128,80]{1,0:T(8,128)} %copy.77.refs_3_, f32[128,1]{1,0:T(8,128)} %copy.78.refs_4_, f32[128,1]{1,0:T(8,128)} %copy.79.refs_5_), custom_call_target="tpu_custom_call" | custom-call | flops 4194304 | bytes 4194304 | tf_op jit(solution)/shard_map/pack/pallas_call | solution.py:51
  13.1 7.4 %all-to-all-done.2 = bf16[8,80,640]{2,1,0:T(8,128)(2,1)} async-done(((bf16[8,80,640]{2,1,0:T(8,128)(2,1)}), bf16[8,80,640]{2,1,0:T(8,128)(2,1)}, u32[]{:S(2)}, u32[]{:S(2)}) %all-to-all-start.2) | async-done | bytes 819232 | tf_op jit(solution)/shard_map/all_to_all | solution.py:297
  20.5 3.6 %all-to-all-start = ((bf16[8,128,1024]{2,1,0:T(8,128)(2,1)}), bf16[8,128,1024]{2,1,0:T(8,128)(2,1)S(1)}, u32[]{:S(2)}, u32[]{:S(2)}) async-start(bf16[8,128,1024]{2,1,0:T(8,128)(2,1)} %pack.1), calls=%async_computation | async-start | bytes 4194304 | tf_op jit(solution)/shard_map/all_to_all | solution.py:297
  24.2 2.4 %copy.80 = bf16[128,5120]{0,1:T(8,128)(2,1)} copy(bf16[128,5120]{1,0:T(8,128)(2,1)} %param.14) | data formatting | bytes 2621440 | tf_op args[3]
  26.7 2.4 %copy.81 = bf16[128,8,640]{2,0,1:T(8,128)(2,1)} copy(bf16[128,8,640]{0,2,1:T(8,128)(2,1)} %bitcast.154) | data formatting | bytes 2621440 | tf_op jit(solution)/shard_map/reshape | solution.py:361
  32.2 2.0 %collective-permute-start.2 = (bf16[640,640]{1,0:T(8,128)(2,1)}, bf16[640,640]{1,0:T(8,128)(2,1)}, u32[]{:S(2)}, u32[]{:S(2)}) collective-permute-start(bf16[640,640]{1,0:T(8,128)(2,1)} %bitcast.18), channel_id=1, source_target_pairs={{0,8},{1,9},{2,10},{3,11},{4,12},{5,13},{6,14},{7,15},{8,16},{9,17... | collective-permute-start | bytes 2457608 | tf_op jit(solution)/shard_map/ppermute | solution.py:320
  34.2 2.0 %collective-permute-start.13 = (bf16[640,640]{1,0:T(8,128)(2,1)}, bf16[640,640]{1,0:T(8,128)(2,1)}, u32[]{:S(2)}, u32[]{:S(2)}) collective-permute-start(bf16[640,640]{1,0:T(8,128)(2,1)} %bitcast.18), channel_id=1, source_target_pairs={{0,24},{1,25},{2,26},{3,27},{4,28},{5,29},{6,30},{7,31},{8,0},{9,1... | collective-permute-start | bytes 2457608 | tf_op jit(solution)/shard_map/ppermute | solution.py:320
  36.2 14.4 %all-to-all-done.refs_0_ = bf16[8,128,1024]{2,1,0:T(8,128)(2,1)S(1)} async-done(((bf16[8,128,1024]{2,1,0:T(8,128)(2,1)}), bf16[8,128,1024]{2,1,0:T(8,128)(2,1)S(1)}, u32[]{:S(2)}, u32[]{:S(2)}) %all-to-all-start) | async-done | bytes 2097184 | tf_op jit(solution)/shard_map/all_to_all | solution.py:297
  52.0 5.4 %group_states.1 = (bf16[8,128,640]{2,1,0:T(8,128)(2,1)}, bf16[4,128,640]{2,1,0:T(8,128)(2,1)}, bf16[2,128,640]{2,1,0:T(8,128)(2,1)}, bf16[128,640]{1,0:T(8,128)(2,1)}) custom-call(bf16[8,128,1024]{2,1,0:T(8,128)(2,1)} %copy-done.1, bf16[10,640]{1,0:T(8,128)(2,1)} %fusion.30.refs_1_.refs_7_.refs_5_), custom_call_target="tpu_custom_call" | custom-call | flops 536870912 | bytes 8388608 | tf_op jit(solution)/shard_map/group_states/pallas_call | solution.py:112
  60.8 2.1 %collective-permute-start = (bf16[128,640]{1,0:T(8,128)(2,1)S(1)}, bf16[128,640]{1,0:T(8,128)(2,1)S(1)}, u32[]{:S(2)}, u32[]{:S(2)}) collective-permute-start(bf16[128,640]{1,0:T(8,128)(2,1)S(1)} %copy-done.8), channel_id=1, source_target_pairs={{0,8},{1,9},{2,10},{3,11},{4,12},{5,13},{6,14},{7,15},{8,0},{9,1},... | collective-permute-start | bytes 491528 | tf_op jit(solution)/shard_map/ppermute | solution.py:18
  63.8 3.6 %all-to-all-start.1 = ((bf16[8,128,640]{2,1,0:T(8,128)(2,1)}), bf16[8,128,640]{2,1,0:T(8,128)(2,1)S(1)}, u32[]{:S(2)}, u32[]{:S(2)}) async-start(bf16[8,128,640]{2,1,0:T(8,128)(2,1)} %bitcast.3), calls=%async_computation.1 | async-start | bytes 2621440 | tf_op jit(solution)/shard_map/all_to_all | solution.py:297
  67.5 8.3 %collective-permute-done.1 = f32[1,10]{1,0:T(1,128)S(1)} collective-permute-done((f32[1,10]{1,0:T(1,128)S(1)}, f32[1,10]{1,0:T(1,128)S(1)}, u32[]{:S(2)}, u32[]{:S(2)}) %collective-permute-start.1) | collective-permute-done | bytes 72 | tf_op jit(solution)/shard_map/ppermute | solution.py:18
  75.9 2.2 %slice_multiply_fusion.1 = (f32[8,128,10]{2,1,0:T(8,128)}, f32[8,128,10]{2,1,0:T(8,128)}, f32[8,128,10]{2,1,0:T(8,128)}, f32[8,128,10]{2,1,0:T(8,128)}, f32[8,128,10]{2,1,0:T(8,128)}, /*index=5*/f32[8,128,10]{2,1,0:T(8,128)}) fusion(f32[8,128,70]{2,1,0:T(8,128)S(1)} %fusion.27, f32[8,128,10]{2,1,0:T(8,128)S(1)} %get-tuple-element.40.refs_1_, ...), kind=kLoop, calls=%fused_computation.22 | loop fusion | flops 61440 | bytes 451840 | tf_op jit(solution)/shard_map/mul | solution.py:359
  85.7 2.3 %pad_maximum_fusion.refs_3_ = f32[8,128,50]{2,1,0:T(8,128)} fusion(f32[8,128,10]{2,1,0:T(8,128)} %get-tuple-element.42, f32[8,128,10]{2,1,0:T(8,128)S(1)} %copy-done.4, f32[8,128,10]{2,1,0:T(8,128)S(1)} %get-tuple-element.39, f32[8,128,20]{2,1,0:T(8,128)S(1)} %bitcast.153), kind=kLoop, calls=%fused_computation.28 | loop fusion | flops 153600 | bytes 409600 | tf_op jit(solution)/shard_map/concatenate | solution.py:366
  89.3 10.4 %local_mix.1.refs_1_ = f32[1024,640]{1,0:T(8,128)} custom-call(bf16[8,128,1024]{2,1,0:T(8,128)(2,1)} %copy-done.1, f32[8,128,10]{2,1,0:T(8,128)} %copy-done.3, f32[8,10,128]{2,1,0:T(8,128)} %copy.88.refs_2_, f32[8,128,50]{2,1,0:T(8,128)} %pad_maximum_fusion.refs_3_, f32[8,128,1]{2,1,0:T(8,128)} %slice.88.refs_4_, f32[8,1,128]{2,1,0:T(1,128)} %bitcast.169, ...), custom_call_target="tpu_custom_call" | custom-call | flops 4294967296 | bytes 12582912 | tf_op jit(solution)/shard_map/local_mix/pallas_call | solution.py:188
  102.7 8.0 %gate_mix.1 = (bf16[1024,640]{1,0:T(8,128)(2,1)}, f32[8,128,1]{2,1,0:T(8,128)}) custom-call(bf16[8,128,1024]{2,1,0:T(8,128)(2,1)} %copy-done.1, f32[1024,640]{1,0:T(8,128)} %local_mix.1.refs_1_, f32[8,128,20]{2,1,0:T(8,128)} %copy.97.refs_2_, bf16[8,128,640]{2,1,0:T(8,128)(2,1)} %copy-done.2, f32[1,640]{1,0:T(1,128)} %broadcast_in_dim.112.refs_4_, ...), custom_call_target="tpu_custom_call" | custom-call | flops 1073741824 | bytes 8388608 | tf_op jit(solution)/shard_map/gate_mix/pallas_call | solution.py:239
  110.8 2.9 %fusion.47 = f32[2,2,2,128,640]{4,3,2,1,0:T(8,128)S(1)} fusion(bf16[2,2,2,128,640]{4,3,2,1,0:T(8,128)(2,1)} %bitcast.174, bf16[640,640,1,1,1]{1,0,4,3,2:T(8,128)(2,1)} %bitcast.21), kind=kOutput, calls=%fused_computation.126 | convolution fusion | flops 838860800 | bytes 4751360 | tf_op jit(solution)/shard_map/dot_general | solution.py:424
  115.6 2.9 %fusion.48 = f32[1024,640]{1,0:T(8,128)S(1)} fusion(bf16[1024,640]{1,0:T(8,128)(2,1)} %get-tuple-element.34, bf16[640,640]{1,0:T(8,128)(2,1)} %collective-permute-done.2), kind=kOutput, calls=%fused_computation.127 | convolution fusion | flops 838860800 | bytes 4751360 | tf_op jit(solution)/shard_map/dot_general | solution.py:424
  119.8 2.5 %fusion.49 = f32[1024,640]{1,0:T(8,128)S(1)} fusion(bf16[1024,640]{1,0:T(8,128)(2,1)S(1)} %copy-done.10, bf16[640,640]{1,0:T(8,128)(2,1)} %collective-permute-done.13), kind=kOutput, calls=%fused_computation.128 | convolution fusion | flops 838860800 | bytes 4751360 | tf_op jit(solution)/shard_map/dot_general | solution.py:424
  124.2 2.5 %fusion.50 = f32[1024,640]{1,0:T(8,128)S(1)} fusion(bf16[1024,640]{1,0:T(8,128)(2,1)S(1)} %copy-done.10, bf16[640,640]{1,0:T(8,128)(2,1)} %collective-permute-done.17), kind=kOutput, calls=%fused_computation.129 | convolution fusion | flops 838860800 | bytes 4751360 | tf_op jit(solution)/shard_map/dot_general | solution.py:424
  136.5 5.8 %collective-permute-done.5 = bf16[2,128,640]{2,1,0:T(8,128)(2,1)S(1)} collective-permute-done((bf16[2,128,640]{2,1,0:T(8,128)(2,1)S(1)}, bf16[2,128,640]{2,1,0:T(8,128)(2,1)S(1)}, u32[]{:S(2)}, u32[]{:S(2)}) %collective-permute-start.5) | collective-permute-done | bytes 327712 | tf_op jit(solution)/shard_map/ppermute | solution.py:18
  145.2 4.0 %collective-permute-done.15 = bf16[2,128,640]{2,1,0:T(8,128)(2,1)S(1)} collective-permute-done((bf16[2,128,640]{2,1,0:T(8,128)(2,1)S(1)}, bf16[2,128,640]{2,1,0:T(8,128)(2,1)S(1)}, u32[]{:S(2)}, u32[]{:S(2)}) %collective-permute-start.15) | collective-permute-done | bytes 327712 | tf_op jit(solution)/shard_map/ppermute | solution.py:18
  (148 shorter events, 48.7 us)
Async XLA Ops:
  2.2 18.4 %all-to-all-start.2 = ((bf16[8,80,640]{2,1,0:T(8,128)(2,1)}), bf16[8,80,640]{2,1,0:T(8,128)(2,1)}, u32[]{:S(2)}, u32[]{:S(2)}) async-start(bf16[8,80,640]{2,1,0:T(8,128)(2,1)} %bitcast.151), calls=%async_computation.2 | async-start | bytes 1638400 | tf_op jit(solution)/shard_map/all_to_all | solution.py:297
  20.5 30.2 %all-to-all-start = ((bf16[8,128,1024]{2,1,0:T(8,128)(2,1)}), bf16[8,128,1024]{2,1,0:T(8,128)(2,1)S(1)}, u32[]{:S(2)}, u32[]{:S(2)}) async-start(bf16[8,128,1024]{2,1,0:T(8,128)(2,1)} %pack.1), calls=%async_computation | async-start | bytes 4194304 | tf_op jit(solution)/shard_map/all_to_all | solution.py:297
  32.2 67.5 %collective-permute-start.2 = (bf16[640,640]{1,0:T(8,128)(2,1)}, bf16[640,640]{1,0:T(8,128)(2,1)}, u32[]{:S(2)}, u32[]{:S(2)}) collective-permute-start(bf16[640,640]{1,0:T(8,128)(2,1)} %bitcast.18), channel_id=1, source_target_pairs={{0,8},{1,9},{2,10},{3,11},{4,12},{5,13},{6,14},{7,15},{8,16},{9,17... | collective-permute-start | bytes 2457608 | tf_op jit(solution)/shard_map/ppermute | solution.py:320
  34.2 84.5 %collective-permute-start.13 = (bf16[640,640]{1,0:T(8,128)(2,1)}, bf16[640,640]{1,0:T(8,128)(2,1)}, u32[]{:S(2)}, u32[]{:S(2)}) collective-permute-start(bf16[640,640]{1,0:T(8,128)(2,1)} %bitcast.18), channel_id=1, source_target_pairs={{0,24},{1,25},{2,26},{3,27},{4,28},{5,29},{6,30},{7,31},{8,0},{9,1... | collective-permute-start | bytes 2457608 | tf_op jit(solution)/shard_map/ppermute | solution.py:320
  60.8 27.2 %collective-permute-start = (bf16[128,640]{1,0:T(8,128)(2,1)S(1)}, bf16[128,640]{1,0:T(8,128)(2,1)S(1)}, u32[]{:S(2)}, u32[]{:S(2)}) collective-permute-start(bf16[128,640]{1,0:T(8,128)(2,1)S(1)} %copy-done.8), channel_id=1, source_target_pairs={{0,8},{1,9},{2,10},{3,11},{4,12},{5,13},{6,14},{7,15},{8,0},{9,1},... | collective-permute-start | bytes 491528 | tf_op jit(solution)/shard_map/ppermute | solution.py:18
  62.9 12.9 %collective-permute-start.1 = (f32[1,10]{1,0:T(1,128)S(1)}, f32[1,10]{1,0:T(1,128)S(1)}, u32[]{:S(2)}, u32[]{:S(2)}) collective-permute-start(f32[1,10]{1,0:T(1,128)S(1)} %bitcast.172), channel_id=1, source_target_pairs={{0,8},{1,9},{2,10},{3,11},{4,12},{5,13},{6,14},{7,15},{8,0},{9,1},... | collective-permute-start | bytes 128 | tf_op jit(solution)/shard_map/ppermute | solution.py:18
  63.8 37.8 %all-to-all-start.1 = ((bf16[8,128,640]{2,1,0:T(8,128)(2,1)}), bf16[8,128,640]{2,1,0:T(8,128)(2,1)S(1)}, u32[]{:S(2)}, u32[]{:S(2)}) async-start(bf16[8,128,640]{2,1,0:T(8,128)(2,1)} %bitcast.3), calls=%async_computation.1 | async-start | bytes 2621440 | tf_op jit(solution)/shard_map/all_to_all | solution.py:297
  88.1 11.6 %collective-permute-start.3 = (bf16[128,640]{1,0:T(8,128)(2,1)S(1)}, bf16[128,640]{1,0:T(8,128)(2,1)S(1)}, u32[]{:S(2)}, u32[]{:S(2)}) collective-permute-start(bf16[128,640]{1,0:T(8,128)(2,1)S(1)} %add_convert_fusion), channel_id=1, source_target_pairs={{0,16},{1,17},{2,18},{3,19},{4,20},{5,21},{6,22},{7,23},{8,24},{9,... | collective-permute-start | bytes 491528 | tf_op jit(solution)/shard_map/ppermute | solution.py:18
  99.7 24.5 %collective-permute-start.17 = (bf16[640,640]{1,0:T(8,128)(2,1)}, bf16[640,640]{1,0:T(8,128)(2,1)}, u32[]{:S(2)}, u32[]{:S(2)}) collective-permute-start(bf16[640,640]{1,0:T(8,128)(2,1)} %collective-permute-done.2), channel_id=1, source_target_pairs={{0,8},{1,9},{2,10},{3,11},{4,12},{5,13},{6,14},{7,15},{8,16},{9,17... | collective-permute-start | bytes 2457608 | tf_op jit(solution)/shard_map/ppermute | solution.py:320
  113.7 16.7 %collective-permute-start.4 = (bf16[2,2,128,640]{3,2,1,0:T(8,128)(2,1)S(1)}, bf16[2,2,128,640]{3,2,1,0:T(8,128)(2,1)}, u32[]{:S(2)}, u32[]{:S(2)}) collective-permute-start(bf16[2,2,128,640]{3,2,1,0:T(8,128)(2,1)S(1)} %fusion), channel_id=1, source_target_pairs={{0,1},{1,0},{2,3},{3,2},{4,5},{5,4},{6,7},{7,6},{8,9},{9,8},{10,11... | collective-permute-start | bytes 1966088 | tf_op jit(solution)/shard_map/ppermute | solution.py:18
  115.1 7.4 %collective-permute-start.7 = (f32[2,2,128]{2,1,0:T(2,128)S(1)}, f32[2,2,128]{2,1,0:T(2,128)S(1)}, u32[]{:S(2)}, u32[]{:S(2)}) collective-permute-start(f32[2,2,128]{2,1,0:T(2,128)S(1)} %bitcast.171), channel_id=1, source_target_pairs={{0,1},{1,0},{2,3},{3,2},{4,5},{5,4},{6,7},{7,6},{8,9},{9,8},{10,11... | collective-permute-start | bytes 6152 | tf_op jit(solution)/shard_map/ppermute | solution.py:18
  118.6 14.2 %collective-permute-start.10 = (bf16[2,2,128,640]{3,2,1,0:T(8,128)(2,1)S(1)}, bf16[2,2,128,640]{3,2,1,0:T(8,128)(2,1)S(1)}, u32[]{:S(2)}, u32[]{:S(2)}) collective-permute-start(bf16[2,2,128,640]{3,2,1,0:T(8,128)(2,1)S(1)} %fusion.2), channel_id=1, source_target_pairs={{0,1},{1,0},{2,3},{3,2},{4,5},{5,4},{6,7},{7,6},{8,9},{9,8},{10,11... | collective-permute-start | bytes 1966088 | tf_op jit(solution)/shard_map/ppermute | solution.py:18
  122.4 12.1 %collective-permute-start.14 = (bf16[2,2,128,640]{3,2,0,1:T(8,128)(2,1)S(1)}, bf16[2,2,128,640]{3,2,0,1:T(8,128)(2,1)S(1)}, u32[]{:S(2)}, u32[]{:S(2)}) collective-permute-start(bf16[2,2,128,640]{3,2,0,1:T(8,128)(2,1)S(1)} %fusion.1), channel_id=1, source_target_pairs={{0,1},{1,0},{2,3},{3,2},{4,5},{5,4},{6,7},{7,6},{8,9},{9,8},{10,11... | collective-permute-start | bytes 1966088 | tf_op jit(solution)/shard_map/ppermute | solution.py:18
  122.5 4.2 %collective-permute-start.8 = (f32[2,128]{1,0:T(2,128)S(1)}, f32[2,128]{1,0:T(2,128)S(1)}, u32[]{:S(2)}, u32[]{:S(2)}) collective-permute-start(f32[2,128]{1,0:T(2,128)S(1)} %bitcast.173), channel_id=1, source_target_pairs={{0,2},{1,3},{2,0},{3,1},{4,6},{5,7},{6,4},{7,5},{8,10},{9,11},{10,... | collective-permute-start | bytes 3080 | tf_op jit(solution)/shard_map/ppermute | solution.py:18
  126.8 3.6 %collective-permute-start.9 = (f32[128]{0:T(128)S(1)}, f32[128]{0:T(128)S(1)}, u32[]{:S(2)}, u32[]{:S(2)}) collective-permute-start(f32[128]{0:T(128)S(1)} %fusion.46), channel_id=1, source_target_pairs={{0,4},{1,5},{2,6},{3,7},{4,0},{5,1},{6,2},{7,3},{8,12},{9,13},{10,... | collective-permute-start | bytes 1544 | tf_op jit(solution)/shard_map/ppermute | solution.py:18
  128.4 7.4 %collective-permute-start.18 = (bf16[2,2,128,640]{3,2,1,0:T(8,128)(2,1)S(1)}, bf16[2,2,128,640]{3,2,1,0:T(8,128)(2,1)S(1)}, u32[]{:S(2)}, u32[]{:S(2)}) collective-permute-start(bf16[2,2,128,640]{3,2,1,0:T(8,128)(2,1)S(1)} %fusion.3), channel_id=1, source_target_pairs={{0,1},{1,0},{2,3},{3,2},{4,5},{5,4},{6,7},{7,6},{8,9},{9,8},{10,11... | collective-permute-start | bytes 1966088 | tf_op jit(solution)/shard_map/ppermute | solution.py:18
  131.7 10.6 %collective-permute-start.5 = (bf16[2,128,640]{2,1,0:T(8,128)(2,1)S(1)}, bf16[2,128,640]{2,1,0:T(8,128)(2,1)S(1)}, u32[]{:S(2)}, u32[]{:S(2)}) collective-permute-start(bf16[2,128,640]{2,1,0:T(8,128)(2,1)S(1)} %fusion.5), channel_id=1, source_target_pairs={{0,2},{1,3},{2,0},{3,1},{4,6},{5,7},{6,4},{7,5},{8,10},{9,11},{10,... | collective-permute-start | bytes 983048 | tf_op jit(solution)/shard_map/ppermute | solution.py:18
  133.0 11.0 %collective-permute-start.11 = (bf16[2,128,640]{2,1,0:T(8,128)(2,1)S(1)}, bf16[2,128,640]{2,1,0:T(8,128)(2,1)S(1)}, u32[]{:S(2)}, u32[]{:S(2)}) collective-permute-start(bf16[2,128,640]{2,1,0:T(8,128)(2,1)S(1)} %fusion.6), channel_id=1, source_target_pairs={{0,4},{1,5},{2,6},{3,7},{4,0},{5,1},{6,2},{7,3},{8,12},{9,13},{10,... | collective-permute-start | bytes 983048 | tf_op jit(solution)/shard_map/ppermute | solution.py:18
  134.7 14.5 %collective-permute-start.15 = (bf16[2,128,640]{2,1,0:T(8,128)(2,1)S(1)}, bf16[2,128,640]{2,1,0:T(8,128)(2,1)S(1)}, u32[]{:S(2)}, u32[]{:S(2)}) collective-permute-start(bf16[2,128,640]{2,1,0:T(8,128)(2,1)S(1)} %fusion.7), channel_id=1, source_target_pairs={{0,2},{1,3},{2,0},{3,1},{4,6},{5,7},{6,4},{7,5},{8,10},{9,11},{10,... | collective-permute-start | bytes 983048 | tf_op jit(solution)/shard_map/ppermute | solution.py:18
  135.9 15.1 %collective-permute-start.19 = (bf16[2,128,640]{2,1,0:T(8,128)(2,1)S(1)}, bf16[2,128,640]{2,1,0:T(8,128)(2,1)S(1)}, u32[]{:S(2)}, u32[]{:S(2)}) collective-permute-start(bf16[2,128,640]{2,1,0:T(8,128)(2,1)S(1)} %fusion.8), channel_id=1, source_target_pairs={{0,4},{1,5},{2,6},{3,7},{4,0},{5,1},{6,2},{7,3},{8,12},{9,13},{10,... | collective-permute-start | bytes 983048 | tf_op jit(solution)/shard_map/ppermute | solution.py:18
  142.4 10.8 %collective-permute-start.6 = (bf16[128,640]{1,0:T(8,128)(2,1)S(1)}, bf16[128,640]{1,0:T(8,128)(2,1)S(1)}, u32[]{:S(2)}, u32[]{:S(2)}) collective-permute-start(bf16[128,640]{1,0:T(8,128)(2,1)S(1)} %fusion.19), channel_id=1, source_target_pairs={{0,4},{1,5},{2,6},{3,7},{4,0},{5,1},{6,2},{7,3},{8,12},{9,13},{10,... | collective-permute-start | bytes 491528 | tf_op jit(solution)/shard_map/ppermute | solution.py:18
  144.1 9.3 %collective-permute-start.12 = (bf16[128,640]{1,0:T(8,128)(2,1)S(1)}, bf16[128,640]{1,0:T(8,128)(2,1)S(1)}, u32[]{:S(2)}, u32[]{:S(2)}) collective-permute-start(bf16[128,640]{1,0:T(8,128)(2,1)S(1)} %fusion.20), channel_id=1, source_target_pairs={{0,2},{1,3},{2,0},{3,1},{4,6},{5,7},{6,4},{7,5},{8,10},{9,11},{10,... | collective-permute-start | bytes 491528 | tf_op jit(solution)/shard_map/ppermute | solution.py:18
  149.3 5.7 %collective-permute-start.16 = (bf16[128,640]{1,0:T(8,128)(2,1)S(1)}, bf16[128,640]{1,0:T(8,128)(2,1)S(1)}, u32[]{:S(2)}, u32[]{:S(2)}) collective-permute-start(bf16[128,640]{1,0:T(8,128)(2,1)S(1)} %fusion.21), channel_id=1, source_target_pairs={{0,4},{1,5},{2,6},{3,7},{4,0},{5,1},{6,2},{7,3},{8,12},{9,13},{10,... | collective-permute-start | bytes 491528 | tf_op jit(solution)/shard_map/ppermute | solution.py:18
  151.1 5.4 %collective-permute-start.20 = (bf16[128,640]{1,0:T(8,128)(2,1)S(1)}, bf16[128,640]{1,0:T(8,128)(2,1)S(1)}, u32[]{:S(2)}, u32[]{:S(2)}) collective-permute-start(bf16[128,640]{1,0:T(8,128)(2,1)S(1)} %fusion.22), channel_id=1, source_target_pairs={{0,2},{1,3},{2,0},{3,1},{4,6},{5,7},{6,4},{7,5},{8,10},{9,11},{10,... | collective-permute-start | bytes 491528 | tf_op jit(solution)/shard_map/ppermute | solution.py:18
  (14 other events, 98.7 us)

commit v5 on v3

--- a/solution.py
+++ b/solution.py
@@ -362,6 +362,7 @@
     local_scales = jnp.concatenate(local_scales, axis=2)
 
     others, other_scales = [], []
+    local_packed = packed
     for zb in range(z_bits):
         other = xor_permute(state, A << zb)
         other_total = xor_permute(total[None, :], A << zb)[0]
@@ -374,6 +375,7 @@
             low_state = jnp.where(is_up, other, state).astype(f32)
             factor = widen(jnp.exp(jnp.where(is_up, total, other_total)), head_dim)
             state = (up_state + factor[None, :] * low_state).astype(bf16)
+            local_packed, state = lax.optimization_barrier((local_packed, state))
             prefix = prefix + jnp.where(is_up, other_total, 0.0)[None, :]
             total = total + other_total
 
@@ -387,7 +389,7 @@
 
     skip = widen(my_heads(skip_gain, hg, 0), head_dim)[None, :]
     mixed = local_call(
-        packed, cum, cum.swapaxes(1, 2), local_scales, seg, level_states, skip, expand,
+        local_packed, cum, cum.swapaxes(1, 2), local_scales, seg, level_states, skip, expand,
         state_dim=state_dim, head_dim=head_dim,
     )
     gain = my_heads(norm_gain, cg, 0)[None, :]

time: 156 us -> 165 us (1.058)
  waiting for transfers between devices: 44.8 us -> 51.4 us
  local copies, waits for them, and re-layouts: 21.5 us -> 27.1 us
  starting transfers between devices: 36.1 us -> 30.6 us
  other arithmetic: 13.1 us -> 15.7 us
    ppermute x18, waiting for transfers between devices: 22.9 us -> 29.4 us  [xor_permute(): return lax.ppermute(value, 'seq', pairs)]
    ppermute x18, starting transfers between devices: 18.7 us -> 14.2 us  [xor_permute(): return lax.ppermute(value, 'seq', pairs)]
    add x2, local copies, waits for them, and re-layouts: 0.38 us -> 3.12 us  [level_scale(): return jnp.exp(cum + before[:, None, :]) * weight]
    mul x3 -> x4, other arithmetic: 1.92 us -> 4.2 us  [level_scale(): return jnp.exp(cum + before[:, None, :]) * weight]
    exp x0 -> x1, other arithmetic: none -> 1.95 us  [per_device(): end_scale = jnp.exp(span[:, None, :] - cum)]
    add x2 -> x0, other arithmetic: 1.72 us -> none  [level_scale(): return jnp.exp(cum + before[:, None, :]) * weight]
    unnamed x36 -> x38, local copies, waits for them, and re-layouts: 6.21 us -> 7.23 us
  transfers between devices with their start and end apart: 24 -> 24, of which waited for: 9 -> 10; matrix products, arithmetic and copies ran while one was open for 26% -> 29% of each run, Pallas kernels for 18% -> 17%
where the time goes in v5:
time: 165 us; the launch traced here: 164 us
  waiting for transfers between devices  51.4 us (31%)
  starting transfers between devices  30.6 us (19%)
  Pallas kernels  27.2 us (16%)
  local copies, waits for them, and re-layouts  27.1 us (16%)
  other arithmetic  15.7 us (10%)
  matrix products  11.3 us (7%)
    ppermute x18, waiting for transfers between devices, xor_permute(): return lax.ppermute(value, 'seq', pairs)  29.4 us
    all_to_all x3, waiting for transfers between devices, exchange(): lax.all_to_all(blocks, 'seq', 0, 0, tiled=True, axis_index_groups=groups)  21.9 us
    ppermute x18, starting transfers between devices, xor_permute(): return lax.ppermute(value, 'seq', pairs)  14.2 us
    all_to_all x3, starting transfers between devices, exchange(): lax.all_to_all(blocks, 'seq', 0, 0, tiled=True, axis_index_groups=groups)  12.4 us
    dot_general x4, matrix products, per_device(): lax.dot_general(hidden, w_part, (((1,), (1,)), ((), ())), preferred_eleme...  10.9 us
    pallas_call x1, Pallas kernels, local_call(): pl.pallas_call(lambda *refs: local_kernel(state_dim, head_dim, bits, *ref...  10.4 us
    pallas_call x1, Pallas kernels, gate_call(): pl.pallas_call(lambda *refs: gate_kernel(levels, *refs), grid=(A,), out_s...  8.03 us
    unnamed x38, local copies, waits for them, and re-layouts  7.23 us
  transfers between devices with their start and end apart: 24, of which 10 were waited for; matrix products, arithmetic and copies ran while one was open for 29% of the time, Pallas kernels for 17%

profile of v5, /device:TPU:0, one launch (start us, length us, event | category | flops | bytes accessed | tf_op | source)
XLA Modules:
  0.0 163.9 jit_solution(7852758551075470828)
XLA Ops:
  0.0 2.2 %copy.115 = bf16[10,8,8,640]{3,2,0,1:T(8,128)(2,1)} copy(bf16[10,8,8,640]{3,2,1,0:T(8,128)(2,1)} %bitcast.162) | data formatting | bytes 1638400 | tf_op jit(solution)/shard_map/reshape | solution.py:294
  2.2 5.2 %all-to-all-start.2 = ((bf16[8,80,640]{2,1,0:T(8,128)(2,1)}), bf16[8,80,640]{2,1,0:T(8,128)(2,1)}, u32[]{:S(2)}, u32[]{:S(2)}) async-start(bf16[8,80,640]{2,1,0:T(8,128)(2,1)} %bitcast.151), calls=%async_computation.2 | async-start | bytes 1638400 | tf_op jit(solution)/shard_map/all_to_all | solution.py:287
  9.6 3.3 %pack.1 = bf16[8,128,1024]{2,1,0:T(8,128)(2,1)} custom-call(bf16[128,128]{1,0:T(8,128)(2,1)} %refs_0_.1, bf16[128,128]{1,0:T(8,128)(2,1)} %refs_1_.1, bf16[128,5120]{1,0:T(8,128)(2,1)} %refs_2_.1, f32[128,80]{1,0:T(8,128)} %copy.77.refs_3_, f32[128,1]{1,0:T(8,128)} %copy.78.refs_4_, f32[128,1]{1,0:T(8,128)} %copy.79.refs_5_), custom_call_target="tpu_custom_call" | custom-call | flops 4194304 | bytes 4194304 | tf_op jit(solution)/shard_map/pack/pallas_call | solution.py:51
  12.9 7.5 %all-to-all-done.2 = bf16[8,80,640]{2,1,0:T(8,128)(2,1)} async-done(((bf16[8,80,640]{2,1,0:T(8,128)(2,1)}), bf16[8,80,640]{2,1,0:T(8,128)(2,1)}, u32[]{:S(2)}, u32[]{:S(2)}) %all-to-all-start.2) | async-done | bytes 819232 | tf_op jit(solution)/shard_map/all_to_all | solution.py:287
  20.4 3.6 %all-to-all-start = ((bf16[8,128,1024]{2,1,0:T(8,128)(2,1)}), bf16[8,128,1024]{2,1,0:T(8,128)(2,1)S(1)}, u32[]{:S(2)}, u32[]{:S(2)}) async-start(bf16[8,128,1024]{2,1,0:T(8,128)(2,1)} %pack.1), calls=%async_computation | async-start | bytes 4194304 | tf_op jit(solution)/shard_map/all_to_all | solution.py:287
  24.4 2.4 %copy.80 = bf16[128,5120]{0,1:T(8,128)(2,1)} copy(bf16[128,5120]{1,0:T(8,128)(2,1)} %param.14) | data formatting | bytes 2621440 | tf_op args[3]
  26.8 2.5 %copy.81 = bf16[128,8,640]{2,0,1:T(8,128)(2,1)} copy(bf16[128,8,640]{0,2,1:T(8,128)(2,1)} %bitcast.155) | data formatting | bytes 2621440 | tf_op jit(solution)/shard_map/reshape | solution.py:357
  34.1 2.0 %collective-permute-start.13 = (bf16[640,640]{1,0:T(8,128)(2,1)}, bf16[640,640]{1,0:T(8,128)(2,1)}, u32[]{:S(2)}, u32[]{:S(2)}) collective-permute-start(bf16[640,640]{1,0:T(8,128)(2,1)} %bitcast.18), channel_id=1, source_target_pairs={{0,24},{1,25},{2,26},{3,27},{4,28},{5,29},{6,30},{7,31},{8,0},{9,1... | collective-permute-start | bytes 2457608 | tf_op jit(solution)/shard_map/ppermute | solution.py:311
  36.1 14.5 %all-to-all-done.refs_0_ = bf16[8,128,1024]{2,1,0:T(8,128)(2,1)S(1)} async-done(((bf16[8,128,1024]{2,1,0:T(8,128)(2,1)}), bf16[8,128,1024]{2,1,0:T(8,128)(2,1)S(1)}, u32[]{:S(2)}, u32[]{:S(2)}) %all-to-all-start) | async-done | bytes 2097184 | tf_op jit(solution)/shard_map/all_to_all | solution.py:287
  57.8 5.4 %group_states.1 = (bf16[8,128,640]{2,1,0:T(8,128)(2,1)}, bf16[4,128,640]{2,1,0:T(8,128)(2,1)}, bf16[2,128,640]{2,1,0:T(8,128)(2,1)}, bf16[128,640]{1,0:T(8,128)(2,1)}) custom-call(bf16[8,128,1024]{2,1,0:T(8,128)(2,1)} %copy-done.1, f32[8,128,10]{2,1,0:T(8,128)} %subtract_exponential_fusion.refs_1_, f32[7,10]{1,0:T(8,128)} %pad_maximum_fusion.2.refs_2_, ...), custom_call_target="tpu_custom_call" | custom-call | flops 536870912 | bytes 8388608 | tf_op jit(solution)/shard_map/group_states/pallas_call | solution.py:102
  66.1 3.6 %all-to-all-start.1 = ((bf16[8,128,640]{2,1,0:T(8,128)(2,1)}), bf16[8,128,640]{2,1,0:T(8,128)(2,1)S(1)}, u32[]{:S(2)}, u32[]{:S(2)}) async-start(bf16[8,128,640]{2,1,0:T(8,128)(2,1)} %bitcast.3), calls=%async_computation.1 | async-start | bytes 2621440 | tf_op jit(solution)/shard_map/all_to_all | solution.py:287
  69.8 3.0 %collective-permute-done.1 = f32[1,10]{1,0:T(1,128)S(1)} collective-permute-done((f32[1,10]{1,0:T(1,128)S(1)}, f32[1,10]{1,0:T(1,128)S(1)}, u32[]{:S(2)}, u32[]{:S(2)}) %collective-permute-start.1) | collective-permute-done | bytes 72 | tf_op jit(solution)/shard_map/ppermute | solution.py:18
  72.9 2.1 %slice_multiply_fusion.1 = (f32[8,128,10]{2,1,0:T(8,128)S(1)}, f32[8,128,10]{2,1,0:T(8,128)}, f32[8,128,10]{2,1,0:T(8,128)}, f32[8,128,10]{2,1,0:T(8,128)}, f32[8,128,10]{2,1,0:T(8,128)}, /*index=5*/f32[8,128,10]{2,1,0:T(8,128)}) fusion(f32[8,128,70]{2,1,0:T(8,128)S(1)} %fusion.27, f32[8,128,10]{2,1,0:T(8,128)S(1)} %copy-done.3, ...), kind=kLoop, calls=%fused_computation.22 | loop fusion | flops 61440 | bytes 451840 | tf_op jit(solution)/shard_map/mul | solution.py:350
  83.2 7.6 %collective-permute-done.3.refs_7_ = bf16[128,640]{1,0:T(8,128)(2,1)S(1)} collective-permute-done((bf16[128,640]{1,0:T(8,128)(2,1)S(1)}, bf16[128,640]{1,0:T(8,128)(2,1)S(1)}, u32[]{:S(2)}, u32[]{:S(2)}) %collective-permute-start.3) | collective-permute-done | bytes 163872 | tf_op jit(solution)/shard_map/ppermute | solution.py:18
  91.9 2.4 %pad_maximum_fusion.refs_3_ = f32[8,128,50]{2,1,0:T(8,128)} fusion(f32[8,128,10]{2,1,0:T(8,128)} %get-tuple-element.38, f32[8,128,10]{2,1,0:T(8,128)S(1)} %get-tuple-element.37, f32[8,128,10]{2,1,0:T(8,128)S(1)} %copy-done.5, f32[8,128,20]{2,1,0:T(8,128)S(1)} %bitcast.153), kind=kLoop, calls=%fused_computation.28 | loop fusion | flops 153600 | bytes 409600 | tf_op jit(solution)/shard_map/concatenate | solution.py:362
  94.3 10.4 %local_mix.1.refs_1_ = f32[1024,640]{1,0:T(8,128)} custom-call(bf16[8,128,1024]{2,1,0:T(8,128)(2,1)} %copy-done.1, f32[8,128,10]{2,1,0:T(8,128)} %copy-done.2, f32[8,10,128]{2,1,0:T(8,128)} %copy.88.refs_2_, f32[8,128,50]{2,1,0:T(8,128)} %pad_maximum_fusion.refs_3_, f32[8,128,1]{2,1,0:T(8,128)} %get-tuple-element.44.refs_4_, f32[8,1,128]{2,1,0:T(1,128)} %bitcast.170, ...), custom_call_target="tpu_custom_call" | custom-call | flops 4294967296 | bytes 12582912 | tf_op jit(solution)/shard_map/local_mix/pallas_call | solution.py:178
  105.7 8.0 %gate_mix.1 = (bf16[1024,640]{1,0:T(8,128)(2,1)}, f32[8,128,1]{2,1,0:T(8,128)}) custom-call(bf16[8,128,1024]{2,1,0:T(8,128)(2,1)} %copy-done.1, f32[1024,640]{1,0:T(8,128)} %local_mix.1.refs_1_, f32[8,128,20]{2,1,0:T(8,128)} %copy.97.refs_2_, bf16[8,128,640]{2,1,0:T(8,128)(2,1)} %copy-done.4, f32[1,640]{1,0:T(1,128)} %broadcast_in_dim.112.refs_4_, ...), custom_call_target="tpu_custom_call" | custom-call | flops 1073741824 | bytes 8388608 | tf_op jit(solution)/shard_map/gate_mix/pallas_call | solution.py:229
  113.7 2.9 %fusion.52 = f32[1024,640]{1,0:T(8,128)S(1)} fusion(bf16[1024,640]{1,0:T(8,128)(2,1)} %get-tuple-element.30, bf16[640,640]{1,0:T(8,128)(2,1)} %collective-permute-done.17), kind=kOutput, calls=%fused_computation.135 | convolution fusion | flops 838860800 | bytes 4751360 | tf_op jit(solution)/shard_map/dot_general | solution.py:420
  118.9 2.5 %fusion.51 = f32[1024,640]{1,0:T(8,128)S(1)} fusion(bf16[1024,640]{1,0:T(8,128)(2,1)S(1)} %copy-done.13, bf16[640,640]{1,0:T(8,128)(2,1)} %collective-permute-done.13), kind=kOutput, calls=%fused_computation.134 | convolution fusion | flops 838860800 | bytes 4751360 | tf_op jit(solution)/shard_map/dot_general | solution.py:420
  123.4 2.9 %fusion.50 = f32[1024,640]{1,0:T(8,128)S(1)} fusion(bf16[1024,640]{1,0:T(8,128)(2,1)} %get-tuple-element.30, bf16[640,640]{1,0:T(8,128)(2,1)} %collective-permute-done.2), kind=kOutput, calls=%fused_computation.133 | convolution fusion | flops 838860800 | bytes 4751360 | tf_op jit(solution)/shard_map/dot_general | solution.py:420
  128.2 2.6 %fusion.49 = f32[2,2,2,128,640]{4,3,2,1,0:T(8,128)S(1)} fusion(bf16[2,2,2,128,640]{4,3,2,1,0:T(8,128)(2,1)S(1)} %bitcast.175, bf16[640,640,1,1,1]{1,0,4,3,2:T(8,128)(2,1)} %bitcast.21), kind=kOutput, calls=%fused_computation.132 | convolution fusion | flops 838860800 | bytes 4751360 | tf_op jit(solution)/shard_map/dot_general | solution.py:420
  141.8 4.7 %collective-permute-done.19 = bf16[2,128,640]{2,1,0:T(8,128)(2,1)S(1)} collective-permute-done((bf16[2,128,640]{2,1,0:T(8,128)(2,1)S(1)}, bf16[2,128,640]{2,1,0:T(8,128)(2,1)S(1)}, u32[]{:S(2)}, u32[]{:S(2)}) %collective-permute-start.19) | collective-permute-done | bytes 327712 | tf_op jit(solution)/shard_map/ppermute | solution.py:18
  150.0 6.3 %collective-permute-done.5 = bf16[2,128,640]{2,1,0:T(8,128)(2,1)S(1)} collective-permute-done((bf16[2,128,640]{2,1,0:T(8,128)(2,1)S(1)}, bf16[2,128,640]{2,1,0:T(8,128)(2,1)S(1)}, u32[]{:S(2)}, u32[]{:S(2)}) %collective-permute-start.5) | collective-permute-done | bytes 327712 | tf_op jit(solution)/shard_map/ppermute | solution.py:18
  157.7 4.1 %collective-permute-done.6 = bf16[128,640]{1,0:T(8,128)(2,1)S(1)} collective-permute-done((bf16[128,640]{1,0:T(8,128)(2,1)S(1)}, bf16[128,640]{1,0:T(8,128)(2,1)S(1)}, u32[]{:S(2)}, u32[]{:S(2)}) %collective-permute-start.6) | collective-permute-done | bytes 163872 | tf_op jit(solution)/shard_map/ppermute | solution.py:18
  (156 shorter events, 51.7 us)
Async XLA Ops:
  2.2 18.2 %all-to-all-start.2 = ((bf16[8,80,640]{2,1,0:T(8,128)(2,1)}), bf16[8,80,640]{2,1,0:T(8,128)(2,1)}, u32[]{:S(2)}, u32[]{:S(2)}) async-start(bf16[8,80,640]{2,1,0:T(8,128)(2,1)} %bitcast.151), calls=%async_computation.2 | async-start | bytes 1638400 | tf_op jit(solution)/shard_map/all_to_all | solution.py:287
  20.4 30.2 %all-to-all-start = ((bf16[8,128,1024]{2,1,0:T(8,128)(2,1)}), bf16[8,128,1024]{2,1,0:T(8,128)(2,1)S(1)}, u32[]{:S(2)}, u32[]{:S(2)}) async-start(bf16[8,128,1024]{2,1,0:T(8,128)(2,1)} %pack.1), calls=%async_computation | async-start | bytes 4194304 | tf_op jit(solution)/shard_map/all_to_all | solution.py:287
  32.1 51.1 %collective-permute-start.2 = (bf16[640,640]{1,0:T(8,128)(2,1)}, bf16[640,640]{1,0:T(8,128)(2,1)}, u32[]{:S(2)}, u32[]{:S(2)}) collective-permute-start(bf16[640,640]{1,0:T(8,128)(2,1)} %bitcast.18), channel_id=1, source_target_pairs={{0,8},{1,9},{2,10},{3,11},{4,12},{5,13},{6,14},{7,15},{8,16},{9,17... | collective-permute-start | bytes 2457608 | tf_op jit(solution)/shard_map/ppermute | solution.py:311
  34.1 83.5 %collective-permute-start.13 = (bf16[640,640]{1,0:T(8,128)(2,1)}, bf16[640,640]{1,0:T(8,128)(2,1)}, u32[]{:S(2)}, u32[]{:S(2)}) collective-permute-start(bf16[640,640]{1,0:T(8,128)(2,1)} %bitcast.18), channel_id=1, source_target_pairs={{0,24},{1,25},{2,26},{3,27},{4,28},{5,29},{6,30},{7,31},{8,0},{9,1... | collective-permute-start | bytes 2457608 | tf_op jit(solution)/shard_map/ppermute | solution.py:311
  63.2 9.5 %collective-permute-start.1 = (f32[1,10]{1,0:T(1,128)S(1)}, f32[1,10]{1,0:T(1,128)S(1)}, u32[]{:S(2)}, u32[]{:S(2)}) collective-permute-start(f32[1,10]{1,0:T(1,128)S(1)} %bitcast.172), channel_id=1, source_target_pairs={{0,8},{1,9},{2,10},{3,11},{4,12},{5,13},{6,14},{7,15},{8,0},{9,1},... | collective-permute-start | bytes 128 | tf_op jit(solution)/shard_map/ppermute | solution.py:18
  65.2 16.1 %collective-permute-start = (bf16[128,640]{1,0:T(8,128)(2,1)}, bf16[128,640]{1,0:T(8,128)(2,1)S(1)}, u32[]{:S(2)}, u32[]{:S(2)}) collective-permute-start(bf16[128,640]{1,0:T(8,128)(2,1)} %get-tuple-element.20), channel_id=1, source_target_pairs={{0,8},{1,9},{2,10},{3,11},{4,12},{5,13},{6,14},{7,15},{8,0},{9,1},... | collective-permute-start | bytes 491528 | tf_op jit(solution)/shard_map/ppermute | solution.py:18
  66.1 38.5 %all-to-all-start.1 = ((bf16[8,128,640]{2,1,0:T(8,128)(2,1)}), bf16[8,128,640]{2,1,0:T(8,128)(2,1)S(1)}, u32[]{:S(2)}, u32[]{:S(2)}) async-start(bf16[8,128,640]{2,1,0:T(8,128)(2,1)} %bitcast.3), calls=%async_computation.1 | async-start | bytes 2621440 | tf_op jit(solution)/shard_map/all_to_all | solution.py:287
  81.4 9.4 %collective-permute-start.3 = (bf16[128,640]{1,0:T(8,128)(2,1)S(1)}, bf16[128,640]{1,0:T(8,128)(2,1)S(1)}, u32[]{:S(2)}, u32[]{:S(2)}) collective-permute-start(bf16[128,640]{1,0:T(8,128)(2,1)S(1)} %add_convert_fusion), channel_id=1, source_target_pairs={{0,16},{1,17},{2,18},{3,19},{4,20},{5,21},{6,22},{7,23},{8,24},{9,... | collective-permute-start | bytes 491528 | tf_op jit(solution)/shard_map/ppermute | solution.py:18
  90.8 22.9 %collective-permute-start.17 = (bf16[640,640]{1,0:T(8,128)(2,1)}, bf16[640,640]{1,0:T(8,128)(2,1)}, u32[]{:S(2)}, u32[]{:S(2)}) collective-permute-start(bf16[640,640]{1,0:T(8,128)(2,1)} %collective-permute-done.2), channel_id=1, source_target_pairs={{0,8},{1,9},{2,10},{3,11},{4,12},{5,13},{6,14},{7,15},{8,16},{9,17... | collective-permute-start | bytes 2457608 | tf_op jit(solution)/shard_map/ppermute | solution.py:311
  117.6 17.0 %collective-permute-start.18 = (bf16[2,2,128,640]{3,2,1,0:T(8,128)(2,1)}, bf16[2,2,128,640]{3,2,1,0:T(8,128)(2,1)}, u32[]{:S(2)}, u32[]{:S(2)}) collective-permute-start(bf16[2,2,128,640]{3,2,1,0:T(8,128)(2,1)} %fusion.3), channel_id=1, source_target_pairs={{0,1},{1,0},{2,3},{3,2},{4,5},{5,4},{6,7},{7,6},{8,9},{9,8},{10,11... | collective-permute-start | bytes 1966088 | tf_op jit(solution)/shard_map/ppermute | solution.py:18
  121.5 15.9 %collective-permute-start.14 = (bf16[2,2,128,640]{3,2,0,1:T(8,128)(2,1)S(1)}, bf16[2,2,128,640]{3,2,0,1:T(8,128)(2,1)}, u32[]{:S(2)}, u32[]{:S(2)}) collective-permute-start(bf16[2,2,128,640]{3,2,0,1:T(8,128)(2,1)S(1)} %fusion.1), channel_id=1, source_target_pairs={{0,1},{1,0},{2,3},{3,2},{4,5},{5,4},{6,7},{7,6},{8,9},{9,8},{10,11... | collective-permute-start | bytes 1966088 | tf_op jit(solution)/shard_map/ppermute | solution.py:18
  122.9 3.6 %collective-permute-start.7 = (f32[2,2,128]{2,1,0:T(2,128)S(1)}, f32[2,2,128]{2,1,0:T(2,128)S(1)}, u32[]{:S(2)}, u32[]{:S(2)}) collective-permute-start(f32[2,2,128]{2,1,0:T(2,128)S(1)} %bitcast.173), channel_id=1, source_target_pairs={{0,1},{1,0},{2,3},{3,2},{4,5},{5,4},{6,7},{7,6},{8,9},{9,8},{10,11... | collective-permute-start | bytes 6152 | tf_op jit(solution)/shard_map/ppermute | solution.py:18
  126.4 13.4 %collective-permute-start.10 = (bf16[2,2,128,640]{3,2,1,0:T(8,128)(2,1)S(1)}, bf16[2,2,128,640]{3,2,1,0:T(8,128)(2,1)S(1)}, u32[]{:S(2)}, u32[]{:S(2)}) collective-permute-start(bf16[2,2,128,640]{3,2,1,0:T(8,128)(2,1)S(1)} %fusion.2), channel_id=1, source_target_pairs={{0,1},{1,0},{2,3},{3,2},{4,5},{5,4},{6,7},{7,6},{8,9},{9,8},{10,11... | collective-permute-start | bytes 1966088 | tf_op jit(solution)/shard_map/ppermute | solution.py:18
  126.5 4.4 %collective-permute-start.8 = (f32[2,128]{1,0:T(2,128)S(1)}, f32[2,128]{1,0:T(2,128)S(1)}, u32[]{:S(2)}, u32[]{:S(2)}) collective-permute-start(f32[2,128]{1,0:T(2,128)S(1)} %bitcast.174), channel_id=1, source_target_pairs={{0,2},{1,3},{2,0},{3,1},{4,6},{5,7},{6,4},{7,5},{8,10},{9,11},{10,... | collective-permute-start | bytes 3080 | tf_op jit(solution)/shard_map/ppermute | solution.py:18
  130.9 3.6 %collective-permute-start.9 = (f32[128]{0:T(128)S(1)}, f32[128]{0:T(128)S(1)}, u32[]{:S(2)}, u32[]{:S(2)}) collective-permute-start(f32[128]{0:T(128)S(1)} %fusion.46), channel_id=1, source_target_pairs={{0,4},{1,5},{2,6},{3,7},{4,0},{5,1},{6,2},{7,3},{8,12},{9,13},{10,... | collective-permute-start | bytes 1544 | tf_op jit(solution)/shard_map/ppermute | solution.py:18
  132.5 8.0 %collective-permute-start.4 = (bf16[2,2,128,640]{3,2,1,0:T(8,128)(2,1)S(1)}, bf16[2,2,128,640]{3,2,1,0:T(8,128)(2,1)S(1)}, u32[]{:S(2)}, u32[]{:S(2)}) collective-permute-start(bf16[2,2,128,640]{3,2,1,0:T(8,128)(2,1)S(1)} %fusion), channel_id=1, source_target_pairs={{0,1},{1,0},{2,3},{3,2},{4,5},{5,4},{6,7},{7,6},{8,9},{9,8},{10,11... | collective-permute-start | bytes 1966088 | tf_op jit(solution)/shard_map/ppermute | solution.py:18
  135.9 10.6 %collective-permute-start.19 = (bf16[2,128,640]{2,1,0:T(8,128)(2,1)S(1)}, bf16[2,128,640]{2,1,0:T(8,128)(2,1)S(1)}, u32[]{:S(2)}, u32[]{:S(2)}) collective-permute-start(bf16[2,128,640]{2,1,0:T(8,128)(2,1)S(1)} %fusion.8), channel_id=1, source_target_pairs={{0,4},{1,5},{2,6},{3,7},{4,0},{5,1},{6,2},{7,3},{8,12},{9,13},{10,... | collective-permute-start | bytes 983048 | tf_op jit(solution)/shard_map/ppermute | solution.py:18
  138.7 10.6 %collective-permute-start.15 = (bf16[2,128,640]{2,1,0:T(8,128)(2,1)S(1)}, bf16[2,128,640]{2,1,0:T(8,128)(2,1)S(1)}, u32[]{:S(2)}, u32[]{:S(2)}) collective-permute-start(bf16[2,128,640]{2,1,0:T(8,128)(2,1)S(1)} %fusion.7), channel_id=1, source_target_pairs={{0,2},{1,3},{2,0},{3,1},{4,6},{5,7},{6,4},{7,5},{8,10},{9,11},{10,... | collective-permute-start | bytes 983048 | tf_op jit(solution)/shard_map/ppermute | solution.py:18
  140.0 16.7 %collective-permute-start.11 = (bf16[2,128,640]{2,1,0:T(8,128)(2,1)S(1)}, bf16[2,128,640]{2,1,0:T(8,128)(2,1)S(1)}, u32[]{:S(2)}, u32[]{:S(2)}) collective-permute-start(bf16[2,128,640]{2,1,0:T(8,128)(2,1)S(1)} %fusion.6), channel_id=1, source_target_pairs={{0,4},{1,5},{2,6},{3,7},{4,0},{5,1},{6,2},{7,3},{8,12},{9,13},{10,... | collective-permute-start | bytes 983048 | tf_op jit(solution)/shard_map/ppermute | solution.py:18
  140.7 15.6 %collective-permute-start.5 = (bf16[2,128,640]{2,1,0:T(8,128)(2,1)S(1)}, bf16[2,128,640]{2,1,0:T(8,128)(2,1)S(1)}, u32[]{:S(2)}, u32[]{:S(2)}) collective-permute-start(bf16[2,128,640]{2,1,0:T(8,128)(2,1)S(1)} %fusion.5), channel_id=1, source_target_pairs={{0,2},{1,3},{2,0},{3,1},{4,6},{5,7},{6,4},{7,5},{8,10},{9,11},{10,... | collective-permute-start | bytes 983048 | tf_op jit(solution)/shard_map/ppermute | solution.py:18
  146.6 15.7 %collective-permute-start.20 = (bf16[128,640]{1,0:T(8,128)(2,1)S(1)}, bf16[128,640]{1,0:T(8,128)(2,1)S(1)}, u32[]{:S(2)}, u32[]{:S(2)}) collective-permute-start(bf16[128,640]{1,0:T(8,128)(2,1)S(1)} %fusion.22), channel_id=1, source_target_pairs={{0,2},{1,3},{2,0},{3,1},{4,6},{5,7},{6,4},{7,5},{8,10},{9,11},{10,... | collective-permute-start | bytes 491528 | tf_op jit(solution)/shard_map/ppermute | solution.py:18
  149.4 12.8 %collective-permute-start.16 = (bf16[128,640]{1,0:T(8,128)(2,1)S(1)}, bf16[128,640]{1,0:T(8,128)(2,1)S(1)}, u32[]{:S(2)}, u32[]{:S(2)}) collective-permute-start(bf16[128,640]{1,0:T(8,128)(2,1)S(1)} %fusion.21), channel_id=1, source_target_pairs={{0,4},{1,5},{2,6},{3,7},{4,0},{5,1},{6,2},{7,3},{8,12},{9,13},{10,... | collective-permute-start | bytes 491528 | tf_op jit(solution)/shard_map/ppermute | solution.py:18
  156.4 5.4 %collective-permute-start.6 = (bf16[128,640]{1,0:T(8,128)(2,1)S(1)}, bf16[128,640]{1,0:T(8,128)(2,1)S(1)}, u32[]{:S(2)}, u32[]{:S(2)}) collective-permute-start(bf16[128,640]{1,0:T(8,128)(2,1)S(1)} %fusion.19), channel_id=1, source_target_pairs={{0,4},{1,5},{2,6},{3,7},{4,0},{5,1},{6,2},{7,3},{8,12},{9,13},{10,... | collective-permute-start | bytes 491528 | tf_op jit(solution)/shard_map/ppermute | solution.py:18
  156.7 5.4 %collective-permute-start.12 = (bf16[128,640]{1,0:T(8,128)(2,1)S(1)}, bf16[128,640]{1,0:T(8,128)(2,1)S(1)}, u32[]{:S(2)}, u32[]{:S(2)}) collective-permute-start(bf16[128,640]{1,0:T(8,128)(2,1)S(1)} %fusion.20), channel_id=1, source_target_pairs={{0,2},{1,3},{2,0},{3,1},{4,6},{5,7},{6,4},{7,5},{8,10},{9,11},{10,... | collective-permute-start | bytes 491528 | tf_op jit(solution)/shard_map/ppermute | solution.py:18
  (18 other events, 114.5 us)
